TPU v7x, 32 devices: a whole 2x2x4 slice. The times are simulated.
32 devices in a mesh: dp: 8 (over z, x), tensor: 4 (over y, core).
Axes of the slice: x: 2, y: 2, z: 4, core: 2. Of those that a mesh axis runs over, the one named last changes fastest.
Arguments:
- inputs: bfloat16 [2, 8192, 768], P(None, 'dp'), may hold values from -6 to 6
- cotangent: bfloat16 [2, 8192, 768], P(None, 'dp'), may hold values from -6 to 6
- segment: int32 [2, 8192], P(None, 'dp'), may hold values from 0 to 15, never falling along the last dimension, each value on 1 to 4096 neighbouring positions
- attn_gain: bfloat16 [768], replicated, may hold values from 0.5 to 1.5
- attn_shift: bfloat16 [768], replicated, may hold values from -2 to 2
- qkv_weight: bfloat16 [768, 3, 768], P('dp', None, 'tensor'), may hold values from -0.21875 to 0.21875
- qkv_bias: bfloat16 [3, 768], P(None, 'tensor'), may hold values from -2 to 2
- query_map: bfloat16 [12, 64, 64], P('tensor'), may hold values from -2 to 2
- key_map: bfloat16 [12, 64, 64], P('tensor'), may hold values from -2 to 2
- proj_weight: bfloat16 [768, 768], P('tensor', 'dp'), may hold values from -0.875 to 0.875
- proj_bias: bfloat16 [768], replicated, may hold values from -2 to 2
- mlp_gain: bfloat16 [768], replicated, may hold values from 0.5 to 1.5
- mlp_shift: bfloat16 [768], replicated, may hold values from -2 to 2
- fc_weight: bfloat16 [768, 3072], P('dp', 'tensor'), may hold values from -0.21875 to 0.21875
- fc_bias: bfloat16 [3072], P('tensor'), may hold values from -2 to 2
- out_weight: bfloat16 [3072, 768], P('tensor', 'dp'), may hold values from -0.109375 to 0.109375
- out_bias: bfloat16 [768], replicated, may hold values from -2 to 2
Outputs:
- output: bfloat16 [2, 8192, 768], P(None, 'dp')
- input_grad: bfloat16 [2, 8192, 768], P(None, 'dp')
- grad_attn_gain: float32 [768], replicated
- grad_attn_shift: float32 [768], replicated
- grad_qkv_weight: float32 [768, 3, 768], P('dp', None, 'tensor')
- grad_qkv_bias: float32 [3, 768], P(None, 'tensor')
- grad_query_map: float32 [12, 64, 64], P('tensor')
- grad_key_map: float32 [12, 64, 64], P('tensor')
- grad_proj_weight: float32 [768, 768], P('tensor', 'dp')
- grad_proj_bias: float32 [768], replicated
- grad_mlp_gain: float32 [768], replicated
- grad_mlp_shift: float32 [768], replicated
- grad_fc_weight: float32 [768, 3072], P('dp', 'tensor')
- grad_fc_bias: float32 [3072], P('tensor')
- grad_out_weight: float32 [3072, 768], P('tensor', 'dp')
- grad_out_bias: float32 [768], replicated
Inputs may be any that keep to these rules, and one draw needn't show every extreme that they name: `segment`: along each micro-batch's tokens the numbers never fall; each number covers 1 to 4096 consecutive tokens, some number exactly that many, and every number in the range occurs.
All inputs are finite; a program needn't handle non-finite values.
Results may differ from a plain program's by a relative error of at most 0.018.
Values may be sent and summed in bfloat16 or wider, within the bound.
No kernel may reach another device: no remote copies, remote signals or barrier semaphores. Data moves between devices by JAX's collectives and lax.ppermute only.
A program may use at most 256 MiB of HBM per device.

v0:
```python
import jax
import jax.numpy as jnp
from jax import lax
from jax.sharding import PartitionSpec as P

BLOCK = 64
SEQ_LEN = 8192


EPSILON = 1e-05
PRECISION_TOP = lax.Precision.HIGHEST
GELU_SCALE = 0.7978845608028654
GELU_CUBIC = 0.044715


def carried_in(array, axis, join, neutral):
    place = lax.axis_index(axis)
    gathered = jax.tree.map(
        lambda a, kind: lax.all_gather(a.astype(kind), axis),
        array,
        (jnp.bfloat16, jnp.bfloat16, jnp.bfloat16, jnp.bfloat16, jnp.bfloat16),
    )
    state = jax.tree.map(lambda a, e: jnp.zeros_like(a) + jnp.asarray(e, a.dtype), array, neutral)

    def carried_one(lap, state):
        return join(
            state,
            jax.tree.map(
                lambda a, own: lax.dynamic_index_in_dim(a, lap, 0, False).astype(own.dtype),
                gathered,
                array,
            ),
        )

    return lax.fori_loop(0, place, carried_one, state)


def entering(array, axis, join, neutral):
    count = lax.axis_size(axis)
    place = lax.axis_index(axis)
    ahead = count - 1 - place
    gathered = jax.tree.map(
        lambda a, kind: lax.all_gather(a.astype(kind), axis),
        array,
        jax.tree.map(lambda a: jnp.bfloat16 if a.dtype == jnp.float32 else a.dtype, array),
    )
    state = jax.tree.map(lambda a, e: jnp.zeros_like(a) + jnp.asarray(e, a.dtype), array, neutral)

    def entering_one(lap, state):
        source = count - 1 - lap
        return join(
            state,
            jax.tree.map(
                lambda a, own: lax.dynamic_index_in_dim(a, source, 0, False).astype(own.dtype),
                gathered,
                array,
            ),
        )

    return lax.fori_loop(0, ahead, entering_one, state)


def norm_forward(values, norm_gain, norm_bias):
    centred = values - jnp.mean(values, axis=-1, keepdims=True)
    inverse = lax.rsqrt(jnp.mean(centred * centred, axis=-1, keepdims=True) + EPSILON)
    normed = centred * inverse
    return (normed * norm_gain + norm_bias, normed, inverse)


def norm_backward(grad_out, normed, inverse, norm_gain):
    scaled = grad_out * norm_gain
    grad_in = inverse * (
        scaled
        - jnp.mean(scaled, axis=-1, keepdims=True)
        - normed * jnp.mean(scaled * normed, axis=-1, keepdims=True)
    )
    return (grad_in, jnp.sum(grad_out * normed, axis=0), jnp.sum(grad_out, axis=0))


def softmax_last(values):
    shifted = values - jnp.max(values, axis=-1, keepdims=True)
    raised = jnp.exp(shifted)
    return raised / jnp.sum(raised, axis=-1, keepdims=True)


def feature_map(mapped):
    positive = softmax_last(mapped)
    negative = softmax_last(-mapped)
    return (jnp.concatenate([positive, negative], axis=-1), positive, negative)


def feature_back(grad_feat, positive, negative):
    half_width = positive.shape[-1]
    grad_positive = grad_feat[..., :half_width]
    grad_negative = grad_feat[..., half_width:]
    pos_part = positive * (
        grad_positive - jnp.sum(positive * grad_positive, axis=-1, keepdims=True)
    )
    neg_part = negative * (
        grad_negative - jnp.sum(negative * grad_negative, axis=-1, keepdims=True)
    )
    return pos_part - neg_part


def gelu_parts(preact):
    argument = GELU_SCALE * (preact + GELU_CUBIC * preact * preact * preact)
    tangent = jnp.tanh(argument)
    output_value = 0.5 * preact * (1.0 + tangent)
    derivative = 0.5 * (1.0 + tangent) + 0.5 * preact * (1.0 - tangent * tangent) * GELU_SCALE * (
        1.0 + 3.0 * GELU_CUBIC * preact * preact
    )
    return (output_value, derivative)


def join_states(earlier, latter):
    state_early, norm_early, first_early, last_early, open_early = earlier
    state_late, norm_late, first_late, last_late, open_late = latter
    empty_early = first_early < 0.0
    empty_late = first_late < 0.0
    linked = open_late * (first_late == last_early).astype(jnp.float32)
    kv_state = jnp.where(empty_late, state_early, state_late + linked * state_early)
    normalizer = jnp.where(empty_late, norm_early, norm_late + linked * norm_early)
    first_seg = jnp.where(empty_early, first_late, first_early)
    last_seg = jnp.where(empty_late, last_early, last_late)
    open_flag = jnp.where(
        empty_late, open_early, jnp.where(empty_early, open_late, open_early * linked)
    )
    return (kv_state, normalizer, first_seg, last_seg, open_flag)


def join_grads(earlier, latter):
    grad_early, gnorm_early, first_early, open_early = earlier
    grad_late, gnorm_late, first_late, open_late = latter
    empty_early = first_early < 0.0
    empty_late = first_late < 0.0
    matching = (first_early == first_late).astype(jnp.float32)
    linked = open_late * matching
    grad_state = jnp.where(empty_late, grad_early, grad_late + linked * grad_early)
    grad_norm = jnp.where(empty_late, gnorm_early, gnorm_late + linked * gnorm_early)
    first_seg = jnp.where(empty_late, first_early, first_late)
    open_flag = jnp.where(
        empty_late, open_early, jnp.where(empty_early, open_late, open_late * open_early * matching)
    )
    return (grad_state, grad_norm, first_seg, open_flag)


def on_device(
    inputs,
    cotangent,
    segment,
    attn_gain,
    attn_shift,
    qkv_weight,
    qkv_bias,
    query_map,
    key_map,
    proj_weight,
    proj_bias,
    mlp_gain,
    mlp_shift,
    fc_weight,
    fc_bias,
    out_weight,
    out_bias,
):
    f32 = jnp.float32
    bf16 = jnp.bfloat16
    micro_count = inputs.shape[0]
    tok_dev = inputs.shape[1]
    heads_dev = query_map.shape[0]
    head_size = query_map.shape[1]
    feat_size = 2 * head_size
    heads_width = heads_dev * head_size
    block_count = tok_dev // BLOCK
    tile_rows = 2 * BLOCK
    tile_count = tok_dev // tile_rows
    piece_index = lax.axis_index("dp")
    starts = piece_index * tok_dev % SEQ_LEN == 0
    attn_g = attn_gain.astype(f32)
    attn_s = attn_shift.astype(f32)
    mlp_g = mlp_gain.astype(f32)
    mlp_s = mlp_shift.astype(f32)
    qkv_b = qkv_bias.astype(f32)
    proj_b = proj_bias.astype(f32)
    fc_b = fc_bias.astype(f32)
    out_b = out_bias.astype(f32)
    positions = jnp.arange(tile_rows)
    same_block = jnp.logical_and(
        positions[:, None] // BLOCK == positions[None, :] // BLOCK,
        positions[None, :] <= positions[:, None],
    )
    columns = jnp.arange(block_count + 1)
    lower_part = columns[None, :] <= columns[:, None]
    not_own_in = jnp.logical_not(
        jnp.logical_and(columns[:, None] == block_count, columns[None, :] == 0)
    )
    totals = None
    outputs_list = []
    input_grads = []
    for micro_index in range(micro_count):
        qkv_full, proj_full, fc_full, out_full = (
            lax.all_gather(qkv_weight, "dp", axis=0, tiled=True),
            lax.all_gather(proj_weight, "dp", axis=1, tiled=True),
            lax.all_gather(fc_weight, "dp", axis=0, tiled=True),
            lax.all_gather(out_weight, "dp", axis=1, tiled=True),
        )
        resid_in = inputs[micro_index].astype(f32)
        attn_full, attn_normed, attn_inverse = norm_forward(resid_in, attn_g, attn_s)
        attn_in = attn_full.astype(bf16)
        qkv_pre = jnp.einsum("td,dce->tce", attn_in, qkv_full, preferred_element_type=f32) + qkv_b
        qkv_low = qkv_pre.astype(bf16)
        queries = qkv_low[:, 0].reshape(tok_dev, heads_dev, head_size)
        keys_low = qkv_low[:, 1].reshape(tok_dev, heads_dev, head_size)
        values_low = qkv_low[:, 2].reshape(tok_dev, heads_dev, head_size)
        query_mapped = jnp.einsum("the,hef->thf", queries, query_map, preferred_element_type=f32)
        key_mapped = jnp.einsum("the,hef->thf", keys_low, key_map, preferred_element_type=f32)
        query_feat, query_pos, query_neg = feature_map(query_mapped)
        key_feat, key_pos, key_neg = feature_map(key_mapped)
        query_low = query_feat.astype(bf16)
        key_low = key_feat.astype(bf16)
        seg_float = segment[micro_index].astype(f32)
        seg_blocks = seg_float.reshape(block_count, BLOCK)
        block_ends = seg_blocks[:, -1]
        key_blocks = key_low.reshape(block_count, BLOCK, heads_dev, feat_size)
        value_blocks = values_low.reshape(block_count, BLOCK, heads_dev, head_size)
        tail_mask = seg_blocks == block_ends[:, None]
        key_tail = jnp.where(tail_mask[:, :, None, None], key_blocks, jnp.zeros((), bf16))
        block_state = jnp.einsum(
            "jshf,jshd->jhfd", key_tail, value_blocks, preferred_element_type=f32
        )
        norm_per_block = jnp.sum(key_tail.astype(f32), axis=1)
        self_connection = (block_ends == block_ends[-1]).astype(f32)
        own_state = jnp.einsum("k,khfd->hfd", self_connection, block_state, precision=PRECISION_TOP)
        self_norm = jnp.einsum(
            "a,alo->lo", self_connection, norm_per_block, precision=PRECISION_TOP
        )
        first_seg = seg_float[0]
        last_seg = seg_float[-1]
        open_flag = jnp.logical_and(first_seg == last_seg, jnp.logical_not(starts)).astype(f32)
        incoming = carried_in(
            (own_state, self_norm, first_seg, last_seg, open_flag),
            "dp",
            join_states,
            (
                jnp.zeros_like(own_state),
                jnp.zeros_like(self_norm),
                jnp.float32(-1.0),
                jnp.float32(-1.0),
                jnp.float32(1.0),
            ),
        )
        state_in = incoming[0]
        norm_in = incoming[1]
        last_in = jnp.where(starts, jnp.float32(-2.0), incoming[3])
        tags = jnp.concatenate([last_in[None], block_ends])
        connection_matrix = jnp.logical_and(
            jnp.logical_and(lower_part, tags[None, :] == tags[:, None]), not_own_in
        ).astype(f32)
        connection_rows = connection_matrix[:block_count]
        all_state = jnp.concatenate([state_in[None], block_state], axis=0)
        total_norm = jnp.concatenate([norm_in[None], norm_per_block], axis=0)
        full_state = jnp.einsum(
            "ck,khfd->chfd", connection_rows, all_state, precision=PRECISION_TOP
        )
        complete_norm = jnp.einsum(
            "eq,qin->ein", connection_rows, total_norm, precision=PRECISION_TOP
        )
        use_mask = (seg_blocks == tags[:block_count, None]).astype(f32)
        query_blocks_f = query_low.astype(f32).reshape(block_count, BLOCK, heads_dev, feat_size)
        inter_num = (
            jnp.einsum("cthf,chfd->cthd", query_blocks_f, full_state, precision=PRECISION_TOP)
            * use_mask[:, :, None, None]
        )
        inter_den = (
            jnp.einsum("cthf,chf->cth", query_blocks_f, complete_norm, precision=PRECISION_TOP)
            * use_mask[:, :, None]
        )
        query_tiles = query_low.reshape(tile_count, tile_rows, heads_dev, feat_size)
        key_tiles = key_low.reshape(tile_count, tile_rows, heads_dev, feat_size)
        value_tiles = values_low.reshape(tile_count, tile_rows, heads_dev, head_size)
        seg_tiles = seg_float.reshape(tile_count, tile_rows)
        pair_mask = jnp.logical_and(
            same_block[None], seg_tiles[:, :, None] == seg_tiles[:, None, :]
        )
        scores = jnp.einsum("pthf,pshf->phts", query_tiles, key_tiles, preferred_element_type=f32)
        scores_low = jnp.where(pair_mask[:, None], scores.astype(bf16), jnp.zeros((), bf16))
        intra_num = jnp.einsum(
            "phts,pshd->pthd", scores_low, value_tiles, preferred_element_type=f32
        )
        intra_den = jnp.sum(scores_low.astype(f32), axis=-1)
        numerator = intra_num.reshape(tok_dev, heads_dev, head_size) + inter_num.reshape(
            tok_dev, heads_dev, head_size
        )
        denominator = jnp.transpose(intra_den, (0, 2, 1)).reshape(
            tok_dev, heads_dev
        ) + inter_den.reshape(tok_dev, heads_dev)
        attended = numerator / denominator[:, :, None]
        attended_low = attended.astype(bf16).reshape(tok_dev, heads_width)
        attn_part = jnp.dot(attended_low, proj_full, preferred_element_type=f32)
        attn_out = lax.psum(attn_part.astype(jnp.bfloat16), "tensor").astype(jnp.float32) + proj_b
        residual = resid_in + attn_out
        mlp_full, mlp_normed, mlp_inverse = norm_forward(residual, mlp_g, mlp_s)
        mlp_in = mlp_full.astype(bf16)
        preact = jnp.dot(mlp_in, fc_full, preferred_element_type=f32) + fc_b
        activ, derivative = gelu_parts(preact)
        activ_low = activ.astype(bf16)
        mlp_part = jnp.dot(activ_low, out_full, preferred_element_type=f32)
        mlp_total = lax.psum(mlp_part.astype(jnp.bfloat16), "tensor").astype(jnp.float32) + out_b
        outputs_list.append((residual + mlp_total).astype(bf16))
        qkv_full, proj_full, fc_full, out_full = (
            lax.all_gather(qkv_weight, "dp", axis=0, tiled=True),
            lax.all_gather(proj_weight, "dp", axis=1, tiled=True),
            lax.all_gather(fc_weight, "dp", axis=0, tiled=True),
            lax.all_gather(out_weight, "dp", axis=1, tiled=True),
        )
        grad_top = cotangent[micro_index]
        grad_top32 = grad_top.astype(f32)
        grad_out_w = jnp.einsum("tf,td->fd", activ_low, grad_top, preferred_element_type=f32)
        grad_out_b = jnp.sum(grad_top32, axis=0)
        grad_activ = jnp.einsum("td,fd->tf", grad_top, out_full, preferred_element_type=f32)
        grad_pre = (grad_activ * derivative).astype(bf16)
        grad_fc_b = jnp.sum(grad_pre.astype(f32), axis=0)
        grad_fc_w = jnp.einsum("td,tf->df", mlp_in, grad_pre, preferred_element_type=f32)
        mlp_terms = jnp.einsum("tf,df->td", grad_pre, fc_full, preferred_element_type=f32)
        grad_mlp_in = lax.psum(mlp_terms.astype(jnp.bfloat16), "tensor").astype(jnp.float32)
        grad_resid_norm, grad_mlp_g, grad_mlp_s = norm_backward(
            grad_mlp_in, mlp_normed, mlp_inverse, mlp_g
        )
        grad_residual = grad_top32 + grad_resid_norm
        grad_attn = grad_residual.astype(bf16)
        grad_proj_b = jnp.sum(grad_attn.astype(f32), axis=0)
        grad_proj_w = jnp.einsum("te,td->ed", attended_low, grad_attn, preferred_element_type=f32)
        grad_attended = jnp.einsum(
            "td,ed->te", grad_attn, proj_full, preferred_element_type=f32
        ).reshape(tok_dev, heads_dev, head_size)
        grad_num = grad_attended / denominator[:, :, None]
        grad_den = -jnp.sum(grad_attended * attended, axis=-1) / denominator
        grad_num_tiles = grad_num.reshape(tile_count, tile_rows, heads_dev, head_size)
        grad_den_tiles = grad_den.reshape(tile_count, tile_rows, heads_dev)
        grad_scores = (
            jnp.einsum(
                "pthd,pshd->phts", grad_num_tiles, value_tiles.astype(f32), precision=PRECISION_TOP
            )
            + jnp.transpose(grad_den_tiles, (0, 2, 1))[:, :, :, None]
        )
        grad_scores_low = jnp.where(
            pair_mask[:, None], grad_scores.astype(bf16), jnp.zeros((), bf16)
        )
        grad_query_tiles = jnp.einsum(
            "phts,pshf->pthf", grad_scores_low, key_tiles, preferred_element_type=f32
        )
        grad_key_tiles = jnp.einsum(
            "phts,pthf->pshf", grad_scores_low, query_tiles, preferred_element_type=f32
        )
        grad_value_tiles = jnp.einsum(
            "phts,pthd->pshd", scores_low.astype(f32), grad_num_tiles, precision=PRECISION_TOP
        )
        grad_num_blocks = (
            grad_num.reshape(block_count, BLOCK, heads_dev, head_size) * use_mask[:, :, None, None]
        )
        grad_den_blocks = grad_den.reshape(block_count, BLOCK, heads_dev) * use_mask[:, :, None]
        grad_query_inter = (
            jnp.einsum("cthd,chfd->cthf", grad_num_blocks, full_state, precision=PRECISION_TOP)
            + grad_den_blocks[:, :, :, None] * complete_norm[:, None]
        )
        grad_rows = jnp.einsum(
            "cthf,cthd->chfd", query_blocks_f, grad_num_blocks, precision=PRECISION_TOP
        )
        grad_row_norm = jnp.einsum(
            "cthf,cth->chf", query_blocks_f, grad_den_blocks, precision=PRECISION_TOP
        )
        grad_in_state = jnp.einsum(
            "c,chfd->hfd", connection_rows[:, 0], grad_rows, precision=PRECISION_TOP
        )
        grad_in_norm = jnp.einsum(
            "c,chf->hf", connection_rows[:, 0], grad_row_norm, precision=PRECISION_TOP
        )
        returned = entering(
            (grad_in_state, grad_in_norm, first_seg, open_flag),
            "dp",
            join_grads,
            (
                jnp.zeros_like(grad_in_state),
                jnp.zeros_like(grad_in_norm),
                jnp.float32(-1.0),
                jnp.float32(1.0),
            ),
        )
        taken = (returned[2] == last_seg).astype(f32)
        grad_all_rows = jnp.concatenate([grad_rows, (taken * returned[0])[None]], axis=0)
        gradient_total_norm = jnp.concatenate([grad_row_norm, (taken * returned[1])[None]], axis=0)
        grad_block_state = jnp.einsum(
            "ck,chfd->khfd", connection_matrix[:, 1:], grad_all_rows, precision=PRECISION_TOP
        )
        grad_block_norm = jnp.einsum(
            "tv,tmx->vmx", connection_matrix[:, 1:], gradient_total_norm, precision=PRECISION_TOP
        )
        tail_float = tail_mask.astype(f32)
        grad_key_state = (
            jnp.einsum(
                "jshd,jhfd->jshf",
                value_blocks.astype(f32),
                grad_block_state,
                precision=PRECISION_TOP,
            )
            + grad_block_norm[:, None]
        ) * tail_float[:, :, None, None]
        grad_value_state = jnp.einsum(
            "jshf,jhfd->jshd", key_tail.astype(f32), grad_block_state, precision=PRECISION_TOP
        )
        grad_query_feat = grad_query_tiles.reshape(
            tok_dev, heads_dev, feat_size
        ) + grad_query_inter.reshape(tok_dev, heads_dev, feat_size)
        grad_key_feat = grad_key_tiles.reshape(
            tok_dev, heads_dev, feat_size
        ) + grad_key_state.reshape(tok_dev, heads_dev, feat_size)
        grad_values = grad_value_tiles.reshape(
            tok_dev, heads_dev, head_size
        ) + grad_value_state.reshape(tok_dev, heads_dev, head_size)
        grad_query_mapped = feature_back(grad_query_feat, query_pos, query_neg).astype(bf16)
        grad_key_mapped = feature_back(grad_key_feat, key_pos, key_neg).astype(bf16)
        grad_qmap = jnp.einsum(
            "the,thf->hef", queries, grad_query_mapped, preferred_element_type=f32
        )
        grad_kmap = jnp.einsum(
            "the,thf->hef", keys_low, grad_key_mapped, preferred_element_type=f32
        )
        grad_queries = jnp.einsum(
            "thf,hef->the", grad_query_mapped, query_map, preferred_element_type=f32
        )
        grad_keys = jnp.einsum("thf,hef->the", grad_key_mapped, key_map, preferred_element_type=f32)
        grad_qkv = jnp.stack(
            [
                grad_queries.reshape(tok_dev, heads_width),
                grad_keys.reshape(tok_dev, heads_width),
                grad_values.reshape(tok_dev, heads_width),
            ],
            axis=1,
        ).astype(bf16)
        grad_qkv_b = jnp.sum(grad_qkv.astype(f32), axis=0)
        grad_qkv_w = jnp.einsum("td,tce->dce", attn_in, grad_qkv, preferred_element_type=f32)
        attn_terms = jnp.einsum("tce,dce->td", grad_qkv, qkv_full, preferred_element_type=f32)
        grad_attn_in = lax.psum(attn_terms.astype(jnp.bfloat16), "tensor").astype(jnp.float32)
        grad_input_norm, grad_attn_g, grad_attn_s = norm_backward(
            grad_attn_in, attn_normed, attn_inverse, attn_g
        )
        input_grads.append((grad_residual + grad_input_norm).astype(bf16))
        terms = (
            grad_attn_g,
            grad_attn_s,
            grad_qkv_w,
            grad_qkv_b,
            grad_qmap,
            grad_kmap,
            grad_proj_w,
            grad_proj_b,
            grad_mlp_g,
            grad_mlp_s,
            grad_fc_w,
            grad_fc_b,
            grad_out_w,
            grad_out_b,
        )
        totals = (
            terms if totals is None else tuple((left + right for left, right in zip(totals, terms)))
        )
    output_stack = jnp.stack(outputs_list, axis=0)
    input_stack = jnp.stack(input_grads, axis=0)
    norm_attn_g, norm_attn_s, norm_mlp_g, norm_mlp_s = (totals[0], totals[1], totals[8], totals[9])
    matrix_grads = (
        lax.psum_scatter(totals[2], "dp", scatter_dimension=0, tiled=True),
        lax.psum_scatter(totals[6], "dp", scatter_dimension=1, tiled=True),
        lax.psum_scatter(totals[10], "dp", scatter_dimension=0, tiled=True),
        lax.psum_scatter(totals[12], "dp", scatter_dimension=1, tiled=True),
    )
    small_sums = lax.psum(
        (
            norm_attn_g,
            norm_attn_s,
            totals[3],
            totals[4],
            totals[5],
            totals[7],
            norm_mlp_g,
            norm_mlp_s,
            totals[11],
            totals[13],
        ),
        "dp",
    )
    return (
        output_stack,
        input_stack,
        small_sums[0],
        small_sums[1],
        matrix_grads[0],
        small_sums[2],
        small_sums[3],
        small_sums[4],
        matrix_grads[1],
        small_sums[5],
        small_sums[6],
        small_sums[7],
        matrix_grads[2],
        small_sums[8],
        matrix_grads[3],
        small_sums[9],
    )


def solution(mesh):
    in_specs = (
        P(None, "dp", None),
        P(None, "dp", None),
        P(None, "dp"),
        P(),
        P(),
        P("dp", None, "tensor"),
        P(None, "tensor"),
        P("tensor", None, None),
        P("tensor", None, None),
        P("tensor", "dp"),
        P(),
        P(),
        P(),
        P("dp", "tensor"),
        P("tensor"),
        P("tensor", "dp"),
        P(),
    )
    out_specs = (
        P(None, "dp", None),
        P(None, "dp", None),
        P(),
        P(),
        P("dp", None, "tensor"),
        P(None, "tensor"),
        P("tensor", None, None),
        P("tensor", None, None),
        P("tensor", "dp"),
        P(),
        P(),
        P(),
        P("dp", "tensor"),
        P("tensor"),
        P("tensor", "dp"),
        P(),
    )
    return jax.shard_map(
        on_device, mesh=mesh, in_specs=in_specs, out_specs=out_specs, check_vma=False
    )
```

profile of v0, /device:TPU:0, one launch (start us, length us, event | category | flops | bytes accessed | tf_op | source)
XLA Modules:
  0.0 1467.1 jit_solution(10344402178733796030)
XLA Ops:
  19.2 40.5 %all_gather.116 = bf16[768,3,192]{2,1,0:T(4,128)(2,1)} all-gather(bf16[96,3,192]{2,1,0:T(4,128)(2,1)S(1)} %copy.219), channel_id=1, replica_groups=mesh['dp'=8,'tensor'=4] {'dp'}, dimensions={0}, use_global_device_ids=true | all-gather | bytes 995328 | tf_op jit(solution)/shard_map/all_gather | solution.py:202
  117.8 33.3 %all-gather.2 = bf16[24,128,64]{1,2,0:T(8,128)(2,1)} all-gather(bf16[3,128,64]{1,2,0:T(8,128)(2,1)S(1)} %convert_element_type.588), channel_id=4, replica_groups=mesh['dp'=8,'tensor'=4] {'dp'}, dimensions={0}, use_global_device_ids=true | all-gather | bytes 442368 | tf_op jit(solution)/shard_map/all_gather | solution.py:19
  152.5 19.9 %all-gather.9 = bf16[8,3,128]{2,1,0:T(4,128)(2,1)} all-gather(bf16[1,3,128]{2,1,0:T(4,128)(2,1)S(1)} %copy.512), channel_id=5, replica_groups=mesh['dp'=8,'tensor'=4] {'dp'}, dimensions={0}, use_global_device_ids=true | all-gather | bytes 6912 | tf_op jit(solution)/shard_map/all_gather | solution.py:19
  177.5 17.7 %all-reduce.7 = (bf16[8]{0:T(256)(128)(2,1)}, bf16[8]{0:T(256)(128)(2,1)}, bf16[8]{0:T(256)(128)(2,1)}, bf16[8]{0:T(256)(128)(2,1)}, bf16[8]{0:T(256)(128)(2,1)}, /*index=5*/bf16[8]{0:T(256)(128)(2,1)}) all-reduce(bf16[8]{0:T(256)(128)(2,1)S(1)} %dynamic-update-slice, ...), channel_id=1, replica_groups=mesh['dp'=8,'tensor'=4] {'dp'}, use_global_device_ids=true, to_apply=%add | all-reduce | flops 48 | bytes 192
  217.6 87.2 %all-gather = bf16[24,128,64]{1,2,0:T(8,128)(2,1)} all-gather(bf16[3,128,64]{1,2,0:T(8,128)(2,1)S(1)} %convert_element_type.558), channel_id=2, replica_groups=mesh['dp'=8,'tensor'=4] {'dp'}, dimensions={0}, use_global_device_ids=true | all-gather | bytes 442368 | tf_op jit(solution)/shard_map/all_gather | solution.py:19
  306.2 22.0 %all-gather.8 = bf16[8,3,128]{2,1,0:T(4,128)(2,1)} all-gather(bf16[1,3,128]{2,1,0:T(4,128)(2,1)S(1)} %copy.511), channel_id=3, replica_groups=mesh['dp'=8,'tensor'=4] {'dp'}, dimensions={0}, use_global_device_ids=true | all-gather | bytes 6912 | tf_op jit(solution)/shard_map/all_gather | solution.py:19
  380.4 91.0 %all_gather.127 = bf16[192,768]{0,1:T(8,128)(2,1)} all-gather(bf16[192,96]{0,1:T(8,128)(2,1)S(1)} %copy.242), channel_id=1, replica_groups=mesh['dp'=8,'tensor'=4] {'dp'}, dimensions={1}, use_global_device_ids=true | all-gather | bytes 331776 | tf_op jit(solution)/shard_map/all_gather | solution.py:203
  526.5 68.7 %all-reduce.22.cloned.1.call-done = (bf16[1024,768]{1,0:T(8,128)(2,1)}, bf16[1024,768]{1,0:T(8,128)(2,1)}) async-done(((bf16[1024,768]{1,0:T(8,128)(2,1)}, bf16[1024,768]{1,0:T(8,128)(2,1)}), (bf16[1024,768]{1,0:T(8,128)(2,1)}, bf16[1024,768]{1,0:T(8,128)(2,1)})) %all-reduce.22.cloned.1.call-update) | async-done | bytes 3145744 | tf_op jit(solution)/shard_map/psum | solution.py:300
  602.5 5.0 fusion.411
  612.1 6.2 convert_reduce_fusion.9
  636.1 5.7 convolution_convert_fusion.4
  645.1 49.9 %all-reduce.20.cloned.1.call-done = (bf16[1024,768]{1,0:T(8,128)(2,1)}, bf16[1024,768]{1,0:T(8,128)(2,1)}) async-done(((bf16[1024,768]{1,0:T(8,128)(2,1)}, bf16[1024,768]{1,0:T(8,128)(2,1)}), (bf16[1024,768]{1,0:T(8,128)(2,1)}, bf16[1024,768]{1,0:T(8,128)(2,1)})) %all-reduce.20.cloned.1.call-update) | async-done | bytes 3145744 | tf_op jit(solution)/shard_map/psum | solution.py:325
  695.0 6.4 fusion.87
  701.6 5.2 convert_reduce_fusion.11
  737.5 4.4 fusion.255
  741.9 3.8 bitcast_add_fusion
  758.2 21.7 %all-gather.11 = bf16[8,3,128]{2,1,0:T(4,128)(2,1)} all-gather(bf16[1,3,128]{2,1,0:T(4,128)(2,1)S(1)} %copy.514), channel_id=9, replica_groups=mesh['dp'=8,'tensor'=4] {'dp'}, dimensions={0}, use_global_device_ids=true | all-gather | bytes 6912 | tf_op jit(solution)/shard_map/all_gather | solution.py:43
  782.7 33.1 %all-gather.6 = bf16[24,128,64]{1,2,0:T(8,128)(2,1)} all-gather(bf16[3,128,64]{1,2,0:T(8,128)(2,1)S(1)} %convert_element_type.626), channel_id=8, replica_groups=mesh['dp'=8,'tensor'=4] {'dp'}, dimensions={0}, use_global_device_ids=true | all-gather | bytes 442368 | tf_op jit(solution)/shard_map/all_gather | solution.py:43
  815.9 48.3 %while.73 = (s32[]{:T(128)}, f32[3,128,64]{2,1,0:T(8,128)S(1)}, f32[3,128]{1,0:T(4,128)S(1)}, f32[]{:T(128)}, s32[]{:T(128)}, /*index=5*/bf16[8]{0:T(256)(128)(2...) while((s32[]{:T(128)}, f32[3,128,64]{2,1,0:T(8,128)S(1)}, ...), condition=%wide.region_56.57_spmd, body=%wide.region_55.56_spmd.sunk | while | flops 99850 | bytes 446457 | solution.py:60
  895.2 4.3 fusion.252
  915.8 16.3 %all-gather.10 = bf16[8,3,128]{2,1,0:T(4,128)(2,1)S(1)} all-gather(bf16[1,3,128]{2,1,0:T(4,128)(2,1)S(1)} %copy.513), channel_id=7, replica_groups=mesh['dp'=8,'tensor'=4] {'dp'}, dimensions={0}, use_global_device_ids=true | all-gather | bytes 6912 | tf_op jit(solution)/shard_map/all_gather | solution.py:43
  935.0 33.0 %all-gather.4 = bf16[24,128,64]{1,2,0:T(8,128)(2,1)} all-gather(bf16[3,128,64]{1,2,0:T(8,128)(2,1)S(1)} %convert_element_type.611), channel_id=6, replica_groups=mesh['dp'=8,'tensor'=4] {'dp'}, dimensions={0}, use_global_device_ids=true | all-gather | bytes 442368 | tf_op jit(solution)/shard_map/all_gather | solution.py:43
  968.0 43.7 %while.72 = (s32[]{:T(128)}, f32[3,128,64]{2,1,0:T(8,128)S(1)}, f32[3,128]{1,0:T(4,128)S(1)}, f32[]{:T(128)}, s32[]{:T(128)}, /*index=5*/bf16[8]{0:T(256)(128)(2...) while((s32[]{:T(128)}, f32[3,128,64]{2,1,0:T(8,128)S(1)}, ...), condition=%wide.region_43.44_spmd, body=%wide.region_42.43_spmd.sunk | while | flops 99850 | bytes 446457 | solution.py:60
  1098.3 4.4 fusion.112
  1125.4 4.5 fusion.108
  1130.0 68.7 %all-reduce.18.cloned.1.call-done = (bf16[1024,768]{1,0:T(8,128)(2,1)}, bf16[1024,768]{1,0:T(8,128)(2,1)}, bf16[1024,768]{1,0:T(8,128)(2,1)}, bf16[1024,768]{1,0:T(8,128)(2,1)}) async-done(((bf16[1024,768]{1,0:T(8,128)(2,1)}, bf16[1024,768]{1,0:T(8,128)(2,1)}, bf16[1024,768]{1,0:T(8,128)(2,1)}, bf16[1024,768]{1,0:T(8,128)(2,1)}), (bf16[1024,768]{1,0:T(8,128)(2,1)}, bf16[1024,768]{1,0:T(8,128)(2,1)}, ...) | async-done | bytes 6291472 | tf_op jit(solution)/shard_map/psum | solution.py:308
  1198.7 8.1 fusion.88
  1208.0 5.4 fusion.128
  1215.1 5.5 fusion.106
  1225.6 69.9 %reduce-scatter.11.cloned.1.call-done = f32[768,96]{0,1:T(8,128)} async-done(((f32[768,768]{0,1:T(8,128)}), f32[768,96]{0,1:T(8,128)}) %reduce-scatter.11.cloned.1.call-update) | async-done | bytes 294928 | tf_op jit(solution)/shard_map/reduce_scatter | solution.py:474
  1295.4 78.0 %all-reduce.16.cloned.1.call-done = (f32[768]{0:T(1024)}, f32[768]{0:T(1024)}, f32[3,192]{1,0:T(4,128)}, f32[3,64,64]{2,1,0:T(8,128)}, f32[3,64,64]{2,1,0:T(8,12...) async-done(((f32[768]{0:T(1024)}, f32[768]{0:T(1024)}, f32[3,192]{1,0:T(4,128)}, f32[3,64,64]{2,1,0:T(8,128)}, ...) | async-done | bytes 122128 | tf_op jit(solution)/shard_map/psum | solution.py:476
  1373.4 73.1 %reduce-scatter.7.cloned.1.call-done = f32[96,3,192]{2,0,1:T(8,128)} async-done(((f32[768,3,192]{2,0,1:T(8,128)}), f32[96,3,192]{2,0,1:T(8,128)}) %reduce-scatter.7.cloned.1.call-update) | async-done | bytes 221200 | tf_op jit(solution)/shard_map/reduce_scatter | solution.py:471
  (827 shorter events, 512.6 us)
Async XLA Ops:
  8.0 77.1 %copy-start = (bf16[3,64,64]{2,1,0:T(8,128)(2,1)S(1)}, bf16[3,64,64]{2,1,0:T(8,128)(2,1)}, u32[]{:S(2)}) copy-start(bf16[3,64,64]{2,1,0:T(8,128)(2,1)} %param.32) | copy-start | bytes 73732
  8.0 587.2 %all-reduce.22.cloned.1.call-start = ((), (), s32[]{:S(2)}) async-start(), calls=%async_computation.13 | async-start | bytes 6291456 | tf_op jit(solution)/shard_map/psum | solution.py:300
  17.6 45.5 %copy-start.125 = (f32[1024]{0:T(1024)}, f32[1024]{0:T(1024)S(1)}, u32[]{:S(2)}) copy-start(f32[1024]{0:T(1024)S(1)} %get-tuple-element.725) | copy-start | bytes 12292
  17.6 48.1 %copy-start.123 = (f32[1024]{0:T(1024)}, f32[1024]{0:T(1024)S(1)}, u32[]{:S(2)}) copy-start(f32[1024]{0:T(1024)S(1)} %get-tuple-element.724) | copy-start | bytes 12292
  19.0 44.1 %copy-start.139 = (f32[1024]{0:T(1024)}, f32[1024]{0:T(1024)S(1)}, u32[]{:S(2)}) copy-start(f32[1024]{0:T(1024)S(1)} %add_rsqrt_fusion.3) | copy-start | bytes 12292
  19.1 46.7 %copy-start.141 = (f32[768]{0:T(1024)}, f32[768]{0:T(1024)S(1)}, u32[]{:S(2)}) copy-start(f32[768]{0:T(1024)S(1)} %convert_element_type.548) | copy-start | bytes 9220
  19.2 43.9 %copy-start.173 = (bf16[768]{0:T(1024)(128)(2,1)S(1)}, bf16[768]{0:T(1024)(128)(2,1)}, u32[]{:S(2)}) copy-start(bf16[768]{0:T(1024)(128)(2,1)} %param.29) | copy-start | bytes 4612
  74.9 31.0 %copy-start.103 = (f32[16,64]{1,0:T(8,128)}, f32[16,64]{1,0:T(8,128)S(1)}, u32[]{:S(2)}) copy-start(f32[16,64]{1,0:T(8,128)S(1)} %convert_element_type.587) | copy-start | bytes 12292
  83.3 122.8 %copy-start.101 = (f32[16,64]{1,0:T(8,128)}, f32[16,64]{1,0:T(8,128)S(1)}, u32[]{:S(2)}) copy-start(f32[16,64]{1,0:T(8,128)S(1)} %convert_element_type.557) | copy-start | bytes 12292
  114.4 57.9 %copy-start.188 = (u32[32]{0:T(128)S(1)}, u32[32]{0:T(128)}, u32[]{:S(2)}) copy-start(u32[32]{0:T(128)} %constant.236) | copy-start | bytes 388
  214.3 114.6 %copy-start.187 = (bf16[8]{0:T(256)(128)(2,1)S(1)}, bf16[8]{0:T(256)(128)(2,1)}, u32[]{:S(2)}) copy-start(bf16[8]{0:T(256)(128)(2,1)} %get-tuple-element.975) | copy-start | bytes 52
  329.0 10.3 copy-start.163
  340.0 22.9 %copy-start.120 = (pred[17,17]{1,0:T(8,128)(4,1)}, pred[17,17]{1,0:T(8,128)(4,1)S(1)}, u32[]{:S(2)}) copy-start(pred[17,17]{1,0:T(8,128)(4,1)S(1)} %get-tuple-element.698) | copy-start | bytes 871
  525.1 77.4 %all-gather.15.cloned.1.call-start = ((), (), s32[]{:S(2)}) async-start(), calls=%async_computation.4 | async-start | bytes 1327104 | tf_op jit(solution)/shard_map/all_gather | solution.py:204
  525.7 86.4 %all-gather.17.cloned.1.call-start = ((), (), s32[]{:S(2)}) async-start(), calls=%async_computation.5 | async-start | bytes 1327104 | tf_op jit(solution)/shard_map/all_gather | solution.py:205
  526.3 168.7 %all-reduce.20.cloned.1.call-start = ((), (), s32[]{:S(2)}) async-start(), calls=%async_computation.12 | async-start | bytes 6291456 | tf_op jit(solution)/shard_map/psum | solution.py:325
  526.4 175.1 %copy-start.95 = (f32[768]{0:T(1024)}, f32[768]{0:T(1024)S(1)}, u32[]{:S(2)}) copy-start(f32[768]{0:T(1024)S(1)} %convert_element_type.569) | copy-start | bytes 9220
  526.4 175.1 %copy-start.130 = (f32[768]{0:T(1024)}, f32[768]{0:T(1024)S(1)}, u32[]{:S(2)}) copy-start(f32[768]{0:T(1024)S(1)} %convert_element_type.570) | copy-start | bytes 9220
  526.4 81.0 %copy-start.157 = (f32[768]{0:T(1024)}, f32[768]{0:T(1024)S(1)}, u32[]{:S(2)}) copy-start(f32[768]{0:T(1024)S(1)} %convert_element_type.571) | copy-start | bytes 9220
  526.4 91.9 %copy-start.169 = (f32[768]{0:T(1024)}, f32[768]{0:T(1024)S(1)}, u32[]{:S(2)}) copy-start(f32[768]{0:T(1024)S(1)} %convert_element_type.573) | copy-start | bytes 9220
  598.4 103.1 %copy-start.132 = (f32[1024]{0:T(1024)}, f32[1024]{0:T(1024)S(1)}, u32[]{:S(2)}) copy-start(f32[1024]{0:T(1024)S(1)} %broadcast_multiply_fusion.8) | copy-start | bytes 12292
  600.4 101.1 %copy-start.145 = (f32[1024]{0:T(1024)}, f32[1024]{0:T(1024)S(1)}, u32[]{:S(2)}) copy-start(f32[1024]{0:T(1024)S(1)} %add_rsqrt_fusion) | copy-start | bytes 12292
  627.2 571.4 %all-reduce.18.cloned.1.call-start = ((), (), s32[]{:S(2)}) async-start(), calls=%async_computation.11 | async-start | bytes 12582912 | tf_op jit(solution)/shard_map/psum | solution.py:308
  815.9 48.9 %copy-start.122 = (pred[17,17]{1,0:T(8,128)(4,1)S(1)}, pred[17,17]{1,0:T(8,128)(4,1)}, u32[]{:S(2)}) copy-start(pred[17,17]{1,0:T(8,128)(4,1)} %copy-done.120) | copy-start | bytes 871
  967.9 44.3 %copy-start.119 = (pred[17,17]{1,0:T(8,128)(4,1)S(1)}, pred[17,17]{1,0:T(8,128)(4,1)}, u32[]{:S(2)}) copy-start(pred[17,17]{1,0:T(8,128)(4,1)} %get-tuple-element.699) | copy-start | bytes 871
  1082.3 131.2 %reduce-scatter.13.cloned.1.call-start = ((), (), s32[]{:S(2)}) async-start(), calls=%async_computation.9 | async-start | bytes 884736
  1090.0 135.6 %reduce-scatter.9.cloned.1.call-start = ((), (), s32[]{:S(2)}) async-start(), calls=%async_computation.7 | async-start | bytes 2654208 | tf_op jit(solution)/shard_map/reduce_scatter | solution.py:473
  1097.6 197.9 %reduce-scatter.11.cloned.1.call-start = ((), (), s32[]{:S(2)}) async-start(), calls=%async_computation.8 | async-start | bytes 2654208 | tf_op jit(solution)/shard_map/reduce_scatter | solution.py:474
  1106.2 267.3 %all-reduce.16.cloned.1.call-start = ((), (), s32[]{:S(2)}) async-start(), calls=%async_computation.10 | async-start | bytes 458752 | tf_op jit(solution)/shard_map/psum | solution.py:476
  1125.4 73.2 %copy-start.126 = (f32[1024]{0:T(1024)S(1)}, f32[1024]{0:T(1024)}, u32[]{:S(2)}) copy-start(f32[1024]{0:T(1024)} %copy-done.125) | copy-start | bytes 12292
  1125.4 73.2 %copy-start.140 = (f32[1024]{0:T(1024)S(1)}, f32[1024]{0:T(1024)}, u32[]{:S(2)}) copy-start(f32[1024]{0:T(1024)} %copy-done.139) | copy-start | bytes 12292
  1207.9 238.6 %reduce-scatter.7.cloned.1.call-start = ((), (), s32[]{:S(2)}) async-start(), calls=%async_computation.6 | async-start | bytes 2654208 | tf_op jit(solution)/shard_map/reduce_scatter | solution.py:471
  (173 other events, 567.4 us)
Sparse Core Ops, SparseCore 0:
  525.2 69.9 all-reduce.21
  627.3 67.6 all-reduce.19
  1082.4 116.2 all-reduce.17
Sparse Core Ops, SparseCore 1:
  527.8 42.6 all-gather.14
  572.5 39.5 all-gather.16
  1090.0 59.1 reduce-scatter.12
  1153.3 69.0 reduce-scatter.8
  1226.4 68.9 reduce-scatter.10
  1301.2 72.2 all-reduce.15
  1377.4 69.1 reduce-scatter.6
where the time goes:
time: 1480 us; the launch traced here: 1470 us
  blocking collectives  416 us (28%)
  waiting for transfers between devices  410 us (28%)
  local copies, waits for them, and re-layouts  279 us (19%)
  matrix products  202 us (14%)
  other arithmetic  97.1 us (7%)
  loops' own time  37.4 us (3%)
  between operations  24.1 us (2%)
    all_gather x4, blocking collectives, carried_in(): lax.all_gather(a.astype(kind), axis)  162 us
    all_gather x4, blocking collectives, entering(): lax.all_gather(a.astype(kind), axis)  104 us
    all_gather x1, blocking collectives, on_device(): lax.all_gather(proj_weight, 'dp', axis=1, tiled=True)  91 us
    psum x1, waiting for transfers between devices, on_device(): lax.psum((norm_attn_g, norm_attn_s, totals[3], totals[4], totals[5], tota...  78 us
    reduce_scatter x1, waiting for transfers between devices, on_device(): lax.psum_scatter(totals[2], 'dp', scatter_dimension=0, tiled=True)  73.1 us
    reduce_scatter x1, waiting for transfers between devices, on_device(): lax.psum_scatter(totals[12], 'dp', scatter_dimension=1, tiled=True)  69.9 us
    psum x1, waiting for transfers between devices, on_device(): lax.psum(attn_part.astype(jnp.bfloat16), 'tensor').astype(jnp.float32)  68.7 us
    psum x1, waiting for transfers between devices, on_device(): lax.psum(mlp_part.astype(jnp.bfloat16), 'tensor').astype(jnp.float32)  68.7 us
  transfers between devices with their start and end apart: 10, of which 7 were waited for; matrix products, arithmetic and copies ran while one was open for 7% of the time, Pallas kernels for 0%

commit v1 on v0

v1 whole, which is shorter than its diff:
```python
import functools

import jax
import jax.numpy as jnp
from jax import lax
from jax.experimental import pallas as pl
from jax.experimental.pallas import tpu as pltpu
from jax.sharding import PartitionSpec as P

SEQ_LEN = 8192
MAX_SEGMENT = 4096
EPSILON = 1e-05
GELU_SCALE = 0.7978845608028654
GELU_CUBIC = 0.044715
PAD = 16

f32 = jnp.float32
bf16 = jnp.bfloat16


def dot_nn(a, b):
    return lax.dot_general(a, b, (((1,), (0,)), ((), ())), preferred_element_type=f32)


def dot_nt(a, b):
    return lax.dot_general(a, b, (((1,), (1,)), ((), ())), preferred_element_type=f32)


def dot_tn(a, b):
    return lax.dot_general(a, b, (((0,), (0,)), ((), ())), preferred_element_type=f32)


def split(value):
    high = value.astype(bf16)
    return high, (value - high.astype(f32)).astype(bf16)


def norm_parts(values):
    centred = values - jnp.mean(values, axis=-1, keepdims=True)
    inverse = lax.rsqrt(jnp.mean(centred * centred, axis=-1, keepdims=True) + EPSILON)
    return centred * inverse, inverse


def norm_back(grad, normed, inverse, gain):
    scaled = grad * gain
    return inverse * (
        scaled
        - jnp.mean(scaled, axis=-1, keepdims=True)
        - normed * jnp.mean(scaled * normed, axis=-1, keepdims=True)
    )


def softmax_rows(values):
    raised = jnp.exp(values - jnp.max(values, axis=0, keepdims=True))
    return raised * (1.0 / jnp.sum(raised, axis=0, keepdims=True))


def relative(value):
    return ((value & 1) << 1) | (value >> 1)


def with_ones(values):
    width = values.shape[1]
    rows = lax.broadcasted_iota(jnp.int32, (PAD, width), 0)
    return jnp.concatenate([values, (rows == 0).astype(f32).astype(bf16)], axis=0)


def call(kernel, grid, ids, inputs, outputs, scratch, flops, vmem=None):
    moved = sum(a.size * a.dtype.itemsize for a, _, _ in inputs)
    return pl.pallas_call(
        kernel,
        grid_spec=pltpu.PrefetchScalarGridSpec(
            num_scalar_prefetch=1,
            grid=grid,
            in_specs=[pl.BlockSpec(block, index) for _, block, index in inputs],
            out_specs=[pl.BlockSpec(block, index) for _, _, block, index in outputs],
            scratch_shapes=scratch,
        ),
        out_shape=[jax.ShapeDtypeStruct(shape, kind) for shape, kind, _, _ in outputs],
        cost_estimate=pl.CostEstimate(flops=flops, bytes_accessed=moved, transcendentals=0),
        compiler_params=pltpu.CompilerParams(dimension_semantics=("arbitrary",) * len(grid)),
    )(ids, *[a for a, _, _ in inputs])


def whole(array):
    return (array, array.shape, lambda i, ids: (0,) * array.ndim)


def whole_out(shape, kind):
    return (shape, kind, shape, lambda i, ids: (0,) * len(shape))


def join_kernel(count, widths, flip, ids, *refs):
    pieces, outs = refs[:count], refs[count : count + len(widths)]
    rows = pieces[0].shape[0]
    place = ids[1]
    target = refs[-1] if flip else None
    for step in range(count):
        source = lax.rem(place - step + count, count)
        where = pl.ds(pl.multiple_of(source * rows, rows), rows)
        if flip:
            target[where, :] = pieces[step][...].astype(f32)
        else:
            at = 0
            for out, width in zip(outs, widths):
                out[where, :] = pieces[step][:, at : at + width]
                at += width
    if flip:
        outs[0][...] = target[...].T.astype(bf16)


def project_kernel(heads, ids, x, gain, shift, weight, bias, maps, seg, seg_last, attn_in, qkv, feats, state, total):
    step = pl.program_id(0)
    normed, _ = norm_parts(x[...].astype(f32))
    rows = (normed * gain[...] + shift[...]).astype(bf16)
    attn_in[...] = rows
    low = (dot_nt(weight[...], rows) + bias[...]).astype(bf16)
    qkv[...] = low
    width = low.shape[0] // 3
    size = width // heads
    mapped = [dot_nn(maps[part], low[part * width : (part + 1) * width]) for part in range(2)]

    @pl.when(step == 0)
    def _():
        total[...] = jnp.zeros_like(total)

    tail = (seg[...] == seg_last[:, -1:]).astype(f32).astype(bf16)
    for head in range(heads):
        for part in range(2):
            own = mapped[part][head * size : (head + 1) * size]
            both = jnp.concatenate([softmax_rows(own), softmax_rows(-own)], axis=0).astype(bf16)
            at = (part * heads + head) * 2 * size
            feats[at : at + 2 * size, :] = both
        value = with_ones(low[2 * width + head * size : 2 * width + (head + 1) * size])
        at = head * (size + PAD)
        total[at : at + size + PAD, :] += dot_nt(value * tail, both)
    used = heads * (size + PAD)

    @pl.when(step == pl.num_programs(0) - 1)
    def _():
        state[:used, :] = total[...].astype(bf16)
        state[used:, :] = jnp.broadcast_to(seg_last[:, -1:], (PAD, 2 * size)).astype(bf16)


def pair_mask(seg_col, seg_row):
    tile = seg_row.shape[1]
    early = lax.broadcasted_iota(jnp.int32, (tile, tile), 0)
    late = lax.broadcasted_iota(jnp.int32, (tile, tile), 1)
    return jnp.where(early <= late, (seg_col == seg_row).astype(f32), 0.0)


def attend_kernel(heads, pieces, hops, ids, qkv_v, feats, seg, seg_col, *refs):
    received, refs = refs[:hops], refs[hops:]
    attended, attended_low, denominators, states, state, previous = refs
    step = pl.program_id(0)
    size = qkv_v.shape[0] // heads
    rows = size + PAD
    used = heads * rows
    place = lax.rem(ids[1], pieces)

    @pl.when(step == 0)
    def _():
        start = jnp.zeros((used, 2 * size), f32)
        for hop in range(hops):
            latest = received[0][used : used + 1, :].astype(f32)
            linked = (received[hop][used : used + 1, :].astype(f32) == latest).astype(f32)
            linked = linked * (place > hop).astype(f32)
            start = start + linked * received[hop][:used, :].astype(f32)
        state[...] = start
        first = received[0][used : used + 1, :1].astype(f32)
        previous[...] = jnp.broadcast_to(jnp.where(place > 0, first, -2.0), previous.shape)

    row = seg[...]
    end = row[:, -1:]
    mask = pair_mask(seg_col[...], row)
    before = previous[...]
    carried = (row == before).astype(f32)
    tail = (row == end).astype(f32).astype(bf16)
    keep = (before[:, : 2 * size] == end).astype(f32)
    states[...] = state[...]
    for head in range(heads):
        query = feats[head * 2 * size : (head + 1) * 2 * size, :]
        key = feats[(heads + head) * 2 * size : (heads + head + 1) * 2 * size, :]
        value = with_ones(qkv_v[head * size : (head + 1) * size, :])
        scores = (dot_tn(key, query) * mask).astype(bf16)
        own = state[head * rows : (head + 1) * rows, :]
        inter = dot_nn(jnp.concatenate(split(own), axis=0), query)
        both = dot_nn(value, scores) + carried * (inter[:rows] + inter[rows:])
        lower = both[size : size + 1]
        result = both[:size] / lower
        attended[head * size : (head + 1) * size, :] = result
        attended_low[head * size : (head + 1) * size, :] = result.astype(bf16)
        denominators[head : head + 1, :] = lower
        state[head * rows : (head + 1) * rows, :] = keep * own + dot_nt(value * tail, key)
    previous[...] = jnp.broadcast_to(end, previous.shape)


def mlp_kernel(chunks, first, ids, x, cot, a0, a1, a2, a3, p0, p1, p2, p3, proj_bias, gain, shift, fc, out_t, fc_bias, *refs):
    if first:
        residual, out_part, grad_part, fc_acc, out_acc, bias_acc = refs
    else:
        fc_in, out_in, bias_in, residual, out_part, grad_part, vectors, bias_out = refs[:8]
        pieces = refs[8 : 8 + chunks]
        fc_acc, out_acc, bias_acc = refs[8 + chunks :]
    step = pl.program_id(0)

    @pl.when(step == 0)
    def _():
        if first:
            fc_acc[...] = jnp.zeros_like(fc_acc)
            out_acc[...] = jnp.zeros_like(out_acc)
            bias_acc[...] = jnp.zeros_like(bias_acc)
        else:
            fc_acc[...] = fc_in[...]
            out_acc[...] = out_in[...]
            bias_acc[...] = bias_in[...]

    resid = x[...].astype(f32) + proj_bias[...]
    for part, proj in zip((a0, a1, a2, a3), (p0, p1, p2, p3)):
        resid = resid + dot_nt(part[...].T, proj[...])
    residual[...] = resid
    normed, _ = norm_parts(resid)
    mlp_in = (normed * gain[...] + shift[...]).astype(bf16)
    preact = dot_nn(mlp_in, fc[...]) + fc_bias[...]
    square = preact * preact
    tangent = jnp.tanh(GELU_SCALE * (preact + GELU_CUBIC * square * preact))
    half = 0.5 * (1.0 + tangent)
    activ = (preact * half).astype(bf16)
    slope = half + 0.5 * preact * (1.0 - tangent * tangent) * GELU_SCALE * (1.0 + 3.0 * GELU_CUBIC * square)
    out_part[...] = dot_nt(activ, out_t[...]).astype(bf16)
    top = cot[...]
    grad_pre = (dot_nn(top, out_t[...]) * slope).astype(bf16)
    grad_part[...] = dot_nt(grad_pre, fc[...]).astype(bf16)
    fc_acc[...] += dot_tn(mlp_in, grad_pre)
    out_acc[...] += dot_tn(top, activ)
    bias_acc[...] += jnp.sum(grad_pre.astype(f32), axis=0, keepdims=True)
    if not first:

        @pl.when(step == pl.num_programs(0) - 1)
        def _():
            rows, width = fc_acc.shape[0] // chunks, fc_acc.shape[1]
            for ahead in range(chunks):
                source = lax.rem(ids[1] + ahead, chunks)
                where = pl.ds(pl.multiple_of(source * rows, rows), rows)
                pieces[ahead][:, :width] = fc_acc[where, :].astype(bf16)
                pieces[ahead][:, width:] = out_acc[where, :].astype(bf16)
            wide = fc[...].astype(f32)
            vectors[:, 0:1] = jnp.sum(wide * fc_acc[...], axis=1, keepdims=True)
            vectors[:, 1:2] = jnp.sum(wide * bias_acc[...], axis=1, keepdims=True)
            bias_out[...] = bias_acc[...]


def middle_kernel(ids, residual, cot, part, arrived, gain, grad_residual, grad_attn, sums):
    normed, inverse = norm_parts(residual[...])
    grad = part[...].astype(f32) + arrived[...].astype(f32)
    top = cot[...].astype(f32)
    total = top + norm_back(grad, normed, inverse, gain[...])
    grad_residual[...] = total
    low = total.astype(bf16)
    grad_attn[...] = low
    sums[0:1, :] = jnp.sum(low.astype(f32), axis=0, keepdims=True)
    sums[1:2, :] = jnp.sum(top, axis=0, keepdims=True)


def last_kernel(ids, x, part, arrived, grad_residual, gain, out):
    normed, inverse = norm_parts(x[...].astype(f32))
    grad = part[...].astype(f32) + arrived[...].astype(f32)
    out[...] = (grad_residual[...] + norm_back(grad, normed, inverse, gain[...])).astype(bf16)


def finish_kernel(ids, residual, part, arrived, bias, out):
    out[...] = (residual[...] + bias[...] + part[...].astype(f32) + arrived[...].astype(f32)).astype(bf16)


def order_kernel(count, ids, *refs):
    out = refs[count]
    for at in range(count):

        @pl.when(pl.program_id(0) == at)
        def _():
            out[...] = refs[at][...]


def grads_in_kernel(heads, pieces, first, ids, g0, g1, g2, g3, proj_t, feats_q, attended, attended_low, denominators, seg, seg_last_before, *refs):
    if first:
        grads, state, proj_acc, total = refs
    else:
        proj_in, grads, state, proj_acc, total = refs
    step = pl.program_id(0)
    size = attended.shape[0] // heads
    rows = size + PAD
    used = heads * rows

    @pl.when(step == 0)
    def _():
        total[...] = jnp.zeros_like(total)
        proj_acc[...] = jnp.zeros_like(proj_acc) if first else proj_in[...]

    def work(source):
        grad = source[...]
        proj_acc[...] += dot_nn(attended_low[...], grad)
        grad_att = dot_tn(proj_t[...], grad.T)
        before = seg_last_before[used : used + 1, :1].astype(f32)
        before = jnp.where(lax.rem(ids[1], pieces) > 0, before, -2.0)
        carried = (seg[...] == before).astype(f32)
        for head in range(heads):
            own = grad_att[head * size : (head + 1) * size]
            inverse = 1.0 / denominators[head : head + 1, :]
            lower = -inverse * jnp.sum(own * attended[head * size : (head + 1) * size, :], axis=0, keepdims=True)
            filler = lax.broadcasted_iota(jnp.int32, (PAD, own.shape[1]), 0)
            both = jnp.concatenate([own * inverse, jnp.where(filler == 0, lower, 0.0)], axis=0)
            grads[head * rows : (head + 1) * rows, :] = both
            query = feats_q[head * 2 * size : (head + 1) * 2 * size, :]
            sums = dot_nt(jnp.concatenate(split(both * carried), axis=0), query)
            total[head * rows : (head + 1) * rows, :] += sums[:rows] + sums[rows:]

    for at, source in enumerate((g0, g1, g2, g3)):

        @pl.when(step == at)
        def _():
            work(source)

    @pl.when(step == pl.num_programs(0) - 1)
    def _():
        state[:used, :] = total[...].astype(bf16)
        before = seg_last_before[used:, :].astype(f32)
        state[used:, :] = jnp.where(lax.rem(ids[1], pieces) > 0, before, -2.0).astype(bf16)


def softmax_back(grad, positive, negative):
    size = positive.shape[0]
    upper, lower = grad[:size], grad[size:]
    return positive * (upper - jnp.sum(positive * upper, axis=0, keepdims=True)) - negative * (
        lower - jnp.sum(negative * lower, axis=0, keepdims=True)
    )


def grads_kernel(
    heads, pieces, hops, chunks, first, ids, qkv, feats, grads, states, seg, seg_col, seg_before, attn_in, weight, maps, maps_back, *refs
):
    received, refs = refs[:hops], refs[hops:]
    if first:
        grad_part, weight_acc, map_acc, bias_acc, state, total = refs
    else:
        weight_in, map_in, bias_in, proj_in, gain, shift, grad_part, map_out, bias_out, vectors = refs[:10]
        outs = refs[10 : 10 + chunks]
        weight_acc, map_acc, bias_acc, state, total = refs[10 + chunks :]
    step = pl.program_id(0)
    count = pl.num_programs(0)
    width = qkv.shape[0] // 3
    size = width // heads
    rows = size + PAD
    used = heads * rows
    row = seg[...]
    end = row[:, -1:]

    @pl.when(step == 0)
    def _():
        start = jnp.zeros((used, 2 * size), f32)
        place = lax.rem(ids[1], pieces)
        for hop in range(hops):
            linked = (received[hop][used : used + 1, :].astype(f32) == end).astype(f32)
            linked = linked * (place + hop + 1 < pieces).astype(f32)
            start = start + linked * received[hop][:used, :].astype(f32)
        state[...] = start
        if first:
            weight_acc[...] = jnp.zeros_like(weight_acc)
            map_acc[...] = jnp.zeros_like(map_acc)
            bias_acc[...] = jnp.zeros_like(bias_acc)
        else:
            weight_acc[...] = weight_in[...]
            map_acc[...] = map_in[...]
            bias_acc[...] = bias_in[...]

    before = seg_before[...]
    mask = pair_mask(seg_col[...], row)
    carried = (row == before).astype(f32)
    tail = (row == end).astype(f32)
    keep = (before == end).astype(f32)
    mapped = [dot_nn(maps[part], qkv[part * width : (part + 1) * width, :]) for part in range(2)]
    back = [[], []]
    grad_values = []
    for head in range(heads):
        query = feats[head * 2 * size : (head + 1) * 2 * size, :]
        key = feats[(heads + head) * 2 * size : (heads + head + 1) * 2 * size, :]
        at = 2 * width + head * size
        value = with_ones(qkv[at : at + size, :])
        value_two = jnp.concatenate([value, value], axis=0)
        own = grads[head * rows : (head + 1) * rows, :]
        high, low = split(own)
        grad_two = jnp.concatenate([high, low], axis=0)
        scores = (dot_tn(key, query) * mask).astype(bf16)
        grad_scores = (dot_tn(value_two, grad_two) * mask).astype(bf16)
        into = states[head * rows : (head + 1) * rows, :]
        into_high, into_low = split(into)
        inter = dot_tn(
            jnp.concatenate([into_high, into_low, into_high], axis=0),
            jnp.concatenate([high, high, low], axis=0),
        )
        grad_query = dot_nn(key, grad_scores) + carried * inter
        after = state[head * rows : (head + 1) * rows, :]
        after_two = jnp.concatenate(split(after), axis=0)
        grad_key = dot_nt(query, grad_scores) + tail * dot_tn(after_two, value_two)
        straight = dot_nt(grad_two, scores)
        through = dot_nn(after_two, key)
        grad_values.append(
            straight[:size] + straight[rows : rows + size] + tail * (through[:size] + through[rows : rows + size])
        )
        carried_two = jnp.concatenate(split(own * carried), axis=0)
        added = dot_nt(carried_two, query)
        state[head * rows : (head + 1) * rows, :] = keep * after + added[:rows] + added[rows:]
        for part, grad in ((0, grad_query), (1, grad_key)):
            plain = mapped[part][head * size : (head + 1) * size]
            back[part].append(softmax_back(grad, softmax_rows(plain), softmax_rows(-plain)))
    pieces_low = []
    for part in range(2):
        grad_mapped = jnp.concatenate(back[part], axis=0).astype(bf16)
        map_acc[part] += dot_nt(qkv[part * width : (part + 1) * width, :], grad_mapped)
        pieces_low.append(dot_nn(maps_back[part], grad_mapped))
    pieces_low.append(jnp.concatenate(grad_values, axis=0))
    grad_qkv = jnp.concatenate(pieces_low, axis=0).astype(bf16)
    grad_part[...] = dot_tn(grad_qkv, weight[...]).astype(bf16)
    weight_acc[...] += dot_nn(grad_qkv, attn_in[...])
    bias_acc[...] += jnp.sum(grad_qkv.astype(f32), axis=1, keepdims=True)
    if not first:

        @pl.when(step == count - 1)
        def _():
            total[:, : 3 * width] = weight_acc[...].T
            total[:, 3 * width :] = proj_in[...].T
            chunk = total.shape[0] // chunks
            for ahead in range(chunks):
                source = lax.rem(ids[1] + ahead, chunks)
                where = pl.ds(pl.multiple_of(source * chunk, chunk), chunk)
                outs[ahead][...] = total[where, :].astype(bf16)
            wide = weight[...].astype(f32)
            grad_shift = jnp.sum(wide * bias_acc[...], axis=0, keepdims=True)
            grad_gain = jnp.sum(wide * weight_acc[...], axis=0, keepdims=True)
            vectors[0:1, :] = (grad_gain - shift[...] * grad_shift) / gain[...]
            vectors[1:2, :] = grad_shift
            map_out[...] = map_acc[...]
            bias_out[...] = bias_acc[...]


def around(array, axis, shift, size):
    return lax.ppermute(array, axis, [(i, (i + shift) % size) for i in range(size)])


def swap(array, bit):
    return lax.ppermute(array, "tensor", [(i, i ^ bit) for i in range(4)])


def gather_tensor(array):
    across = swap(array, 2)
    return (array, across, swap(array, 1), swap(across, 1))


def scatter_tensor(parts):
    arrived = swap(parts[2:], 1)
    sums = (parts[:2].astype(f32) + arrived.astype(f32)).astype(bf16)
    return sums[0], swap(sums[1], 2)


def block_diagonal(blocks):
    count, size, _ = blocks.shape
    eye = jnp.eye(count, dtype=blocks.dtype)
    return (eye[:, None, :, None] * blocks[:, :, None, :]).reshape(count * size, count * size)


def on_device(
    inputs, cotangent, segment, attn_gain, attn_shift, qkv_weight, qkv_bias, query_map, key_map,
    proj_weight, proj_bias, mlp_gain, mlp_shift, fc_weight, fc_bias, out_weight, out_bias,
):
    micro, tokens, dim = inputs.shape
    heads, size, _ = query_map.shape
    width = heads * size
    units = fc_weight.shape[1]
    count = lax.axis_size("dp")
    tiles = lax.axis_size("tensor")
    tile = tokens // tiles
    pieces = SEQ_LEN // tokens
    hops = min(-(-MAX_SEGMENT // tokens), pieces - 1)
    rows = size + PAD
    used = heads * rows
    shard = dim // count
    direct = shard % 16 == 0
    chunks = count if direct else 1
    place = lax.axis_index("dp")
    ids = jnp.stack([lax.axis_index("tensor"), place]).astype(jnp.int32)

    qkv_own = qkv_weight.reshape(shard, 3 * width)
    rest_own = jnp.concatenate([fc_weight, out_weight.T, proj_weight.T], axis=1)
    if direct:
        qkv_pieces = [qkv_own] + [around(qkv_own, "dp", k, count) for k in range(1, count)]
        rest_own, qkv_pieces = lax.optimization_barrier((rest_own, qkv_pieces))
        rest_pieces = [rest_own] + [around(rest_own, "dp", k, count) for k in range(1, count)]
        (weight_t,) = call(
            functools.partial(join_kernel, count, (3 * width,), True), (1,), ids,
            [whole(a) for a in qkv_pieces], [whole_out((3 * width, dim), bf16)],
            [pltpu.VMEM((dim, 3 * width), f32)], 0,
        )
        fc_full, out_t, proj_t = call(
            functools.partial(join_kernel, count, (units, units, width), False), (1,), ids,
            [whole(a) for a in rest_pieces],
            [whole_out((dim, units), bf16), whole_out((dim, units), bf16), whole_out((dim, width), bf16)],
            [], 0,
        )
    else:
        weight_t = lax.all_gather(qkv_own, "dp", axis=0, tiled=True).T
        rest = lax.all_gather(rest_own, "dp", axis=0, tiled=True)
        fc_full, out_t, proj_t = rest[:, :units], rest[:, units : 2 * units], rest[:, 2 * units :]
    proj_slots = gather_tensor(proj_t)

    row = lambda v: v.astype(f32).reshape(1, -1)
    gain_a, shift_a, gain_m, shift_m = row(attn_gain), row(attn_shift), row(mlp_gain), row(mlp_shift)
    bias_p, bias_f, bias_o = row(proj_bias), row(fc_bias), row(out_bias)
    bias_qkv = qkv_bias.astype(f32).reshape(3 * width, 1)
    maps_back = jnp.stack([block_diagonal(query_map), block_diagonal(key_map)])
    maps = jnp.swapaxes(maps_back, 1, 2)
    seg = segment.astype(f32).reshape(micro, tiles, 1, tile)
    seg_col = segment.astype(f32).reshape(micro, tiles, tile, 1)

    def rows_of(array, m, at=None):
        return (array, (None, tile, dim), lambda i, ids: (m, i if at is None else at(i, ids), 0))

    def own_rows(array, m):
        return (array, (None, tile, dim), lambda i, ids: (m, ids[0], 0))

    def columns(array, at=None):
        return (array, (array.shape[0], tile), lambda i, ids: (0, i if at is None else at(i, ids)))

    def columns_out(height, kind, at=None):
        return ((height, tokens), kind, (height, tile), lambda i, ids: (0, i if at is None else at(i, ids)))

    def seg_row(m, at=None):
        return (seg, (None, None, 1, tile), lambda i, ids: (m, i if at is None else at(i, ids), 0, 0))

    def seg_column(m, at=None):
        return (seg_col, (None, None, tile, 1), lambda i, ids: (m, i if at is None else at(i, ids), 0, 0))

    slots_out = lambda at=None: (
        (tiles, tile, dim), bf16, (None, tile, dim),
        lambda i, ids: (relative(ids[0] ^ (i if at is None else at(i, ids))), 0, 0),
    )
    near = lambda i, ids: ids[0] ^ relative(i)

    attn_ins, qkvs, feats, incoming = [], [], [], []
    for m in range(micro):
        attn_in, qkv, feat, state = call(
            functools.partial(project_kernel, heads), (tiles,), ids,
            [
                rows_of(inputs, m), whole(gain_a), whole(shift_a), whole(weight_t), whole(bias_qkv), whole(maps),
                seg_row(m), seg_row(m, lambda i, ids: tiles - 1),
            ],
            [
                ((tokens, dim), bf16, (tile, dim), lambda i, ids: (i, 0)),
                columns_out(3 * width, bf16), columns_out(4 * width, bf16), whole_out((used + PAD, 2 * size), bf16),
            ],
            [pltpu.VMEM((used, 2 * size), f32)],
            2 * tokens * dim * 3 * width,
        )
        attn_ins.append(attn_in)
        qkvs.append(qkv)
        feats.append(feat)
        incoming.append([
            lax.ppermute(state, "dp", [(i, i + k) for i in range(count - k)]) for k in range(1, hops + 1)
        ])
    attended, attended_low, denominators, states, slots = [], [], [], [], []
    for m in range(micro):
        result = call(
            functools.partial(attend_kernel, heads, pieces, hops), (tiles,), ids,
            [
                (qkvs[m], (width, tile), lambda i, ids: (2, i)), columns(feats[m]), seg_row(m), seg_column(m),
            ]
            + [whole(a) for a in incoming[m]],
            [
                columns_out(width, f32), columns_out(width, bf16), columns_out(8, f32),
                ((tiles, used, 2 * size), f32, (None, used, 2 * size), lambda i, ids: (i, 0, 0)),
            ],
            [pltpu.VMEM((used, 2 * size), f32), pltpu.VMEM((1, tile), f32)],
            4 * tokens * tile * width,
        )
        attended.append(result[0])
        attended_low.append(result[1])
        denominators.append(result[2])
        states.append(result[3])
        slots.append(gather_tensor(result[1]))

    acc = ()
    residuals, out_parts, mlp_parts = [], [], []
    for m in range(micro):
        first = m == 0
        final = m == micro - 1
        result = call(
            functools.partial(mlp_kernel, chunks, not final), (tiles,), ids,
            [rows_of(inputs, m), rows_of(cotangent, m)]
            + [columns(a) for a in slots[m]]
            + [whole(a) for a in proj_slots]
            + [whole(a) for a in (bias_p, gain_m, shift_m, fc_full, out_t, bias_f)]
            + [whole(a) for a in acc],
            [
                ((tiles, tile, dim), f32, (None, tile, dim), lambda i, ids: (i, 0, 0)),
                slots_out(), slots_out(),
            ]
            + (
                [whole_out((dim, 2), f32), whole_out((1, units), f32)]
                + [whole_out((dim // chunks, 2 * units), bf16)] * chunks
                if final
                else [whole_out((dim, units), f32), whole_out((dim, units), f32), whole_out((1, units), f32)]
            ),
            [pltpu.VMEM((dim, units), f32), pltpu.VMEM((dim, units), f32), pltpu.VMEM((1, units), f32)] if final else [],
            2 * tokens * dim * (dim + 6 * units),
        )
        residuals.append(result[0])
        out_parts.append(result[1])
        mlp_parts.append(result[2])
        acc = result[3:]
    mlp_vectors, grad_fc_bias, rest_grads = acc[0], acc[1], acc[2:]

    grad_residuals, grad_slots, row_sums, outputs = [], [], [], []
    own_tile = lambda array: (array, (None, tile, dim), lambda i, ids: (ids[0], 0, 0))
    for m in range(micro):
        kept, arrived = scatter_tensor(mlp_parts[m])
        grad_residual, grad_attn, sums = call(
            middle_kernel, (1,), ids,
            [own_tile(residuals[m]), own_rows(cotangent, m), whole(kept), whole(arrived), whole(gain_m)],
            [whole_out((tile, dim), f32), whole_out((tile, dim), bf16), whole_out((2, dim), f32)],
            [], 0,
        )
        grad_residuals.append(grad_residual)
        grad_slots.append(gather_tensor(grad_attn))
        row_sums.append(sums)
    if direct:
        rest_terms = [rest_grads[0]] + [around(rest_grads[k], "dp", k, count) for k in range(1, count)]
        rest_sum = sum(a.astype(f32) for a in rest_terms)
    else:
        rest_sum = lax.psum_scatter(rest_grads[0], "dp", scatter_dimension=0, tiled=True).astype(f32)
    for m in range(micro):
        kept, arrived = scatter_tensor(out_parts[m])
        (finished,) = call(
            finish_kernel, (1,), ids,
            [own_tile(residuals[m]), whole(kept), whole(arrived), whole(bias_o)],
            [whole_out((tile, dim), bf16)], [], 0,
        )
        outputs.append(gather_tensor(finished))

    proj_acc = ()
    grads, returned = [], []
    for m in range(micro):
        first = m == 0
        result = call(
            functools.partial(grads_in_kernel, heads, pieces, first), (tiles,), ids,
            [whole(a) for a in grad_slots[m]]
            + [
                whole(proj_t), (feats[m], (2 * width, tile), lambda i, ids: (0, near(i, ids))),
                columns(attended[m], near), columns(attended_low[m], near), columns(denominators[m], near),
                seg_row(m, near), whole(incoming[m][0]),
            ]
            + [whole(a) for a in proj_acc],
            [columns_out(used, f32, near), whole_out((used + PAD, 2 * size), bf16), whole_out((width, dim), f32)],
            [pltpu.VMEM((used, 2 * size), f32)],
            4 * tokens * dim * width,
        )
        grads.append(result[0])
        proj_acc = (result[2],)
        returned.append([
            lax.ppermute(result[1], "dp", [(i + k, i) for i in range(count - k)]) for k in range(1, hops + 1)
        ])
    acc = ()
    attn_parts = []
    turned = lambda i, ids: tiles - 1 - i
    for m in range(micro):
        first = m == 0
        final = m == micro - 1
        lasts = jnp.concatenate([
            jnp.where(place % pieces > 0, incoming[m][0][used, 0].astype(f32), -2.0)[None],
            seg[m, :-1, 0, -1],
        ]).reshape(tiles, 1, 1)
        result = call(
            functools.partial(grads_kernel, heads, pieces, hops, chunks, not final), (tiles,), ids,
            [
                columns(qkvs[m], turned), columns(feats[m], turned), columns(grads[m], turned),
                (states[m], (None, used, 2 * size), lambda i, ids: (tiles - 1 - i, 0, 0)),
                seg_row(m, turned), seg_column(m, turned),
                (lasts, (None, 1, 1), lambda i, ids: (tiles - 1 - i, 0, 0)),
                (attn_ins[m], (tile, dim), lambda i, ids: (tiles - 1 - i, 0)),
                whole(weight_t), whole(maps), whole(maps_back),
            ]
            + [whole(a) for a in returned[m]]
            + [whole(a) for a in acc]
            + ([whole(a) for a in (proj_acc[0], gain_a, shift_a)] if final else []),
            [slots_out(turned)]
            + (
                [whole_out((2, width, width), f32), whole_out((3 * width, 1), f32), whole_out((2, dim), f32)]
                + [whole_out((dim // chunks, 4 * width), bf16)] * chunks
                if final
                else [whole_out((3 * width, dim), f32), whole_out((2, width, width), f32), whole_out((3 * width, 1), f32)]
            ),
            (
                [pltpu.VMEM((3 * width, dim), f32), pltpu.VMEM((2, width, width), f32), pltpu.VMEM((3 * width, 1), f32)]
                if final
                else []
            )
            + [pltpu.VMEM((used, 2 * size), f32), pltpu.VMEM((dim, 4 * width), f32)],
            4 * tokens * dim * 3 * width + 16 * tokens * tile * width,
        )
        attn_parts.append(result[0])
        acc = result[1:]
    grad_maps, grad_qkv_bias, attn_vectors, qkv_grads = acc[0], acc[1], acc[2], acc[3:]
    if direct:
        qkv_terms = [qkv_grads[0]] + [around(qkv_grads[k], "dp", k, count) for k in range(1, count)]
        qkv_sum = sum(a.astype(f32) for a in qkv_terms)
    else:
        qkv_sum = lax.psum_scatter(qkv_grads[0], "dp", scatter_dimension=0, tiled=True).astype(f32)
    input_grads = []
    for m in range(micro):
        kept, arrived = scatter_tensor(attn_parts[m])
        (finished,) = call(
            last_kernel, (1,), ids,
            [own_rows(inputs, m), whole(kept), whole(arrived), whole(grad_residuals[m]), whole(gain_a)],
            [whole_out((tile, dim), bf16)], [], 0,
        )
        input_grads.append(gather_tensor(finished))

    def ordered(slots_of):
        flat = [a for slot in slots_of for a in slot]
        (result,) = call(
            functools.partial(order_kernel, len(flat)), (len(flat),), ids,
            [whole(a) for a in flat],
            [(
                (micro, tokens, dim), bf16, (None, tile, dim),
                lambda i, ids: (lax.div(i, tiles), ids[0] ^ relative(lax.rem(i, tiles)), 0),
            )],
            [], 0,
        )
        return result

    mlp_shift_grad = mlp_vectors[:, 1]
    mlp_gain_grad = (mlp_vectors[:, 0] - mlp_shift.astype(f32) * mlp_shift_grad) / mlp_gain.astype(f32)
    shared = jnp.concatenate([attn_vectors, sum(row_sums), mlp_gain_grad[None], mlp_shift_grad[None]], axis=0)
    shared = shared + swap(shared, 1)
    shared = shared + swap(shared, 2)
    blocks = jnp.stack([
        grad_maps[:, h * size : (h + 1) * size, h * size : (h + 1) * size] for h in range(heads)
    ], axis=1)
    small = jnp.concatenate([
        shared.reshape(-1, 2 * size), blocks.reshape(-1, 2 * size), grad_fc_bias.reshape(-1, 2 * size),
        jnp.pad(grad_qkv_bias.reshape(-1), (0, -(3 * width) % (2 * size))).reshape(-1, 2 * size),
    ], axis=0)
    if direct:
        small_low = small.astype(bf16)
        terms = [around(small_low, "dp", k, count) for k in range(1, count)]
        small = small + sum(a.astype(f32) for a in terms)
        small = lax.optimization_barrier(small)
    else:
        small = lax.psum(small, "dp")
    n_shared = 6 * dim // (2 * size)
    n_blocks = 2 * heads * size * size // (2 * size)
    n_units = units // (2 * size)
    shared = small[:n_shared].reshape(6, dim)
    blocks = small[n_shared : n_shared + n_blocks].reshape(2, heads, size, size)
    grad_fc_bias = small[n_shared + n_blocks : n_shared + n_blocks + n_units].reshape(units)
    grad_qkv_bias = small[n_shared + n_blocks + n_units :].reshape(-1)[: 3 * width].reshape(3, width)
    return (
        ordered(outputs),
        ordered(input_grads),
        shared[0],
        shared[1],
        qkv_sum[:, : 3 * width].reshape(shard, 3, width),
        grad_qkv_bias,
        blocks[0],
        blocks[1],
        qkv_sum[:, 3 * width :].T,
        shared[2],
        shared[4],
        shared[5],
        rest_sum[:, :units],
        grad_fc_bias,
        rest_sum[:, units:].T,
        shared[3],
    )


def solution(mesh):
    in_specs = (
        P(None, "dp", None), P(None, "dp", None), P(None, "dp"), P(), P(), P("dp", None, "tensor"),
        P(None, "tensor"), P("tensor", None, None), P("tensor", None, None), P("tensor", "dp"), P(), P(), P(),
        P("dp", "tensor"), P("tensor"), P("tensor", "dp"), P(),
    )
    out_specs = (
        P(None, "dp", None), P(None, "dp", None), P(), P(), P("dp", None, "tensor"), P(None, "tensor"),
        P("tensor", None, None), P("tensor", None, None), P("tensor", "dp"), P(), P(), P(),
        P("dp", "tensor"), P("tensor"), P("tensor", "dp"), P(),
    )
    return jax.shard_map(
        on_device, mesh=mesh, in_specs=in_specs, out_specs=out_specs, check_vma=False
    )
```

time: 1480 us -> 454 us (0.31)
  blocking collectives: 416 us -> 0 us
  waiting for transfers between devices: 410 us -> 72.8 us
  local copies, waits for them, and re-layouts: 279 us -> 38.7 us
  matrix products: 202 us -> 0 us
  starting transfers between devices: 1.06 us -> 163 us
  Pallas kernels: 0 us -> 154 us
  other arithmetic: 97.1 us -> 12.8 us
  loops' own time: 37.4 us -> 0 us
  between operations: 24.1 us -> 3.75 us
    all_gather x10 -> x0, blocking collectives: 398 us -> none  [the longest x4 162 us: carried_in(): lax.all_gather(a.astype(kind), axis)]
    psum x4 -> x0, waiting for transfers between devices: 265 us -> none  [the longest x1 78 us: on_device(): lax.psum((norm_attn_g, norm_attn_s, totals[3], totals[4], totals[5], tota...]
    dot_general x74 -> x0, matrix products: 178 us -> none  [the longest x2 9.97 us: on_device(): jnp.einsum('td,tce->dce', attn_in, grad_qkv, preferred_element_type=f32)]
    ppermute x0 -> x92, starting transfers between devices: none -> 163 us  [the longest x35 92.6 us: around(): lax.ppermute(array, axis, [(i, (i + shift) % size) for i in range(size)])]
    pallas_call x0 -> x20, Pallas kernels: none -> 154 us  [call(): pl.pallas_call(kernel, grid_spec=pltpu.PrefetchScalarGridSpec(num_scalar_...]
    reduce_scatter x3 -> x0, waiting for transfers between devices: 143 us -> none  [the longest x1 73.1 us: on_device(): lax.psum_scatter(totals[2], 'dp', scatter_dimension=0, tiled=True)]
    ppermute x0 -> x92, waiting for transfers between devices: none -> 72.8 us  [the longest x41 39.1 us: swap(): return lax.ppermute(array, 'tensor', [(i, i ^ bit) for i in range(4)])]
    concatenate x24 -> x0, local copies, waits for them, and re-layouts: 58.3 us -> none  [feature_map(): return (jnp.concatenate([positive, negative], axis=-1), positive, negative)]
  transfers between devices with their start and end apart: 10 -> 92, of which waited for: 7 -> 22; matrix products, arithmetic and copies ran while one was open for 7% -> 9% of each run, Pallas kernels for 0% -> 25%
where the time goes in v1:
time: 454 us; the launch traced here: 446 us
  starting transfers between devices  163 us (36%)
  Pallas kernels  154 us (34%)
  waiting for transfers between devices  72.8 us (16%)
  local copies, waits for them, and re-layouts  38.7 us (9%)
  other arithmetic  12.8 us (3%)
    pallas_call x20, Pallas kernels, call(): pl.pallas_call(kernel, grid_spec=pltpu.PrefetchScalarGridSpec(num_scalar_...  154 us
    ppermute x35, starting transfers between devices, around(): lax.ppermute(array, axis, [(i, (i + shift) % size) for i in range(size)])  92.6 us
    ppermute x8, starting transfers between devices, on_device(): lax.ppermute(state, 'dp', [(i, i + k) for i in range(count - k)])  39.9 us
    ppermute x41, waiting for transfers between devices, swap(): return lax.ppermute(array, 'tensor', [(i, i ^ bit) for i in range(4)])  39.1 us
    ppermute x35, waiting for transfers between devices, around(): lax.ppermute(array, axis, [(i, (i + shift) % size) for i in range(size)])  25 us
    ppermute x41, starting transfers between devices, swap(): return lax.ppermute(array, 'tensor', [(i, i ^ bit) for i in range(4)])  20.2 us
    ppermute x8, starting transfers between devices, on_device(): lax.ppermute(result[1], 'dp', [(i + k, i) for i in range(count - k)])  10.7 us
    unnamed x201, local copies, waits for them, and re-layouts  10.5 us
  transfers between devices with their start and end apart: 92, of which 22 were waited for; matrix products, arithmetic and copies ran while one was open for 9% of the time, Pallas kernels for 25%

profile of v1, /device:TPU:0, one launch (start us, length us, event | category | flops | bytes accessed | tf_op | source)
XLA Modules:
  0.0 445.8 jit_solution(16308987038321272536)
XLA Ops:
  22.4 4.1 collective-permute-done.5.refs_6_
  41.0 9.0 %shard_map.289 = (bf16[1024,768]{1,0:T(8,128)(2,1)}, bf16[576,1024]{1,0:T(8,128)(2,1)}, bf16[768,1024]{1,0:T(8,128)(2,1)}, bf16[256,128]{1,0:T(8,128)(2,1)}) custom-call(s32[2]{0:T(128)} %pad_add_fusion.ids, bf16[2,1024,768]{2,1,0:T(8,128)(2,1)} %x.13, f32[1,768]{1,0:T(1,128)} %reshape.215.gain.refs_8_, f32[1,768]{1,0:T(1,128)} %reshape.217.shift.refs_9_, ...), custom_call_target="tpu_custom_call" | custom-call | flops 905969664 | bytes 4202752 | tf_op jit(solution)/shard_map/pallas_call | solution.py:70
  53.6 4.1 collective-permute-start.7
  60.8 8.1 %collective-permute-start.9 = (bf16[256,128]{1,0:T(8,128)(2,1)}, bf16[256,128]{1,0:T(8,128)(2,1)S(1)}, u32[]{:S(2)}, u32[]{:S(2)}) collective-permute-start(bf16[256,128]{1,0:T(8,128)(2,1)} %get-tuple-element.101), channel_id=1, source_target_pairs={{0,12},{4,16},{8,20},{12,24},{16,28},{1,13},{5,17},{9,21},{13,25},... | collective-permute-start | bytes 196616 | tf_op jit(solution)/shard_map/ppermute | solution.py:566
  71.7 23.4 %collective-permute-start.18 = (bf16[96,1728]{1,0:T(8,128)(2,1)S(1)}, bf16[96,1728]{1,0:T(8,128)(2,1)S(1)}, u32[]{:S(2)}, u32[]{:S(2)}) collective-permute-start(bf16[96,1728]{1,0:T(8,128)(2,1)S(1)} %pad_maximum_fusion.refs_0_), channel_id=1, source_target_pairs={{0,20},{4,24},{8,28},{12,0},{16,4},{20,8},{24,12},{28,16},{1,21},{... | collective-permute-start | bytes 995336 | tf_op jit(solution)/shard_map/ppermute | solution.py:446
  98.7 6.5 %shard_map.290 = (f32[192,1024]{1,0:T(8,128)}, bf16[192,1024]{1,0:T(8,128)(2,1)}, f32[8,1024]{1,0:T(8,128)}, f32[4,240,128]{2,1,0:T(8,128)}) custom-call(s32[2]{0:T(128)} %pad_add_fusion.ids, bf16[576,1024]{1,0:T(8,128)(2,1)} %get-tuple-element.99.qkv_v.qkv, bf16[768,1024]{1,0:T(8,128)(2,1)} %get-tuple-element.100.feats.feats_q, ...), custom_call_target="tpu_custom_call" | custom-call | flops 201326592 | bytes 3031040 | tf_op jit(solution)/shard_map/pallas_call | solution.py:70
  110.3 4.1 shard_map.291
  115.9 9.0 %shard_map.294 = (bf16[1024,768]{1,0:T(8,128)(2,1)}, bf16[576,1024]{1,0:T(8,128)(2,1)}, bf16[768,1024]{1,0:T(8,128)(2,1)}, bf16[256,128]{1,0:T(8,128)(2,1)}) custom-call(s32[2]{0:T(128)} %pad_add_fusion.ids, bf16[2,1024,768]{2,1,0:T(8,128)(2,1)} %x.13, f32[1,768]{1,0:T(1,128)} %reshape.215.gain.refs_8_, f32[1,768]{1,0:T(1,128)} %reshape.217.shift.refs_9_, ...), custom_call_target="tpu_custom_call" | custom-call | flops 905969664 | bytes 4202752 | tf_op jit(solution)/shard_map/pallas_call | solution.py:70
  127.0 10.3 %collective-permute-start.30 = (bf16[256,128]{1,0:T(8,128)(2,1)}, bf16[256,128]{1,0:T(8,128)(2,1)S(1)}, u32[]{:S(2)}, u32[]{:S(2)}) collective-permute-start(bf16[256,128]{1,0:T(8,128)(2,1)} %get-tuple-element.111), channel_id=1, source_target_pairs={{0,8},{4,12},{8,16},{12,20},{16,24},{20,28},{1,9},{5,13},{9,17},{1... | collective-permute-start | bytes 196616 | tf_op jit(solution)/shard_map/ppermute | solution.py:566
  138.6 7.5 %collective-permute-start.32 = (bf16[256,128]{1,0:T(8,128)(2,1)}, bf16[256,128]{1,0:T(8,128)(2,1)S(1)}, u32[]{:S(2)}, u32[]{:S(2)}) collective-permute-start(bf16[256,128]{1,0:T(8,128)(2,1)} %get-tuple-element.111), channel_id=1, source_target_pairs={{0,16},{4,20},{8,24},{12,28},{1,17},{5,21},{9,25},{13,29},{2,18},{... | collective-permute-start | bytes 196616 | tf_op jit(solution)/shard_map/ppermute | solution.py:566
  148.8 6.7 %shard_map.295 = (f32[192,1024]{1,0:T(8,128)}, bf16[192,1024]{1,0:T(8,128)(2,1)}, f32[8,1024]{1,0:T(8,128)}, f32[4,240,128]{2,1,0:T(8,128)}) custom-call(s32[2]{0:T(128)} %pad_add_fusion.ids, bf16[576,1024]{1,0:T(8,128)(2,1)} %get-tuple-element.109.qkv_v.qkv, bf16[768,1024]{1,0:T(8,128)(2,1)} %get-tuple-element.110.feats.feats_q, ...), custom_call_target="tpu_custom_call" | custom-call | flops 201326592 | bytes 3031040 | tf_op jit(solution)/shard_map/pallas_call | solution.py:70
  159.4 4.9 %collective-permute-done.33.a1 = bf16[192,1024]{1,0:T(8,128)(2,1)S(1)} collective-permute-done((bf16[192,1024]{1,0:T(8,128)(2,1)}, bf16[192,1024]{1,0:T(8,128)(2,1)S(1)}, u32[]{:S(2)}, u32[]{:S(2)}) %collective-permute-start.33) | collective-permute-done | bytes 393248 | tf_op jit(solution)/shard_map/ppermute | solution.py:450
  165.9 18.7 %shard_map.292 = (f32[4,256,768]{2,1,0:T(8,128)}, bf16[4,256,768]{2,1,0:T(8,128)(2,1)}, bf16[4,256,768]{2,1,0:T(8,128)(2,1)}, f32[768,768]{1,0:T(8,128)}, f32[768,768]{1,0:T(8,128)}, /*index=5*/f32[1,768]{1,0:T(1,128)}) custom-call(s32[2]{0:T(128)} %pad_add_fusion.ids, bf16[2,1024,768]{2,1,0:T(8,128)(2,1)} %x.13, bf16[2,1024,768]{2,1,0:T(8,128)(2,1)} %cot.7, ...), custom_call_target="tpu_custom_call" | custom-call | flops 8455716864 | bytes 11415552 | tf_op jit(solution)/shard_map/pallas_call | solution.py:70
  185.5 21.3 %shard_map.296 = (f32[4,256,768]{2,1,0:T(8,128)}, bf16[4,256,768]{2,1,0:T(8,128)(2,1)}, bf16[4,256,768]{2,1,0:T(8,128)(2,1)}, f32[768,2]{1,0:T(8,128)}, f32[1,76...) custom-call(s32[2]{0:T(128)} %pad_add_fusion.ids, ...), custom_call_target="tpu_custom_call" | custom-call | flops 8455716864 | bytes 16137216 | tf_op jit(solution)/shard_map/pallas_call | solution.py:70
  228.0 4.7 %collective-permute-done.42.arrived = bf16[256,768]{1,0:T(8,128)(2,1)S(1)} collective-permute-done((bf16[256,768]{1,0:T(8,128)(2,1)S(1)}, bf16[256,768]{1,0:T(8,128)(2,1)S(1)}, u32[]{:S(2)}, u32[]{:S(2)}) %collective-permute-start.42) | collective-permute-done | bytes 393248 | tf_op jit(solution)/shard_map/ppermute | solution.py:450
  235.7 3.8 shard_map.303
  239.6 3.9 shard_map.299
  244.0 4.6 %collective-permute-done.87 = bf16[96,1536]{1,0:T(8,128)(2,1)} collective-permute-done((bf16[96,1536]{1,0:T(8,128)(2,1)}, bf16[96,1536]{1,0:T(8,128)(2,1)}, u32[]{:S(2)}, u32[]{:S(2)}) %collective-permute-start.87) | collective-permute-done | bytes 294944 | tf_op jit(solution)/shard_map/ppermute | solution.py:446
  250.6 3.8 collective-permute-start.89
  278.4 7.4 %collective-permute-done.38.refs_5_ = bf16[256,768]{1,0:T(8,128)(2,1)S(1)} collective-permute-done((bf16[256,768]{1,0:T(8,128)(2,1)S(1)}, bf16[256,768]{1,0:T(8,128)(2,1)S(1)}, u32[]{:S(2)}, u32[]{:S(2)}) %collective-permute-start.38) | collective-permute-done | bytes 393248 | tf_op jit(solution)/shard_map/ppermute | solution.py:450
  285.8 6.7 %collective-permute-done.26.refs_1_ = bf16[256,768]{1,0:T(8,128)(2,1)} collective-permute-done((bf16[256,768]{1,0:T(8,128)(2,1)}, bf16[256,768]{1,0:T(8,128)(2,1)}, u32[]{:S(2)}, u32[]{:S(2)}) %collective-permute-start.26) | collective-permute-done | bytes 393248 | tf_op jit(solution)/shard_map/ppermute | solution.py:450
  295.0 6.7 %shard_map.300 = (f32[240,1024]{1,0:T(8,128)}, bf16[256,128]{1,0:T(8,128)(2,1)}, f32[192,768]{1,0:T(8,128)}) custom-call(s32[2]{0:T(128)} %pad_add_fusion.ids, bf16[256,768]{1,0:T(8,128)(2,1)} %get-tuple-element.119.g0, bf16[256,768]{1,0:T(8,128)(2,1)} %copy-done.16, bf16[256,768]{1,0:T(8,128)(2,1)} %collective-permute-done.44.g2, ...), custom_call_target="tpu_custom_call" | custom-call | flops 603979776 | bytes 4726784 | tf_op jit(solution)/shard_map/pallas_call | solution.py:70
  307.8 7.0 %shard_map.304 = (f32[240,1024]{1,0:T(8,128)}, bf16[256,128]{1,0:T(8,128)(2,1)}, f32[192,768]{1,0:T(8,128)}) custom-call(s32[2]{0:T(128)} %pad_add_fusion.ids, bf16[256,768]{1,0:T(8,128)(2,1)} %get-tuple-element.129.g0, bf16[256,768]{1,0:T(8,128)(2,1)} %copy-done.14, bf16[256,768]{1,0:T(8,128)(2,1)} %copy-done.17, ...), custom_call_target="tpu_custom_call" | custom-call | flops 603979776 | bytes 5316608 | tf_op jit(solution)/shard_map/pallas_call | solution.py:70
  316.3 5.8 %shard_map.298 = bf16[2,1024,768]{2,1,0:T(8,128)(2,1)} custom-call(s32[2]{0:T(128)} %pad_add_fusion.ids, bf16[256,768]{1,0:T(8,128)(2,1)} %shard_map.293.refs_0_, bf16[256,768]{1,0:T(8,128)(2,1)} %collective-permute-done.26.refs_1_, bf16[256,768]{1,0:T(8,128)(2,1)} %copy-done.24, bf16[256,768]{1,0:T(8,128)(2,1)} %collective-permute-done.28.refs_3_, ...), custom_call_target="tpu_custom_call" | custom-call | bytes 3145728 | tf_op jit(solution)/shard_map/pallas_call | solution.py:70
  327.0 13.3 %shard_map.301 = (bf16[4,256,768]{2,1,0:T(8,128)(2,1)}, f32[576,768]{1,0:T(8,128)}, f32[2,192,192]{2,1,0:T(8,128)}, f32[576,1]{1,0:T(8,128)}) custom-call(s32[2]{0:T(128)} %pad_add_fusion.ids, bf16[576,1024]{1,0:T(8,128)(2,1)} %get-tuple-element.99.qkv_v.qkv, bf16[768,1024]{1,0:T(8,128)(2,1)} %get-tuple-element.100.feats.feats_q, ...), custom_call_target="tpu_custom_call" | custom-call | flops 2617245696 | bytes 7258128 | tf_op jit(solution)/shard_map/pallas_call | solution.py:70
  341.6 5.5 %collective-permute-done.63.refs_3_ = bf16[256,128]{1,0:T(8,128)(2,1)S(1)} collective-permute-done((bf16[256,128]{1,0:T(8,128)(2,1)S(1)}, bf16[256,128]{1,0:T(8,128)(2,1)S(1)}, u32[]{:S(2)}, u32[]{:S(2)}) %collective-permute-start.63) | collective-permute-done | bytes 65568 | tf_op jit(solution)/shard_map/ppermute | solution.py:667
  347.7 16.2 %shard_map.305 = (bf16[4,256,768]{2,1,0:T(8,128)(2,1)}, f32[2,192,192]{2,1,0:T(8,128)}, f32[576,1]{1,0:T(8,128)}, f32[2,768]{1,0:T(2,128)}, bf16[96,768]{1,0:T(8...) custom-call(s32[2]{0:T(128)} %pad_add_fusion.ids, ...), custom_call_target="tpu_custom_call" | custom-call | flops 2617245696 | bytes 9920784 | tf_op jit(solution)/shard_map/pallas_call | solution.py:70
  376.0 7.7 %collective-permute-start.72 = (bf16[239,128]{1,0:T(8,128)(2,1)S(1)}, bf16[239,128]{1,0:T(8,128)(2,1)S(1)}, u32[]{:S(2)}, u32[]{:S(2)}) collective-permute-start(bf16[239,128]{1,0:T(8,128)(2,1)S(1)} %fusion), channel_id=1, source_target_pairs={{0,8},{4,12},{8,16},{12,20},{16,24},{20,28},{24,0},{28,4},{1,9},{5... | collective-permute-start | bytes 183560 | tf_op jit(solution)/shard_map/ppermute | solution.py:446
  383.7 3.8 collective-permute-start.73
  389.4 3.9 collective-permute-start.75
  404.3 8.4 %collective-permute-done.65.arrived = bf16[256,768]{1,0:T(8,128)(2,1)S(1)} collective-permute-done((bf16[256,768]{1,0:T(8,128)(2,1)S(1)}, bf16[256,768]{1,0:T(8,128)(2,1)S(1)}, u32[]{:S(2)}, u32[]{:S(2)}) %collective-permute-start.65) | collective-permute-done | bytes 393248 | tf_op jit(solution)/shard_map/ppermute | solution.py:450
  439.6 5.8 %shard_map.307 = bf16[2,1024,768]{2,1,0:T(8,128)(2,1)} custom-call(s32[2]{0:T(128)} %pad_add_fusion.ids, bf16[256,768]{1,0:T(8,128)(2,1)} %shard_map.302.refs_0_, bf16[256,768]{1,0:T(8,128)(2,1)} %copy-done.23, bf16[256,768]{1,0:T(8,128)(2,1)} %copy-done.28, bf16[256,768]{1,0:T(8,128)(2,1)} %collective-permute-done.54.refs_3_, ...), custom_call_target="tpu_custom_call" | custom-call | bytes 3145728 | tf_op jit(solution)/shard_map/pallas_call | solution.py:70
  (449 shorter events, 185.1 us)
Async XLA Ops:
  26.5 68.6 %collective-permute-start.14 = (bf16[96,1728]{1,0:T(8,128)(2,1)S(1)}, bf16[96,1728]{1,0:T(8,128)(2,1)S(1)}, u32[]{:S(2)}, u32[]{:S(2)}) collective-permute-start(bf16[96,1728]{1,0:T(8,128)(2,1)S(1)} %pad_maximum_fusion.refs_0_), channel_id=1, source_target_pairs={{0,4},{4,8},{8,12},{12,16},{16,20},{20,24},{24,28},{28,0},{1,5},{5... | collective-permute-start | bytes 995336 | tf_op jit(solution)/shard_map/ppermute | solution.py:446
  29.3 65.9 %collective-permute-start.15 = (bf16[96,1728]{1,0:T(8,128)(2,1)S(1)}, bf16[96,1728]{1,0:T(8,128)(2,1)S(1)}, u32[]{:S(2)}, u32[]{:S(2)}) collective-permute-start(bf16[96,1728]{1,0:T(8,128)(2,1)S(1)} %pad_maximum_fusion.refs_0_), channel_id=1, source_target_pairs={{0,8},{4,12},{8,16},{12,20},{16,24},{20,28},{24,0},{28,4},{1,9},{5... | collective-permute-start | bytes 995336 | tf_op jit(solution)/shard_map/ppermute | solution.py:446
  36.4 68.9 %collective-permute-start.16 = (bf16[96,1728]{1,0:T(8,128)(2,1)S(1)}, bf16[96,1728]{1,0:T(8,128)(2,1)S(1)}, u32[]{:S(2)}, u32[]{:S(2)}) collective-permute-start(bf16[96,1728]{1,0:T(8,128)(2,1)S(1)} %pad_maximum_fusion.refs_0_), channel_id=1, source_target_pairs={{0,12},{4,16},{8,20},{12,24},{16,28},{20,0},{24,4},{28,8},{1,13},{... | collective-permute-start | bytes 995336 | tf_op jit(solution)/shard_map/ppermute | solution.py:446
  68.9 37.9 %collective-permute-start.17 = (bf16[96,1728]{1,0:T(8,128)(2,1)S(1)}, bf16[96,1728]{1,0:T(8,128)(2,1)S(1)}, u32[]{:S(2)}, u32[]{:S(2)}) collective-permute-start(bf16[96,1728]{1,0:T(8,128)(2,1)S(1)} %pad_maximum_fusion.refs_0_), channel_id=1, source_target_pairs={{0,16},{4,20},{8,24},{12,28},{16,0},{20,4},{24,8},{28,12},{1,17},{... | collective-permute-start | bytes 995336 | tf_op jit(solution)/shard_map/ppermute | solution.py:446
  71.7 35.2 %collective-permute-start.18 = (bf16[96,1728]{1,0:T(8,128)(2,1)S(1)}, bf16[96,1728]{1,0:T(8,128)(2,1)S(1)}, u32[]{:S(2)}, u32[]{:S(2)}) collective-permute-start(bf16[96,1728]{1,0:T(8,128)(2,1)S(1)} %pad_maximum_fusion.refs_0_), channel_id=1, source_target_pairs={{0,20},{4,24},{8,28},{12,0},{16,4},{20,8},{24,12},{28,16},{1,21},{... | collective-permute-start | bytes 995336 | tf_op jit(solution)/shard_map/ppermute | solution.py:446
  105.3 50.8 %collective-permute-start.11 = (bf16[192,1024]{1,0:T(8,128)(2,1)}, bf16[192,1024]{1,0:T(8,128)(2,1)S(1)}, u32[]{:S(2)}, u32[]{:S(2)}) collective-permute-start(bf16[192,1024]{1,0:T(8,128)(2,1)} %get-tuple-element.102.a0.attended_low), channel_id=1, source_target_pairs={{0,2},{1,3},{2,0},{3,1},{4,6},{5,7},{6,4},{7,5},{8,10},{9,11},{10,... | collective-permute-start | bytes 1179656 | tf_op jit(solution)/shard_map/ppermute | solution.py:450
  114.4 42.2 %collective-permute-start.21 = (bf16[768,192]{1,0:T(8,128)(2,1)}, bf16[768,192]{1,0:T(8,128)(2,1)S(1)}, u32[]{:S(2)}, u32[]{:S(2)}) collective-permute-start(bf16[768,192]{1,0:T(8,128)(2,1)} %get-tuple-element.104.p0.proj_t), channel_id=1, source_target_pairs={{0,2},{1,3},{2,0},{3,1},{4,6},{5,7},{6,4},{7,5},{8,10},{9,11},{10,... | collective-permute-start | bytes 884744 | tf_op jit(solution)/shard_map/ppermute | solution.py:450
  127.0 19.2 %collective-permute-start.30 = (bf16[256,128]{1,0:T(8,128)(2,1)}, bf16[256,128]{1,0:T(8,128)(2,1)S(1)}, u32[]{:S(2)}, u32[]{:S(2)}) collective-permute-start(bf16[256,128]{1,0:T(8,128)(2,1)} %get-tuple-element.111), channel_id=1, source_target_pairs={{0,8},{4,12},{8,16},{12,20},{16,24},{20,28},{1,9},{5,13},{9,17},{1... | collective-permute-start | bytes 196616 | tf_op jit(solution)/shard_map/ppermute | solution.py:566
  164.3 20.3 %collective-permute-start.34 = (bf16[192,1024]{1,0:T(8,128)(2,1)}, bf16[192,1024]{1,0:T(8,128)(2,1)S(1)}, u32[]{:S(2)}, u32[]{:S(2)}) collective-permute-start(bf16[192,1024]{1,0:T(8,128)(2,1)} %get-tuple-element.112.a0.attended_low), channel_id=1, source_target_pairs={{0,1},{1,0},{2,3},{3,2},{4,5},{5,4},{6,7},{7,6},{8,9},{9,8},{10,11... | collective-permute-start | bytes 1179656 | tf_op jit(solution)/shard_map/ppermute | solution.py:450
  164.3 20.3 %collective-permute-start.35 = (bf16[192,1024]{1,0:T(8,128)(2,1)S(1)}, bf16[192,1024]{1,0:T(8,128)(2,1)S(1)}, u32[]{:S(2)}, u32[]{:S(2)}) collective-permute-start(bf16[192,1024]{1,0:T(8,128)(2,1)S(1)} %collective-permute-done.33.a1), channel_id=1, source_target_pairs={{0,1},{1,0},{2,3},{3,2},{4,5},{5,4},{6,7},{7,6},{8,9},{9,8},{10,11... | collective-permute-start | bytes 1179656 | tf_op jit(solution)/shard_map/ppermute | solution.py:450
  216.4 38.0 %collective-permute-start.37 = (bf16[256,768]{1,0:T(8,128)(2,1)S(1)}, bf16[256,768]{1,0:T(8,128)(2,1)S(1)}, u32[]{:S(2)}, u32[]{:S(2)}) collective-permute-start(bf16[256,768]{1,0:T(8,128)(2,1)S(1)} %get-tuple-element.210), channel_id=1, source_target_pairs={{0,2},{1,3},{2,0},{3,1},{4,6},{5,7},{6,4},{7,5},{8,10},{9,11},{10,... | collective-permute-start | bytes 1179656 | tf_op jit(solution)/shard_map/ppermute | solution.py:450
  217.9 38.5 %collective-permute-start.25 = (bf16[256,768]{1,0:T(8,128)(2,1)S(1)}, bf16[256,768]{1,0:T(8,128)(2,1)S(1)}, u32[]{:S(2)}, u32[]{:S(2)}) collective-permute-start(bf16[256,768]{1,0:T(8,128)(2,1)S(1)} %get-tuple-element.212), channel_id=1, source_target_pairs={{0,2},{1,3},{2,0},{3,1},{4,6},{5,7},{6,4},{7,5},{8,10},{9,11},{10,... | collective-permute-start | bytes 1179656 | tf_op jit(solution)/shard_map/ppermute | solution.py:450
  221.2 22.2 %collective-permute-start.86 = (bf16[96,1536]{1,0:T(8,128)(2,1)}, bf16[96,1536]{1,0:T(8,128)(2,1)}, u32[]{:S(2)}, u32[]{:S(2)}) collective-permute-start(bf16[96,1536]{1,0:T(8,128)(2,1)} %get-tuple-element.160), channel_id=1, source_target_pairs={{0,8},{4,12},{8,16},{12,20},{16,24},{20,28},{24,0},{28,4},{1,9},{5... | collective-permute-start | bytes 884744 | tf_op jit(solution)/shard_map/ppermute | solution.py:446
  224.3 24.3 %collective-permute-start.87 = (bf16[96,1536]{1,0:T(8,128)(2,1)}, bf16[96,1536]{1,0:T(8,128)(2,1)}, u32[]{:S(2)}, u32[]{:S(2)}) collective-permute-start(bf16[96,1536]{1,0:T(8,128)(2,1)} %get-tuple-element.161), channel_id=1, source_target_pairs={{0,12},{4,16},{8,20},{12,24},{16,28},{20,0},{24,4},{28,8},{1,13},{... | collective-permute-start | bytes 884744 | tf_op jit(solution)/shard_map/ppermute | solution.py:446
  243.5 30.8 %collective-permute-start.57 = (bf16[256,768]{1,0:T(8,128)(2,1)S(1)}, bf16[256,768]{1,0:T(8,128)(2,1)S(1)}, u32[]{:S(2)}, u32[]{:S(2)}) collective-permute-start(bf16[256,768]{1,0:T(8,128)(2,1)S(1)} %copy-done.13), channel_id=1, source_target_pairs={{0,2},{1,3},{2,0},{3,1},{4,6},{5,7},{6,4},{7,5},{8,10},{9,11},{10,... | collective-permute-start | bytes 1179656 | tf_op jit(solution)/shard_map/ppermute | solution.py:450
  248.7 27.2 %collective-permute-start.43 = (bf16[256,768]{1,0:T(8,128)(2,1)}, bf16[256,768]{1,0:T(8,128)(2,1)S(1)}, u32[]{:S(2)}, u32[]{:S(2)}) collective-permute-start(bf16[256,768]{1,0:T(8,128)(2,1)} %get-tuple-element.119.g0), channel_id=1, source_target_pairs={{0,2},{1,3},{2,0},{3,1},{4,6},{5,7},{6,4},{7,5},{8,10},{9,11},{10,... | collective-permute-start | bytes 1179656 | tf_op jit(solution)/shard_map/ppermute | solution.py:450
  277.7 24.0 %collective-permute-start.39 = (bf16[256,768]{1,0:T(8,128)(2,1)S(1)}, bf16[256,768]{1,0:T(8,128)(2,1)S(1)}, u32[]{:S(2)}, u32[]{:S(2)}) collective-permute-start(bf16[256,768]{1,0:T(8,128)(2,1)S(1)} %copy-done.1), channel_id=1, source_target_pairs={{0,1},{1,0},{2,3},{3,2},{4,5},{5,4},{6,7},{7,6},{8,9},{9,8},{10,11... | collective-permute-start | bytes 1179656 | tf_op jit(solution)/shard_map/ppermute | solution.py:450
  278.3 24.7 %collective-permute-start.27 = (bf16[256,768]{1,0:T(8,128)(2,1)}, bf16[256,768]{1,0:T(8,128)(2,1)S(1)}, u32[]{:S(2)}, u32[]{:S(2)}) collective-permute-start(bf16[256,768]{1,0:T(8,128)(2,1)} %shard_map.293.refs_0_), channel_id=1, source_target_pairs={{0,1},{1,0},{2,3},{3,2},{4,5},{5,4},{6,7},{7,6},{8,9},{9,8},{10,11... | collective-permute-start | bytes 1179656 | tf_op jit(solution)/shard_map/ppermute | solution.py:450
  292.5 22.3 %collective-permute-start.28 = (bf16[256,768]{1,0:T(8,128)(2,1)}, bf16[256,768]{1,0:T(8,128)(2,1)}, u32[]{:S(2)}, u32[]{:S(2)}) collective-permute-start(bf16[256,768]{1,0:T(8,128)(2,1)} %collective-permute-done.26.refs_1_), channel_id=1, source_target_pairs={{0,1},{1,0},{2,3},{3,2},{4,5},{5,4},{6,7},{7,6},{8,9},{9,8},{10,11... | collective-permute-start | bytes 1179656 | tf_op jit(solution)/shard_map/ppermute | solution.py:450
  301.7 20.4 %collective-permute-start.46 = (bf16[256,128]{1,0:T(8,128)(2,1)}, bf16[256,128]{1,0:T(8,128)(2,1)S(1)}, u32[]{:S(2)}, u32[]{:S(2)}) collective-permute-start(bf16[256,128]{1,0:T(8,128)(2,1)} %get-tuple-element.125), channel_id=1, source_target_pairs={{4,0},{8,4},{12,8},{16,12},{20,16},{24,20},{28,24},{5,1},{9,5},{13... | collective-permute-start | bytes 196616 | tf_op jit(solution)/shard_map/ppermute | solution.py:667
  303.1 20.4 %collective-permute-start.47 = (bf16[256,128]{1,0:T(8,128)(2,1)}, bf16[256,128]{1,0:T(8,128)(2,1)S(1)}, u32[]{:S(2)}, u32[]{:S(2)}) collective-permute-start(bf16[256,128]{1,0:T(8,128)(2,1)} %get-tuple-element.125), channel_id=1, source_target_pairs={{8,0},{12,4},{16,8},{20,12},{24,16},{28,20},{9,1},{13,5},{17,9},{2... | collective-permute-start | bytes 196616 | tf_op jit(solution)/shard_map/ppermute | solution.py:667
  304.4 20.4 %collective-permute-start.48 = (bf16[256,128]{1,0:T(8,128)(2,1)}, bf16[256,128]{1,0:T(8,128)(2,1)S(1)}, u32[]{:S(2)}, u32[]{:S(2)}) collective-permute-start(bf16[256,128]{1,0:T(8,128)(2,1)} %get-tuple-element.125), channel_id=1, source_target_pairs={{12,0},{16,4},{20,8},{24,12},{28,16},{13,1},{17,5},{21,9},{25,13},... | collective-permute-start | bytes 196616 | tf_op jit(solution)/shard_map/ppermute | solution.py:667
  305.7 20.7 %collective-permute-start.49 = (bf16[256,128]{1,0:T(8,128)(2,1)}, bf16[256,128]{1,0:T(8,128)(2,1)S(1)}, u32[]{:S(2)}, u32[]{:S(2)}) collective-permute-start(bf16[256,128]{1,0:T(8,128)(2,1)} %get-tuple-element.125), channel_id=1, source_target_pairs={{16,0},{20,4},{24,8},{28,12},{17,1},{21,5},{25,9},{29,13},{18,2},{... | collective-permute-start | bytes 196616 | tf_op jit(solution)/shard_map/ppermute | solution.py:667
  314.9 25.4 %collective-permute-start.60 = (bf16[256,128]{1,0:T(8,128)(2,1)}, bf16[256,128]{1,0:T(8,128)(2,1)S(1)}, u32[]{:S(2)}, u32[]{:S(2)}) collective-permute-start(bf16[256,128]{1,0:T(8,128)(2,1)} %get-tuple-element.136), channel_id=1, source_target_pairs={{4,0},{8,4},{12,8},{16,12},{20,16},{24,20},{28,24},{5,1},{9,5},{13... | collective-permute-start | bytes 196616 | tf_op jit(solution)/shard_map/ppermute | solution.py:667
  324.8 22.2 %collective-permute-start.63 = (bf16[256,128]{1,0:T(8,128)(2,1)S(1)}, bf16[256,128]{1,0:T(8,128)(2,1)S(1)}, u32[]{:S(2)}, u32[]{:S(2)}) collective-permute-start(bf16[256,128]{1,0:T(8,128)(2,1)S(1)} %copy-done.96), channel_id=1, source_target_pairs={{16,0},{20,4},{24,8},{28,12},{17,1},{21,5},{25,9},{29,13},{18,2},{... | collective-permute-start | bytes 196616 | tf_op jit(solution)/shard_map/ppermute | solution.py:667
  366.9 20.6 %collective-permute-start.64 = (bf16[2,256,768]{2,1,0:T(8,128)(2,1)}, bf16[2,256,768]{2,1,0:T(8,128)(2,1)}, u32[]{:S(2)}, u32[]{:S(2)}) collective-permute-start(bf16[2,256,768]{2,1,0:T(8,128)(2,1)} %slice.187), channel_id=1, source_target_pairs={{0,1},{1,0},{2,3},{3,2},{4,5},{5,4},{6,7},{7,6},{8,9},{9,8},{10,11... | collective-permute-start | bytes 2359304 | tf_op jit(solution)/shard_map/ppermute | solution.py:450
  368.4 21.0 %collective-permute-start.50 = (bf16[2,256,768]{2,1,0:T(8,128)(2,1)}, bf16[2,256,768]{2,1,0:T(8,128)(2,1)}, u32[]{:S(2)}, u32[]{:S(2)}) collective-permute-start(bf16[2,256,768]{2,1,0:T(8,128)(2,1)} %slice.177), channel_id=1, source_target_pairs={{0,1},{1,0},{2,3},{3,2},{4,5},{5,4},{6,7},{7,6},{8,9},{9,8},{10,11... | collective-permute-start | bytes 2359304 | tf_op jit(solution)/shard_map/ppermute | solution.py:450
  375.2 20.2 %collective-permute-start.71 = (bf16[239,128]{1,0:T(8,128)(2,1)S(1)}, bf16[239,128]{1,0:T(8,128)(2,1)S(1)}, u32[]{:S(2)}, u32[]{:S(2)}) collective-permute-start(bf16[239,128]{1,0:T(8,128)(2,1)S(1)} %fusion), channel_id=1, source_target_pairs={{0,4},{4,8},{8,12},{12,16},{16,20},{20,24},{24,28},{28,0},{1,5},{5... | collective-permute-start | bytes 183560 | tf_op jit(solution)/shard_map/ppermute | solution.py:446
  376.0 19.4 %collective-permute-start.72 = (bf16[239,128]{1,0:T(8,128)(2,1)S(1)}, bf16[239,128]{1,0:T(8,128)(2,1)S(1)}, u32[]{:S(2)}, u32[]{:S(2)}) collective-permute-start(bf16[239,128]{1,0:T(8,128)(2,1)S(1)} %fusion), channel_id=1, source_target_pairs={{0,8},{4,12},{8,16},{12,20},{16,24},{20,28},{24,0},{28,4},{1,9},{5... | collective-permute-start | bytes 183560 | tf_op jit(solution)/shard_map/ppermute | solution.py:446
  398.6 25.5 %collective-permute-start.78 = (bf16[96,768]{1,0:T(8,128)(2,1)}, bf16[96,768]{1,0:T(8,128)(2,1)S(1)}, u32[]{:S(2)}, u32[]{:S(2)}) collective-permute-start(bf16[96,768]{1,0:T(8,128)(2,1)} %get-tuple-element.151), channel_id=1, source_target_pairs={{0,4},{4,8},{8,12},{12,16},{16,20},{20,24},{24,28},{28,0},{1,5},{5... | collective-permute-start | bytes 442376 | tf_op jit(solution)/shard_map/ppermute | solution.py:446
  398.6 27.4 %collective-permute-start.79 = (bf16[96,768]{1,0:T(8,128)(2,1)}, bf16[96,768]{1,0:T(8,128)(2,1)S(1)}, u32[]{:S(2)}, u32[]{:S(2)}) collective-permute-start(bf16[96,768]{1,0:T(8,128)(2,1)} %get-tuple-element.152), channel_id=1, source_target_pairs={{0,8},{4,12},{8,16},{12,20},{16,24},{20,28},{24,0},{28,4},{1,9},{5... | collective-permute-start | bytes 442376 | tf_op jit(solution)/shard_map/ppermute | solution.py:446
  400.3 27.7 %collective-permute-start.80 = (bf16[96,768]{1,0:T(8,128)(2,1)S(1)}, bf16[96,768]{1,0:T(8,128)(2,1)S(1)}, u32[]{:S(2)}, u32[]{:S(2)}) collective-permute-start(bf16[96,768]{1,0:T(8,128)(2,1)S(1)} %copy-done.92), channel_id=1, source_target_pairs={{0,12},{4,16},{8,20},{12,24},{16,28},{20,0},{24,4},{28,8},{1,13},{... | collective-permute-start | bytes 442376 | tf_op jit(solution)/shard_map/ppermute | solution.py:446
  (158 other events, 1717.0 us)

commit v2 on v1

v2 whole, which is shorter than its diff:
```python
import functools

import jax
import jax.numpy as jnp
from jax import lax
from jax.experimental import pallas as pl
from jax.experimental.pallas import tpu as pltpu
from jax.sharding import PartitionSpec as P

SEQ_LEN = 8192
MAX_SEGMENT = 4096
EPSILON = 1e-05
GELU_SCALE = 0.7978845608028654
GELU_CUBIC = 0.044715
PAD = 16
SMALL = 48

f32 = jnp.float32
bf16 = jnp.bfloat16


def dot_nn(a, b):
    return lax.dot_general(a, b, (((1,), (0,)), ((), ())), preferred_element_type=f32)


def dot_nt(a, b):
    return lax.dot_general(a, b, (((1,), (1,)), ((), ())), preferred_element_type=f32)


def dot_tn(a, b):
    return lax.dot_general(a, b, (((0,), (0,)), ((), ())), preferred_element_type=f32)


def split(value):
    high = value.astype(bf16)
    return high, (value - high.astype(f32)).astype(bf16)


def norm_parts(values):
    centred = values - jnp.mean(values, axis=-1, keepdims=True)
    inverse = lax.rsqrt(jnp.mean(centred * centred, axis=-1, keepdims=True) + EPSILON)
    return centred * inverse, inverse


def norm_back(grad, normed, inverse, gain):
    scaled = grad * gain
    return inverse * (
        scaled
        - jnp.mean(scaled, axis=-1, keepdims=True)
        - normed * jnp.mean(scaled * normed, axis=-1, keepdims=True)
    )


def softmax_rows(values):
    raised = jnp.exp(values - jnp.max(values, axis=0, keepdims=True))
    return raised * (1.0 / jnp.sum(raised, axis=0, keepdims=True))


def relative(value):
    return ((value & 1) << 1) | (value >> 1)


def with_ones(values):
    width = values.shape[1]
    rows = lax.broadcasted_iota(jnp.int32, (PAD, width), 0)
    return jnp.concatenate([values, (rows == 0).astype(f32).astype(bf16)], axis=0)


def call(kernel, grid, ids, inputs, outputs, scratch, flops, aliases=None):
    moved = sum(a.size * a.dtype.itemsize for a, _, _ in inputs)
    return pl.pallas_call(
        kernel,
        grid_spec=pltpu.PrefetchScalarGridSpec(
            num_scalar_prefetch=1,
            grid=grid,
            in_specs=[
                pl.BlockSpec(block, index) if block else pl.BlockSpec(memory_space=pl.ANY)
                for _, block, index in inputs
            ],
            out_specs=[pl.BlockSpec(block, index) for _, _, block, index in outputs],
            scratch_shapes=scratch,
        ),
        out_shape=[jax.ShapeDtypeStruct(shape, kind) for shape, kind, _, _ in outputs],
        cost_estimate=pl.CostEstimate(flops=flops, bytes_accessed=moved, transcendentals=0),
        input_output_aliases=aliases or {},
        compiler_params=pltpu.CompilerParams(dimension_semantics=("arbitrary",) * len(grid)),
    )(ids, *[a for a, _, _ in inputs])


def whole(array):
    return (array, array.shape, lambda i, ids: (0,) * array.ndim)


def whole_out(shape, kind):
    return (shape, kind, shape, lambda i, ids: (0,) * len(shape))


def norm_kernel(ids, x, gain, shift, attn_in):
    normed, _ = norm_parts(x[...].astype(f32))
    attn_in[...] = (normed * gain[...] + shift[...]).astype(bf16)


def project_kernel(heads, tiles, ids, attn_in, weight, bias, maps, seg, seg_last, qkv, feats, state, total, turned):
    step = pl.program_id(0)
    wide = bias.shape[0]

    @pl.when(step == 0)
    def _():
        turned[...] = weight[:, :wide].T

    low = (dot_nt(turned[...], attn_in[...]) + bias[...]).astype(bf16)
    qkv[...] = low
    width = wide // 3
    size = width // heads
    mapped = [dot_nn(maps[part], low[part * width : (part + 1) * width]) for part in range(2)]

    @pl.when(lax.rem(step, tiles) == 0)
    def _():
        total[...] = jnp.zeros_like(total)

    tail = (seg[...] == seg_last[:, -1:]).astype(f32).astype(bf16)
    for head in range(heads):
        for part in range(2):
            own = mapped[part][head * size : (head + 1) * size]
            both = jnp.concatenate([softmax_rows(own), softmax_rows(-own)], axis=0).astype(bf16)
            at = (part * heads + head) * 2 * size
            feats[at : at + 2 * size, :] = both
        value = with_ones(low[2 * width + head * size : 2 * width + (head + 1) * size])
        at = head * (size + PAD)
        total[at : at + size + PAD, :] += dot_nt(value * tail, both)

    @pl.when(lax.rem(step, tiles) == tiles - 1)
    def _():
        whole_state = jnp.concatenate(
            [total[...], jnp.broadcast_to(seg_last[:, -1:], (PAD, 2 * size))], axis=0
        ).astype(bf16)
        for copy in range(state.shape[0]):
            state[copy] = whole_state


def pair_mask(seg_col, seg_row):
    tile = seg_row.shape[1]
    early = lax.broadcasted_iota(jnp.int32, (tile, tile), 0)
    late = lax.broadcasted_iota(jnp.int32, (tile, tile), 1)
    return jnp.where(early <= late, (seg_col == seg_row).astype(f32), 0.0)


def attend_kernel(
    heads, pieces, hops, ids, qkv_v, feats, seg, seg_col, received, attended, attended_low, denominators, states, state, previous
):
    step = pl.program_id(0)
    size = qkv_v.shape[0] // heads
    rows = size + PAD
    used = heads * rows
    place = lax.rem(ids[1], pieces)

    @pl.when(step == 0)
    def _():
        start = jnp.zeros((used, 2 * size), f32)
        latest = received[jnp.maximum(ids[1] - 1, 0), used:, :].astype(f32)[:1]
        for hop in range(hops):
            source = jnp.maximum(ids[1] - 1 - hop, 0)
            linked = (received[source, used:, :].astype(f32)[:1] == latest).astype(f32)
            linked = linked * (place > hop).astype(f32)
            start = start + linked * received[source, :used, :].astype(f32)
        state[...] = start
        first = latest[:, :1]
        previous[...] = jnp.broadcast_to(jnp.where(place > 0, first, -2.0), previous.shape)

    row = seg[...]
    end = row[:, -1:]
    mask = pair_mask(seg_col[...], row)
    before = previous[...]
    carried = (row == before).astype(f32)
    tail = (row == end).astype(f32).astype(bf16)
    keep = (before[:, : 2 * size] == end).astype(f32)
    states[...] = state[...]
    for head in range(heads):
        query = feats[head * 2 * size : (head + 1) * 2 * size, :]
        key = feats[(heads + head) * 2 * size : (heads + head + 1) * 2 * size, :]
        value = with_ones(qkv_v[head * size : (head + 1) * size, :])
        scores = (dot_tn(key, query) * mask).astype(bf16)
        own = state[head * rows : (head + 1) * rows, :]
        inter = dot_nn(jnp.concatenate(split(own), axis=0), query)
        both = dot_nn(value, scores) + carried * (inter[:rows] + inter[rows:])
        lower = both[size : size + 1]
        result = both[:size] / lower
        attended[head * size : (head + 1) * size, :] = result
        attended_low[head * size : (head + 1) * size, :] = result.astype(bf16)
        denominators[head : head + 1, :] = lower
        state[head * rows : (head + 1) * rows, :] = keep * own + dot_nt(value * tail, key)
    previous[...] = jnp.broadcast_to(end, previous.shape)


def sum_of(*terms):
    total = terms[0][...].astype(f32)
    for term in terms[1:]:
        total = total + term[...].astype(f32)
    return total


def store_slots(step, ids, low, slots):
    apart = ids[0] ^ step
    if len(slots) == 4:
        slot = relative(apart)
        for at in range(4):

            @pl.when(slot == at)
            def _():
                slots[at][...] = low
    else:
        for at in range(2):

            @pl.when((apart & 1) == at)
            def _():
                slots[at][apart >> 1] = low


def turn_columns(*columns):
    lane = lax.broadcasted_iota(jnp.int32, (columns[0].shape[0], 128), 1)
    wide = jnp.zeros(lane.shape, f32)
    for at, column in enumerate(columns):
        wide = jnp.where(lane == at, column, wide)
    return wide.T[:8]


def mlp_kernel(first, ids, x, cot, a0, a1, a2, a3, p0, p1, p2, p3, proj_bias, gain, shift, fc, out_t, fc_bias, *refs):
    if not first:
        fc_in, out_in, bias_in = refs[:3]
        refs = refs[3:]
    slots = 4 if first else 2
    residual, grad_slots, out_slots, refs = refs[0], refs[1 : 1 + slots], refs[1 + slots : 3 + slots], refs[3 + slots :]
    if not first:
        vectors, products = refs[:2]
        refs = refs[2:]
    fc_acc, out_acc, bias_acc = refs
    step = pl.program_id(0)

    @pl.when(step == 0)
    def _():
        if first:
            fc_acc[...] = jnp.zeros_like(fc_acc)
            out_acc[...] = jnp.zeros_like(out_acc)
            bias_acc[...] = jnp.zeros_like(bias_acc)
        else:
            fc_acc[...] = fc_in[...]
            out_acc[...] = out_in[...]
            bias_acc[...] = bias_in[...]

    resid = x[...].astype(f32) + proj_bias[...]
    for part, proj in zip((a0, a1, a2, a3), (p0, p1, p2, p3)):
        resid = resid + dot_nt(part[...].T, proj[...])
    residual[...] = resid
    normed, _ = norm_parts(resid)
    mlp_in = (normed * gain[...] + shift[...]).astype(bf16)
    preact = dot_nn(mlp_in, fc[...]) + fc_bias[...]
    square = preact * preact
    tangent = jnp.tanh(GELU_SCALE * (preact + GELU_CUBIC * square * preact))
    half = 0.5 * (1.0 + tangent)
    activ = (preact * half).astype(bf16)
    slope = half + 0.5 * preact * (1.0 - tangent * tangent) * GELU_SCALE * (1.0 + 3.0 * GELU_CUBIC * square)
    top = cot[...]
    grad_pre = (dot_nn(top, out_t[...]) * slope).astype(bf16)
    grad_low = dot_nt(grad_pre, fc[...]).astype(bf16)
    out_low = dot_nt(activ, out_t[...]).astype(bf16)
    store_slots(step, ids, grad_low, grad_slots)
    store_slots(step, ids, out_low, out_slots)
    fc_acc[...] += dot_tn(mlp_in, grad_pre)
    out_acc[...] += dot_tn(top, activ)
    bias_acc[...] += jnp.sum(grad_pre.astype(f32), axis=0, keepdims=True)
    if not first:

        @pl.when(step == pl.num_programs(0) - 1)
        def _():
            width = fc_acc.shape[1]
            products[:, :width] = fc_acc[...].astype(bf16)
            products[:, width:] = out_acc[...].astype(bf16)
            wide = fc[...].astype(f32)
            sums = turn_columns(
                jnp.sum(wide * fc_acc[...], axis=1, keepdims=True),
                jnp.sum(wide * bias_acc[...], axis=1, keepdims=True),
            )
            vectors[0:1, :] = (sums[0:1] - shift[...] * sums[1:2]) / gain[...]
            vectors[1:2, :] = sums[1:2]
            vectors[2:3, :] = bias_acc[...]


def middle_kernel(ids, residual, cot, gain, *refs):
    grad_residual, grad_attn, sums = refs[-3:]
    normed, inverse = norm_parts(residual[...])
    grad = sum_of(*refs[:-3])
    top = cot[...].astype(f32)
    total = top + norm_back(grad, normed, inverse, gain[...])
    grad_residual[...] = total
    low = total.astype(bf16)
    grad_attn[...] = low
    sums[0:1, :] = jnp.sum(low.astype(f32), axis=0, keepdims=True)
    sums[1:2, :] = jnp.sum(top, axis=0, keepdims=True)


def last_kernel(ids, x, grad_residual, gain, *refs):
    normed, inverse = norm_parts(x[...].astype(f32))
    grad = sum_of(*refs[:-1])
    refs[-1][...] = (grad_residual[...] + norm_back(grad, normed, inverse, gain[...])).astype(bf16)


def finish_kernel(micro, ids, bias, crossed, *refs):
    out = refs[-1]
    for m in range(micro):
        out[m] = (sum_of(*refs[3 * m : 3 * m + 3]) + bias[...] + crossed[m].astype(f32)).astype(bf16)


def fold_kernel(count, ids, *refs):
    out = refs[-1]
    for at in range(count):
        out[at] = sum_of(*refs[2 * at : 2 * at + 2]).astype(bf16)


def order_kernel(tiles, ids, *refs):
    out = refs[-1]
    for at in range(tiles):

        @pl.when(lax.rem(pl.program_id(0), tiles) == at)
        def _():
            out[...] = refs[at][...]


def before_segment(pieces, tile_index, ids, received, seg_before):
    entering = jnp.where(lax.rem(ids[1], pieces) > 0, received[...].astype(f32)[:1, :1], -2.0)
    return jnp.where(tile_index == 0, entering, seg_before[:, -1:])


def grads_in_kernel(heads, pieces, first, ids, g0, g1, g2, g3, proj_t, feats_q, attended, attended_low, denominators, seg, received, *refs):
    if first:
        grads, state, proj_acc, total, proj = refs
    else:
        proj_in, grads, state, proj_acc, total, proj = refs
    step = pl.program_id(0)
    size = attended.shape[0] // heads
    rows = size + PAD
    used = heads * rows
    before = before_segment(pieces, 0, ids, received, seg)

    @pl.when(step == 0)
    def _():
        proj[...] = proj_t[...].T
        total[...] = jnp.zeros_like(total)
        proj_acc[...] = jnp.zeros_like(proj_acc) if first else proj_in[...]

    def work(source):
        grad = source[...]
        proj_acc[...] += dot_nn(attended_low[...], grad)
        grad_att = dot_nt(proj[...], grad)
        carried = (seg[...] == before).astype(f32)
        for head in range(heads):
            own = grad_att[head * size : (head + 1) * size]
            inverse = 1.0 / denominators[head : head + 1, :]
            lower = -inverse * jnp.sum(own * attended[head * size : (head + 1) * size, :], axis=0, keepdims=True)
            filler = lax.broadcasted_iota(jnp.int32, (PAD, own.shape[1]), 0)
            both = jnp.concatenate([own * inverse, jnp.where(filler == 0, lower, 0.0)], axis=0)
            grads[head * rows : (head + 1) * rows, :] = both
            query = feats_q[head * 2 * size : (head + 1) * 2 * size, :]
            sums = dot_nt(jnp.concatenate(split(both * carried), axis=0), query)
            total[head * rows : (head + 1) * rows, :] += sums[:rows] + sums[rows:]

    for at, source in enumerate((g0, g1, g2, g3)):

        @pl.when(step == at)
        def _():
            work(source)

    @pl.when(step == pl.num_programs(0) - 1)
    def _():
        whole_state = jnp.concatenate(
            [total[...], jnp.broadcast_to(before, (PAD, 2 * size))], axis=0
        ).astype(bf16)
        for copy in range(state.shape[0]):
            state[copy] = whole_state


def softmax_back(grad, positive, negative):
    size = positive.shape[0]
    upper, lower = grad[:size], grad[size:]
    return positive * (upper - jnp.sum(positive * upper, axis=0, keepdims=True)) - negative * (
        lower - jnp.sum(negative * lower, axis=0, keepdims=True)
    )


def grads_kernel(
    heads, pieces, hops, first, ids, qkv, feats, grads, states, seg, seg_col, seg_before, entering, attn_in, weight, maps, maps_back,
    received, *refs
):
    if not first:
        weight_in, map_in, bias_in, proj_in, gain, shift, mlp_rows, sums_a, sums_b = refs[:9]
        refs = refs[9:]
    slots, refs = (refs[:4], refs[4:]) if first else (refs[:2], refs[2:])
    if not first:
        packed, refs = refs[0], refs[1:]
    weight_acc, map_acc, bias_acc, state = refs
    step = pl.program_id(0)
    count = pl.num_programs(0)
    width = qkv.shape[0] // 3
    size = width // heads
    rows = size + PAD
    used = heads * rows
    row = seg[...]
    end = row[:, -1:]

    @pl.when(step == 0)
    def _():
        start = jnp.zeros((used, 2 * size), f32)
        place = lax.rem(ids[1], pieces)
        for hop in range(hops):
            source = jnp.minimum(ids[1] + 1 + hop, received.shape[0] - 1)
            linked = (received[source, used:, :].astype(f32)[:1] == end).astype(f32)
            linked = linked * (place + hop + 1 < pieces).astype(f32)
            start = start + linked * received[source, :used, :].astype(f32)
        state[...] = start
        if first:
            weight_acc[...] = jnp.zeros_like(weight_acc)
            map_acc[...] = jnp.zeros_like(map_acc)
            bias_acc[...] = jnp.zeros_like(bias_acc)
        else:
            weight_acc[...] = weight_in[...]
            map_acc[...] = map_in[...]
            bias_acc[...] = bias_in[...]

    before = before_segment(pieces, count - 1 - step, ids, entering, seg_before)
    mask = pair_mask(seg_col[...], row)
    carried = (row == before).astype(f32)
    tail = (row == end).astype(f32)
    keep = (before == end).astype(f32)
    mapped = [dot_nn(maps[part], qkv[part * width : (part + 1) * width, :]) for part in range(2)]
    back = [[], []]
    grad_values = []
    for head in range(heads):
        query = feats[head * 2 * size : (head + 1) * 2 * size, :]
        key = feats[(heads + head) * 2 * size : (heads + head + 1) * 2 * size, :]
        at = 2 * width + head * size
        value = with_ones(qkv[at : at + size, :])
        value_two = jnp.concatenate([value, value], axis=0)
        own = grads[head * rows : (head + 1) * rows, :]
        high, low = split(own)
        grad_two = jnp.concatenate([high, low], axis=0)
        scores = (dot_tn(key, query) * mask).astype(bf16)
        grad_scores = (dot_tn(value_two, grad_two) * mask).astype(bf16)
        into = states[head * rows : (head + 1) * rows, :]
        into_high, into_low = split(into)
        inter = dot_tn(
            jnp.concatenate([into_high, into_low, into_high], axis=0),
            jnp.concatenate([high, high, low], axis=0),
        )
        grad_query = dot_nn(key, grad_scores) + carried * inter
        after = state[head * rows : (head + 1) * rows, :]
        after_two = jnp.concatenate(split(after), axis=0)
        grad_key = dot_nt(query, grad_scores) + tail * dot_tn(after_two, value_two)
        straight = dot_nt(grad_two, scores)
        through = dot_nn(after_two, key)
        grad_values.append(
            straight[:size] + straight[rows : rows + size] + tail * (through[:size] + through[rows : rows + size])
        )
        carried_two = jnp.concatenate(split(own * carried), axis=0)
        added = dot_nt(carried_two, query)
        state[head * rows : (head + 1) * rows, :] = keep * after + added[:rows] + added[rows:]
        for part, grad in ((0, grad_query), (1, grad_key)):
            plain = mapped[part][head * size : (head + 1) * size]
            back[part].append(softmax_back(grad, softmax_rows(plain), softmax_rows(-plain)))
    pieces_low = []
    for part in range(2):
        grad_mapped = jnp.concatenate(back[part], axis=0).astype(bf16)
        map_acc[part] += dot_nt(qkv[part * width : (part + 1) * width, :], grad_mapped)
        pieces_low.append(dot_nn(maps_back[part], grad_mapped))
    pieces_low.append(jnp.concatenate(grad_values, axis=0))
    grad_qkv = jnp.concatenate(pieces_low, axis=0).astype(bf16)
    part_low = dot_nt(grad_qkv.T, weight[:, : 3 * width]).astype(bf16)
    store_slots(count - 1 - step, ids, part_low, slots)
    weight_acc[...] += dot_nn(grad_qkv, attn_in[...])
    bias_acc[...] += jnp.sum(grad_qkv.astype(f32), axis=1, keepdims=True)
    if not first:

        @pl.when(step == count - 1)
        def _():
            wide = weight[:, : 3 * width].astype(f32)
            total = weight_acc[...].T
            bias_row = turn_columns(bias_acc[...])[0:1]
            sums = turn_columns(
                jnp.sum(wide * total, axis=1, keepdims=True), jnp.sum(wide * bias_row, axis=1, keepdims=True)
            )
            dim = wide.shape[0]
            blocks = []
            for part in range(2):
                lane = lax.broadcasted_iota(jnp.int32, (size, width), 1) // size
                own = jnp.zeros((size, width), f32)
                for head in range(heads):
                    own = jnp.where(lane == head, map_acc[part, head * size : (head + 1) * size, :], own)
                blocks.append(own)
            half = size // 2
            turned = jnp.concatenate(
                [blocks[0][:half], blocks[1][:half], blocks[0][half:], blocks[1][half:]], axis=1
            )
            lines = [
                (sums[0:1] - shift[...] * sums[1:2]) / gain[...],
                sums[1:2],
                sums_a[...] + sums_b[...],
                mlp_rows[...],
                jnp.concatenate([bias_row, jnp.zeros((1, dim - 3 * width), f32)], axis=1),
                turned,
            ]
            small = jnp.concatenate(lines, axis=0)
            small = jnp.concatenate([small, jnp.zeros((SMALL - small.shape[0], dim), f32)], axis=0).astype(bf16)
            proj_total = proj_in[...].T
            shard = packed.shape[1] - SMALL
            for copy in range(packed.shape[0]):
                packed[copy, :SMALL, :] = small
                at = copy * shard
                packed[copy, SMALL:, : 3 * width] = total[at : at + shard].astype(bf16)
                packed[copy, SMALL:, 3 * width :] = proj_total[at : at + shard].astype(bf16)


def exchange(array):
    return lax.all_to_all(array, "dp", 0, 0)


def gather_dp(array):
    return exchange(jnp.broadcast_to(array, (lax.axis_size("dp"),) + array.shape)).reshape(-1, array.shape[1])


def swap(array, bit):
    return lax.ppermute(array, "tensor", [(i, i ^ bit) for i in range(4)])


def gather_tensor(array, direct=False):
    across = swap(array, 2)
    return (array, across, swap(array, 1), swap(array, 3) if direct else swap(across, 1))


def scatter_tensor(slots):
    return (slots[0], swap(slots[1], 2), swap(slots[2], 1), swap(slots[3], 3))


def block_diagonal(blocks):
    count, size, _ = blocks.shape
    eye = jnp.eye(count, dtype=blocks.dtype)
    return (eye[:, None, :, None] * blocks[:, :, None, :]).reshape(count * size, count * size)


def on_device(
    inputs, cotangent, segment, attn_gain, attn_shift, qkv_weight, qkv_bias, query_map, key_map,
    proj_weight, proj_bias, mlp_gain, mlp_shift, fc_weight, fc_bias, out_weight, out_bias,
):
    micro, tokens, dim = inputs.shape
    heads, size, _ = query_map.shape
    width = heads * size
    units = fc_weight.shape[1]
    count = lax.axis_size("dp")
    tiles = lax.axis_size("tensor")
    tile = tokens // tiles
    pieces = SEQ_LEN // tokens
    hops = min(-(-MAX_SEGMENT // tokens), pieces - 1)
    rows = size + PAD
    used = heads * rows
    shard = dim // count
    ids = jnp.stack([lax.axis_index("tensor"), lax.axis_index("dp")]).astype(jnp.int32)

    weight = gather_dp(jnp.concatenate([qkv_weight.reshape(shard, 3 * width), proj_weight.T], axis=1))
    proj_t = weight[:, 3 * width :]
    proj_slots = gather_tensor(proj_t)

    row = lambda v: v.astype(f32).reshape(1, -1)
    gain_a, shift_a, gain_m, shift_m = row(attn_gain), row(attn_shift), row(mlp_gain), row(mlp_shift)
    bias_p, bias_f, bias_o = row(proj_bias), row(fc_bias), row(out_bias)
    bias_qkv = qkv_bias.astype(f32).reshape(3 * width, 1)
    maps_back = jnp.stack([block_diagonal(query_map), block_diagonal(key_map)])
    maps = jnp.swapaxes(maps_back, 1, 2)
    seg = segment.astype(f32).reshape(micro, tiles, 1, tile)
    seg_col = segment.astype(f32).reshape(micro, tiles, tile, 1)

    def rows_of(array, m, at=None):
        return (array, (None, tile, dim), lambda i, ids: (m, i if at is None else at(i, ids), 0))

    def own_rows(array, m):
        return (array, (None, tile, dim), lambda i, ids: (m, ids[0], 0))

    def columns(array, at=None, m=0):
        return (
            array, (array.shape[0], tile), lambda i, ids: (0, m * tiles + (i if at is None else at(i, ids)))
        )

    def columns_out(height, kind, at=None):
        return ((height, tokens), kind, (height, tile), lambda i, ids: (0, i if at is None else at(i, ids)))

    def seg_row(m, at=None):
        return (seg, (None, None, 1, tile), lambda i, ids: (m, i if at is None else at(i, ids), 0, 0))

    def seg_column(m, at=None):
        return (seg_col, (None, None, tile, 1), lambda i, ids: (m, i if at is None else at(i, ids), 0, 0))

    def states_of(m):
        return (incoming, (count, used + PAD, 2 * size), lambda i, ids: (0, m, 0))

    def entering(m):
        return (
            incoming, (None, PAD, 2 * size),
            lambda i, ids: (jnp.maximum(ids[1] - 1, 0), (m * (used + PAD) + used) // PAD, 0),
        )

    def half(array, at):
        return (array, (None, tile, dim), lambda i, ids: (at, 0, 0))

    near = lambda i, ids: ids[0] ^ relative(i)

    def pin(*arrays):
        nonlocal ids
        ids, arrays = lax.optimization_barrier((ids, arrays))
        return arrays

    def run(*arguments, **options):
        return pin(*call(arguments[0], arguments[1], ids, *arguments[2:], **options))

    def fold(*pairs):
        (result,) = run(
            functools.partial(fold_kernel, len(pairs)), (1,),
            [half(a, 1) for pair in pairs for a in pair],
            [whole_out((len(pairs), tile, dim), bf16)], [], 0,
        )
        return result

    attn_ins = []
    for m in range(micro):
        (normed,) = run(
            norm_kernel, (tiles,), [rows_of(inputs, m), whole(gain_a), whole(shift_a)],
            [((1, tokens, dim), bf16, (None, tile, dim), lambda i, ids: (0, i, 0))], [], 0,
        )
        attn_ins.append(normed)
        if m == 0:
            fc_own, out_own = pin(fc_weight, out_weight)
            rest = lax.all_gather(jnp.concatenate([fc_own, out_own.T], axis=1), "dp", axis=0, tiled=True)
    fc_block = (rest, (dim, units), lambda i, ids: (0, 0))
    out_block = (rest, (dim, units), lambda i, ids: (0, 1))
    state_out = ((count, used + PAD, 2 * size), bf16)
    every = micro * tiles
    attn_in = jnp.concatenate(attn_ins, axis=0)
    qkv, feats, state = run(
        functools.partial(project_kernel, heads, tiles), (every,),
        [
            (attn_in, (None, tile, dim), lambda i, ids: (lax.div(i, tiles), lax.rem(i, tiles), 0)),
            whole(weight), whole(bias_qkv), whole(maps),
            (seg, (None, None, 1, tile), lambda i, ids: (lax.div(i, tiles), lax.rem(i, tiles), 0, 0)),
            (seg, (None, None, 1, tile), lambda i, ids: (lax.div(i, tiles), tiles - 1, 0, 0)),
        ],
        [
            ((3 * width, micro * tokens), bf16, (3 * width, tile), lambda i, ids: (0, i)),
            ((4 * width, micro * tokens), bf16, (4 * width, tile), lambda i, ids: (0, i)),
            (
                (count, micro * (used + PAD), 2 * size), bf16, (count, used + PAD, 2 * size),
                lambda i, ids: (0, lax.div(i, tiles), 0),
            ),
        ],
        [pltpu.VMEM((used, 2 * size), f32), pltpu.VMEM((3 * width, dim), bf16)],
        2 * micro * tokens * dim * 3 * width,
    )
    incoming = exchange(state)
    attended, attended_low, denominators, states, slots = [], [], [], [], []
    for m in range(micro):
        result = run(
            functools.partial(attend_kernel, heads, pieces, hops), (tiles,),
            [
                (qkv, (width, tile), lambda i, ids, m=m: (2, m * tiles + i)), columns(feats, None, m), seg_row(m), seg_column(m),
                states_of(m),
            ],
            [
                columns_out(width, f32), columns_out(width, bf16), columns_out(8, f32),
                ((tiles, used, 2 * size), f32, (None, used, 2 * size), lambda i, ids: (i, 0, 0)),
            ],
            [pltpu.VMEM((used, 2 * size), f32), pltpu.VMEM((1, tile), f32)],
            4 * tokens * tile * width,
        )
        attended.append(result[0])
        attended_low.append(result[1])
        denominators.append(result[2])
        states.append(result[3])
        slots.append(gather_tensor(result[1]))

    acc = ()
    residuals, mlp_terms, out_pairs = [], [], []
    for m in range(micro):
        final = m == micro - 1
        kept = [((dim, units), f32), ((dim, units), f32), ((1, units), f32)]
        pair = [whole_out((2, tile, dim), bf16)] * 2
        result = run(
            functools.partial(mlp_kernel, not final), (tiles,),
            [rows_of(inputs, m), rows_of(cotangent, m)]
            + [columns(a) for a in slots[m]]
            + [whole(a) for a in proj_slots]
            + [whole(bias_p), whole(gain_m), whole(shift_m), fc_block, out_block, whole(bias_f)]
            + [whole(a) for a in acc],
            [((tiles, tile, dim), f32, (None, tile, dim), lambda i, ids: (i, 0, 0))]
            + (pair if final else [whole_out((tile, dim), bf16)] * 4)
            + pair
            + ([whole_out((3, dim), f32), whole_out((dim, 2 * units), bf16)] if final else [whole_out(*k) for k in kept]),
            [pltpu.VMEM(*k) for k in kept] if final else [],
            2 * tokens * dim * (dim + 6 * units),
        )
        residuals.append(result[0])
        parts = result[1:3] if final else result[1:5]
        mlp_terms.append((parts[0], swap(parts[1], 1)) if final else scatter_tensor(parts))
        result = result[3:] if final else result[5:]
        out_pairs.append((result[0], swap(result[1], 1)))
        acc = result[2:]
    mlp_rows, rest_grads = acc

    own_tile = lambda array: (array, (None, tile, dim), lambda i, ids: (ids[0], 0, 0))
    grad_residuals, grad_slots, row_sums = [], [], []

    def middle(m, terms):
        grad_residual, grad_attn, sums = run(
            middle_kernel, (1,), [own_tile(residuals[m]), own_rows(cotangent, m), whole(gain_m)] + terms,
            [whole_out((tile, dim), f32), whole_out((tile, dim), bf16), whole_out((2, dim), f32)],
            [], 0,
        )
        grad_residuals.append(grad_residual)
        grad_slots.append(gather_tensor(grad_attn))
        row_sums.append(sums)

    proj_acc = ()
    grads, returned = [], []

    def grads_in(m):
        nonlocal proj_acc
        result = run(
            functools.partial(grads_in_kernel, heads, pieces, m == 0), (tiles,),
            [whole(a) for a in grad_slots[m]]
            + [
                whole(proj_t), (feats, (2 * width, tile), lambda i, ids: (0, m * tiles + near(i, ids))),
                columns(attended[m], near), columns(attended_low[m], near), columns(denominators[m], near),
                seg_row(m, near), entering(m),
            ]
            + [whole(a) for a in proj_acc],
            [columns_out(used, f32, near), whole_out(*state_out), whole_out((width, dim), f32)],
            [pltpu.VMEM((used, 2 * size), f32), pltpu.VMEM((width, dim), bf16)],
            4 * tokens * dim * width,
        )
        grads.append(result[0])
        proj_acc = (result[2],)
        returned.append(exchange(result[1]))

    acc = ()
    turned = lambda i, ids: tiles - 1 - i

    def attention_back(m):
        nonlocal acc
        final = m == micro - 1
        kept = [((3 * width, dim), f32), ((2, width, width), f32), ((3 * width, 1), f32)]
        result = run(
            functools.partial(grads_kernel, heads, pieces, hops, not final), (tiles,),
            [
                columns(qkv, turned, m), columns(feats, turned, m), columns(grads[m], turned),
                (states[m], (None, used, 2 * size), lambda i, ids: (tiles - 1 - i, 0, 0)),
                seg_row(m, turned), seg_column(m, turned), seg_row(m, lambda i, ids: jnp.maximum(tiles - 2 - i, 0)),
                entering(m), rows_of(attn_in, m, turned),
                whole(weight), whole(maps), whole(maps_back), whole(returned[m]),
            ]
            + [whole(a) for a in acc]
            + ([whole(a) for a in (proj_acc[0], gain_a, shift_a, mlp_rows, *row_sums)] if final else []),
            ([whole_out((2, tile, dim), bf16)] * 2 if final else [whole_out((tile, dim), bf16)] * 4)
            + ([whole_out((count, SMALL + shard, 4 * width), bf16)] if final else [whole_out(*k) for k in kept]),
            ([pltpu.VMEM(*k) for k in kept] if final else []) + [pltpu.VMEM((used, 2 * size), f32)],
            4 * tokens * dim * 3 * width + 16 * tokens * tile * width,
        )
        acc = result[2:] if final else result[4:]
        return result[:2] if final else result[:4]

    def last(m, terms):
        (finished,) = run(
            last_kernel, (1,), [own_rows(inputs, m), whole(grad_residuals[m]), whole(gain_a)] + terms,
            [whole_out((tile, dim), bf16)], [], 0,
        )
        return gather_tensor(finished)

    def ordered(parts, m, base=()):
        (result,) = run(
            functools.partial(order_kernel, tiles), (tiles,),
            [whole(a) for a in parts] + [(a, None, None) for a in base],
            [((micro, tokens, dim), bf16, (None, tile, dim), lambda i, ids: (m, ids[0] ^ relative(i), 0))],
            [], 0, aliases={tiles + 1: 0} if base else None,
        )
        return result

    def paired(pair, crossed):
        return [half(pair[0], 0), half(pair[1], 0), half(crossed, 0)]

    middle(0, [whole(a) for a in mlp_terms[0]])
    crossed = swap(fold(mlp_terms[1]), 2)
    (rest_grads,) = pin(rest_grads)
    rest_sum = lax.psum_scatter(rest_grads, "dp", scatter_dimension=0, tiled=True)
    grads_in(0)
    middle(1, paired(mlp_terms[1], crossed))
    out_crossed = swap(fold(*out_pairs), 2)
    grads_in(1)
    (finished,) = run(
        functools.partial(finish_kernel, micro), (1,),
        [whole(bias_o), whole(out_crossed)]
        + [spec for m in range(micro) for spec in (own_tile(residuals[m]), half(out_pairs[m][0], 0), half(out_pairs[m][1], 0))],
        [whole_out((micro, tile, dim), bf16)], [], 0,
    )
    outputs = gather_tensor(finished)
    first_terms = scatter_tensor(attention_back(0))
    kept, away = attention_back(1)
    last_pair = (kept, swap(away, 1))
    total = exchange(acc[0])
    crossed = swap(fold(last_pair), 2)
    early = last(0, [whole(a) for a in first_terms])
    (output,) = run(
        functools.partial(order_kernel, tiles), (every,),
        [(a, (None, tile, dim), lambda i, ids: (lax.div(i, tiles), 0, 0)) for a in outputs],
        [(
            (micro, tokens, dim), bf16, (None, tile, dim),
            lambda i, ids: (lax.div(i, tiles), ids[0] ^ relative(lax.rem(i, tiles)), 0),
        )],
        [], 0,
    )
    (rest_sum,) = pin(rest_sum)
    rest_sum = rest_sum.astype(f32)
    fc_grad, out_grad = pin(rest_sum[:, :units], rest_sum[:, units:].T)
    late = last(1, paired(last_pair, crossed))
    input_grad = ordered(early, 0)
    (input_grad,) = (ordered(late, 1, (input_grad,)),)
    total = jnp.sum(total.astype(f32), axis=0)

    shared = total[:6]
    shared = (shared + swap(shared, 1)) + (swap(shared, 2) + swap(shared, 3))
    blocks = total[8 : 8 + size // 2].reshape(size // 2, 2, 2, heads, size)
    blocks = jnp.transpose(blocks, (2, 3, 1, 0, 4)).reshape(2, heads, size, size)
    qkv_sum = total[SMALL:]
    return (
        output,
        input_grad,
        shared[0],
        shared[1],
        qkv_sum[:, : 3 * width].reshape(shard, 3, width),
        total[7, : 3 * width].reshape(3, width),
        blocks[0],
        blocks[1],
        qkv_sum[:, 3 * width :].T,
        shared[2],
        shared[4],
        shared[5],
        fc_grad,
        total[6],
        out_grad,
        shared[3],
    )


def solution(mesh):
    in_specs = (
        P(None, "dp", None), P(None, "dp", None), P(None, "dp"), P(), P(), P("dp", None, "tensor"),
        P(None, "tensor"), P("tensor", None, None), P("tensor", None, None), P("tensor", "dp"), P(), P(), P(),
        P("dp", "tensor"), P("tensor"), P("tensor", "dp"), P(),
    )
    out_specs = (
        P(None, "dp", None), P(None, "dp", None), P(), P(), P("dp", None, "tensor"), P(None, "tensor"),
        P("tensor", None, None), P("tensor", None, None), P("tensor", "dp"), P(), P(), P(),
        P("dp", "tensor"), P("tensor"), P("tensor", "dp"), P(),
    )
    return jax.shard_map(
        on_device, mesh=mesh, in_specs=in_specs, out_specs=out_specs, check_vma=False
    )
```

time: 454 us -> 406 us (0.89); the launches traced: 446 us -> 404 us
  starting transfers between devices: 163 us -> 49.8 us
  waiting for transfers between devices: 72.8 us -> 129 us
  Pallas kernels: 154 us -> 168 us
  between operations: 3.75 us -> 14.7 us
  other arithmetic: 12.8 us -> 3.73 us
    ppermute x51 -> x0, starting transfers between devices: 143 us -> none  [the longest x35 92.6 us: around(): lax.ppermute(array, axis, [(i, (i + shift) % size) for i in range(size)])]
    all_to_all x0 -> x5, waiting for transfers between devices: none -> 51 us  [exchange(): return lax.all_to_all(array, 'dp', 0, 0)]
    ppermute x41 -> x40, waiting for transfers between devices: 39.1 us -> 77.8 us  [swap(): return lax.ppermute(array, 'tensor', [(i, i ^ bit) for i in range(4)])]
    ppermute x51 -> x0, waiting for transfers between devices: 33.8 us -> none  [the longest x35 25 us: around(): lax.ppermute(array, axis, [(i, (i + shift) % size) for i in range(size)])]
    all_to_all x0 -> x5, starting transfers between devices: none -> 27 us  [exchange(): return lax.all_to_all(array, 'dp', 0, 0)]
    pallas_call x20 -> x22, Pallas kernels: 154 us -> 168 us  [call(): pl.pallas_call(kernel, grid_spec=pltpu.PrefetchScalarGridSpec(num_scalar_...]
    unnamed x201 -> x107, local copies, waits for them, and re-layouts: 10.5 us -> 21.3 us
    squeeze x9 -> x0, local copies, waits for them, and re-layouts: 6.94 us -> none  [the longest x6 4.89 us: scatter_tensor(): return (sums[0], swap(sums[1], 2))]
  transfers between devices with their start and end apart: 92 -> 47, of which waited for: 22 -> 14; matrix products, arithmetic and copies ran while one was open for 9% -> 6% of each run, Pallas kernels for 25% -> 41%
where the time goes in v2:
time: 406 us; the launch traced here: 404 us
  Pallas kernels  168 us (41%)
  waiting for transfers between devices  129 us (32%)
  starting transfers between devices  49.8 us (12%)
  local copies, waits for them, and re-layouts  38.7 us (10%)
  between operations  14.7 us (4%)
    pallas_call x22, Pallas kernels, call(): pl.pallas_call(kernel, grid_spec=pltpu.PrefetchScalarGridSpec(num_scalar_...  168 us
    ppermute x40, waiting for transfers between devices, swap(): return lax.ppermute(array, 'tensor', [(i, i ^ bit) for i in range(4)])  77.8 us
    all_to_all x5, waiting for transfers between devices, exchange(): return lax.all_to_all(array, 'dp', 0, 0)  51 us
    all_to_all x5, starting transfers between devices, exchange(): return lax.all_to_all(array, 'dp', 0, 0)  27 us
    ppermute x40, starting transfers between devices, swap(): return lax.ppermute(array, 'tensor', [(i, i ^ bit) for i in range(4)])  22.6 us
    unnamed x107, local copies, waits for them, and re-layouts  21.3 us
  transfers between devices with their start and end apart: 47, of which 14 were waited for; matrix products, arithmetic and copies ran while one was open for 6% of the time, Pallas kernels for 41%

profile of v2, /device:TPU:0, one launch (start us, length us, event | category | flops | bytes accessed | tf_op | source)
XLA Modules:
  0.0 404.1 jit_solution(6275915199748670948)
XLA Ops:
  10.4 7.4 %all-to-all-start = ((bf16[8,96,768]{2,1,0:T(8,128)(2,1)}), bf16[8,96,768]{2,1,0:T(8,128)(2,1)}, u32[]{:S(2)}, u32[]{:S(2)}) async-start(bf16[8,96,768]{2,1,0:T(8,128)(2,1)} %broadcast_in_dim.2), calls=%async_computation | async-start | bytes 2359296 | tf_op jit(solution)/shard_map/all_to_all | solution.py:521
  19.7 4.8 %shard_map.288 = bf16[1,1024,768]{2,1,0:T(8,128)(2,1)} custom-call(s32[2]{0:T(128)} %pad_add_fusion.ids, bf16[2,1024,768]{2,1,0:T(8,128)(2,1)} %x.11, f32[1,768]{1,0:T(1,128)} %reshape.172.gain.refs_4_, f32[1,768]{1,0:T(1,128)} %reshape.174.shift.refs_5_), custom_call_target="tpu_custom_call" | custom-call | bytes 3151872 | tf_op jit(solution)/shard_map/pallas_call | solution.py:71
  25.3 5.0 %shard_map.289 = bf16[1,1024,768]{2,1,0:T(8,128)(2,1)} custom-call(s32[2]{0:T(128)} %pad_add_fusion.ids, bf16[2,1024,768]{2,1,0:T(8,128)(2,1)} %x.11, f32[1,768]{1,0:T(1,128)} %reshape.172.gain.refs_4_, f32[1,768]{1,0:T(1,128)} %reshape.174.shift.refs_5_), custom_call_target="tpu_custom_call" | custom-call | bytes 3151872 | tf_op jit(solution)/shard_map/pallas_call | solution.py:71
  35.4 20.6 %all-to-all-done = bf16[8,96,768]{2,1,0:T(8,128)(2,1)} async-done(((bf16[8,96,768]{2,1,0:T(8,128)(2,1)}), bf16[8,96,768]{2,1,0:T(8,128)(2,1)}, u32[]{:S(2)}, u32[]{:S(2)}) %all-to-all-start) | async-done | bytes 1179680 | tf_op jit(solution)/shard_map/all_to_all | solution.py:521
  56.0 13.4 %shard_map.290 = (bf16[576,2048]{1,0:T(8,128)(2,1)}, bf16[768,2048]{1,0:T(8,128)(2,1)}, bf16[8,512,128]{2,1,0:T(8,128)(2,1)}) custom-call(s32[2]{0:T(128)} %pad_add_fusion.ids, bf16[2,1024,768]{2,1,0:T(8,128)(2,1)} %copy-done.1, bf16[768,768]{1,0:T(8,128)(2,1)} %bitcast.4.weight, f32[576,1]{1,0:T(8,128)} %reshape.187.bias, bf16[2,192,192]{2,1,0:T(8,128)(2,1)} %copy.84.maps, ...), custom_call_target="tpu_custom_call" | custom-call | flops 1811939328 | bytes 4491520 | tf_op jit(solution)/shard_map/pallas_call | solution.py:71
  75.1 30.5 %all-to-all-done.1.received.entering = bf16[8,512,128]{2,1,0:T(8,128)(2,1)S(1)} async-done(((bf16[8,512,128]{2,1,0:T(8,128)(2,1)}), bf16[8,512,128]{2,1,0:T(8,128)(2,1)S(1)}, u32[]{:S(2)}, u32[]{:S(2)}) %all-to-all-start.1) | async-done | bytes 1048608 | tf_op jit(solution)/shard_map/all_to_all | solution.py:521
  106.6 6.5 %shard_map.291 = (f32[192,1024]{1,0:T(8,128)}, bf16[192,1024]{1,0:T(8,128)(2,1)}, f32[8,1024]{1,0:T(8,128)}, f32[4,240,128]{2,1,0:T(8,128)}) custom-call(s32[2]{0:T(128)} %pad_add_fusion.ids, bf16[576,2048]{1,0:T(8,128)(2,1)} %get-tuple-element.167.qkv_v.qkv, bf16[768,2048]{1,0:T(8,128)(2,1)} %get-tuple-element.168.feats.feats_q, ...), custom_call_target="tpu_custom_call" | custom-call | flops 201326592 | bytes 6569984 | tf_op jit(solution)/shard_map/pallas_call | solution.py:71
  116.5 6.5 %shard_map.292 = (f32[192,1024]{1,0:T(8,128)}, bf16[192,1024]{1,0:T(8,128)(2,1)}, f32[8,1024]{1,0:T(8,128)}, f32[4,240,128]{2,1,0:T(8,128)}) custom-call(s32[2]{0:T(128)} %pad_add_fusion.ids, bf16[576,2048]{1,0:T(8,128)(2,1)} %get-tuple-element.167.qkv_v.qkv, bf16[768,2048]{1,0:T(8,128)(2,1)} %get-tuple-element.168.feats.feats_q, ...), custom_call_target="tpu_custom_call" | custom-call | flops 201326592 | bytes 6569984 | tf_op jit(solution)/shard_map/pallas_call | solution.py:71
  125.9 7.9 %collective-permute-done.3.p1 = bf16[768,192]{1,0:T(8,128)(2,1)S(1)} collective-permute-done((bf16[768,192]{1,0:T(8,128)(2,1)S(1)}, bf16[768,192]{1,0:T(8,128)(2,1)S(1)}, u32[]{:S(2)}, u32[]{:S(2)}) %collective-permute-start.3) | collective-permute-done | bytes 294944 | tf_op jit(solution)/shard_map/ppermute | solution.py:529
  136.7 3.9 collective-permute-done.6.a1
  141.5 20.4 %shard_map.293 = (f32[4,256,768]{2,1,0:T(8,128)}, bf16[256,768]{1,0:T(8,128)(2,1)}, bf16[256,768]{1,0:T(8,128)(2,1)}, bf16[256,768]{1,0:T(8,128)(2,1)}, bf16[256...) custom-call(s32[2]{0:T(128)} %pad_add_fusion.ids, ...), custom_call_target="tpu_custom_call" | custom-call | flops 8455716864 | bytes 13774848 | tf_op jit(solution)/shard_map/pallas_call | solution.py:71
  165.7 22.8 %shard_map.294 = (f32[4,256,768]{2,1,0:T(8,128)}, bf16[2,256,768]{2,1,0:T(8,128)(2,1)}, bf16[2,256,768]{2,1,0:T(8,128)(2,1)}, bf16[2,256,768]{2,1,0:T(8,128)(2,1...) custom-call(s32[2]{0:T(128)} %pad_add_fusion.ids, bf16[2,1024,768]{2,1,0:T(8,128)(2,1)} %x.11, ...), custom_call_target="tpu_custom_call" | custom-call | flops 8455716864 | bytes 18496512 | tf_op jit(solution)/shard_map/pallas_call | solution.py:71
  190.3 4.1 %shard_map.295 = (f32[256,768]{1,0:T(8,128)}, bf16[256,768]{1,0:T(8,128)(2,1)}, f32[2,768]{1,0:T(2,128)}) custom-call(s32[2]{0:T(128)} %pad_add_fusion.ids, f32[4,256,768]{2,1,0:T(8,128)} %get-tuple-element.206.residual.refs_0_, bf16[2,1024,768]{2,1,0:T(8,128)(2,1)} %cot.7, f32[1,768]{1,0:T(1,128)} %reshape.180.gain, ...), custom_call_target="tpu_custom_call" | custom-call | bytes 7867392 | tf_op jit(solution)/shard_map/pallas_call | solution.py:71
  196.1 10.0 %collective-permute-done.13.g1 = bf16[256,768]{1,0:T(8,128)(2,1)S(1)} collective-permute-done((bf16[256,768]{1,0:T(8,128)(2,1)}, bf16[256,768]{1,0:T(8,128)(2,1)S(1)}, u32[]{:S(2)}, u32[]{:S(2)}) %collective-permute-start.13) | collective-permute-done | bytes 393248 | tf_op jit(solution)/shard_map/ppermute | solution.py:529
  212.7 7.1 %shard_map.297 = (f32[240,1024]{1,0:T(8,128)}, bf16[8,256,128]{2,1,0:T(8,128)(2,1)}, f32[192,768]{1,0:T(8,128)}) custom-call(s32[2]{0:T(128)} %pad_add_fusion.ids, bf16[256,768]{1,0:T(8,128)(2,1)} %get-tuple-element.220.g0, bf16[256,768]{1,0:T(8,128)(2,1)} %copy-done.21, bf16[256,768]{1,0:T(8,128)(2,1)} %copy-done.23, bf16[256,768]{1,0:T(8,128)(2,1)} %copy-done.25, ...), custom_call_target="tpu_custom_call" | custom-call | flops 603979776 | bytes 7282688 | tf_op jit(solution)/shard_map/pallas_call | solution.py:71
  219.8 3.9 all-to-all-start.2
  225.0 4.0 shard_map.298
  229.4 10.9 %collective-permute-done.19.g1 = bf16[256,768]{1,0:T(8,128)(2,1)S(1)} collective-permute-done((bf16[256,768]{1,0:T(8,128)(2,1)}, bf16[256,768]{1,0:T(8,128)(2,1)S(1)}, u32[]{:S(2)}, u32[]{:S(2)}) %collective-permute-start.19) | collective-permute-done | bytes 393248 | tf_op jit(solution)/shard_map/ppermute | solution.py:529
  247.2 7.2 %shard_map.300 = (f32[240,1024]{1,0:T(8,128)}, bf16[8,256,128]{2,1,0:T(8,128)(2,1)}, f32[192,768]{1,0:T(8,128)}) custom-call(s32[2]{0:T(128)} %pad_add_fusion.ids, bf16[256,768]{1,0:T(8,128)(2,1)} %get-tuple-element.238.g0, bf16[256,768]{1,0:T(8,128)(2,1)} %copy-done.22, bf16[256,768]{1,0:T(8,128)(2,1)} %copy-done.24, bf16[256,768]{1,0:T(8,128)(2,1)} %copy-done.26, ...), custom_call_target="tpu_custom_call" | custom-call | flops 603979776 | bytes 7872512 | tf_op jit(solution)/shard_map/pallas_call | solution.py:71
  254.4 5.9 %all-to-all-start.3 = ((bf16[8,256,128]{2,1,0:T(8,128)(2,1)}), bf16[8,256,128]{2,1,0:T(8,128)(2,1)S(1)}, u32[]{:S(2)}, u32[]{:S(2)}) async-start(bf16[8,256,128]{2,1,0:T(8,128)(2,1)} %get-tuple-element.261), calls=%async_computation.3 | async-start | bytes 1048576 | tf_op jit(solution)/shard_map/all_to_all | solution.py:521
  260.9 4.5 %collective-permute-done.22.crossed = bf16[2,256,768]{2,1,0:T(8,128)(2,1)S(1)} collective-permute-done((bf16[2,256,768]{2,1,0:T(8,128)(2,1)}, bf16[2,256,768]{2,1,0:T(8,128)(2,1)S(1)}, u32[]{:S(2)}, u32[]{:S(2)}) %collective-permute-start.22) | collective-permute-done | bytes 786464 | tf_op jit(solution)/shard_map/ppermute | solution.py:529
  266.3 4.0 shard_map.301.refs_0_
  270.3 15.2 %shard_map.302 = (bf16[256,768]{1,0:T(8,128)(2,1)}, bf16[256,768]{1,0:T(8,128)(2,1)}, bf16[256,768]{1,0:T(8,128)(2,1)}, bf16[256,768]{1,0:T(8,128)(2,1)}, f32[57...) custom-call(s32[2]{0:T(128)} %pad_add_fusion.ids, bf16[576,2048]{1,0:T(8,128)(2,1)} %get-tuple-element.167.qkv_v.qkv, ...), custom_call_target="tpu_custom_call" | custom-call | flops 2617245696 | bytes 13197312 | tf_op jit(solution)/shard_map/pallas_call | solution.py:71
  286.3 18.0 %shard_map.303 = (bf16[2,256,768]{2,1,0:T(8,128)(2,1)}, bf16[2,256,768]{2,1,0:T(8,128)(2,1)}, bf16[8,144,768]{2,1,0:T(8,128)(2,1)}) custom-call(s32[2]{0:T(128)} %pad_add_fusion.ids, bf16[576,2048]{1,0:T(8,128)(2,1)} %get-tuple-element.167.qkv_v.qkv, bf16[768,2048]{1,0:T(8,128)(2,1)} %get-tuple-element.168.feats.feats_q, ...), custom_call_target="tpu_custom_call" | custom-call | flops 2617245696 | bytes 15881472 | tf_op jit(solution)/shard_map/pallas_call | solution.py:71
  304.3 6.1 %all-to-all-start.4 = ((bf16[8,144,768]{2,1,0:T(8,128)(2,1)}), bf16[8,144,768]{2,1,0:T(8,128)(2,1)S(1)}, u32[]{:S(2)}, u32[]{:S(2)}) async-start(bf16[8,144,768]{2,1,0:T(8,128)(2,1)} %get-tuple-element.297), calls=%async_computation.5 | async-start | bytes 3538944 | tf_op jit(solution)/shard_map/all_to_all | solution.py:521
  313.1 17.9 %collective-permute-done.27.refs_1_ = bf16[2,256,768]{2,1,0:T(8,128)(2,1)} collective-permute-done((bf16[2,256,768]{2,1,0:T(8,128)(2,1)S(1)}, bf16[2,256,768]{2,1,0:T(8,128)(2,1)}, u32[]{:S(2)}, u32[]{:S(2)}) %collective-permute-start.27) | collective-permute-done | bytes 786464 | tf_op jit(solution)/shard_map/ppermute | solution.py:529
  334.5 4.9 %collective-permute-done.24.refs_1_ = bf16[256,768]{1,0:T(8,128)(2,1)} collective-permute-done((bf16[256,768]{1,0:T(8,128)(2,1)}, bf16[256,768]{1,0:T(8,128)(2,1)}, u32[]{:S(2)}, u32[]{:S(2)}) %collective-permute-start.24) | collective-permute-done | bytes 393248 | tf_op jit(solution)/shard_map/ppermute | solution.py:529
  339.4 5.1 %collective-permute-done.26.refs_3_ = bf16[256,768]{1,0:T(8,128)(2,1)} collective-permute-done((bf16[256,768]{1,0:T(8,128)(2,1)}, bf16[256,768]{1,0:T(8,128)(2,1)}, u32[]{:S(2)}, u32[]{:S(2)}) %collective-permute-start.26) | collective-permute-done | bytes 393248 | tf_op jit(solution)/shard_map/ppermute | solution.py:529
  344.5 3.8 shard_map.305.refs_0_
  351.3 6.2 %shard_map.306 = bf16[2,1024,768]{2,1,0:T(8,128)(2,1)} custom-call(s32[2]{0:T(128)} %pad_add_fusion.ids, bf16[2,256,768]{2,1,0:T(8,128)(2,1)} %shard_map.301.refs_0_, bf16[2,256,768]{2,1,0:T(8,128)(2,1)} %collective-permute-done.27.refs_1_, bf16[2,256,768]{2,1,0:T(8,128)(2,1)} %collective-permute-done.28.refs_2_, ...), custom_call_target="tpu_custom_call" | custom-call | bytes 3145728 | tf_op jit(solution)/shard_map/pallas_call | solution.py:71
  364.5 3.9 collective-permute-done.30.refs_2_
  378.8 5.6 %collective-permute-done.34.refs_1_ = bf16[256,768]{1,0:T(8,128)(2,1)S(1)} collective-permute-done((bf16[256,768]{1,0:T(8,128)(2,1)}, bf16[256,768]{1,0:T(8,128)(2,1)S(1)}, u32[]{:S(2)}, u32[]{:S(2)}) %collective-permute-start.34) | collective-permute-done | bytes 393248 | tf_op jit(solution)/shard_map/ppermute | solution.py:529
  (235 shorter events, 91.7 us)
Async XLA Ops:
  10.4 45.6 %all-to-all-start = ((bf16[8,96,768]{2,1,0:T(8,128)(2,1)}), bf16[8,96,768]{2,1,0:T(8,128)(2,1)}, u32[]{:S(2)}, u32[]{:S(2)}) async-start(bf16[8,96,768]{2,1,0:T(8,128)(2,1)} %broadcast_in_dim.2), calls=%async_computation | async-start | bytes 2359296 | tf_op jit(solution)/shard_map/all_to_all | solution.py:521
  17.8 122.8 %all-gather.2.cloned.1.call-start = ((), (), s32[]{:S(2)}) async-start(), calls=%async_computation.6 | async-start | bytes 2654208 | tf_op jit(solution)/shard_map/all_gather | solution.py:637
  69.3 36.3 %all-to-all-start.1 = ((bf16[8,512,128]{2,1,0:T(8,128)(2,1)}), bf16[8,512,128]{2,1,0:T(8,128)(2,1)S(1)}, u32[]{:S(2)}, u32[]{:S(2)}) async-start(bf16[8,512,128]{2,1,0:T(8,128)(2,1)} %get-tuple-element.169), calls=%async_computation.1 | async-start | bytes 2097152 | tf_op jit(solution)/shard_map/all_to_all | solution.py:521
  73.0 288.2 %reduce-scatter.2.cloned.1.call-start = ((), (), s32[]{:S(2)}) async-start(), calls=%async_computation.7 | async-start | bytes 2654208 | tf_op jit(solution)/shard_map/reduce_scatter | solution.py:795
  116.0 17.9 %collective-permute-start.3 = (bf16[768,192]{1,0:T(8,128)(2,1)S(1)}, bf16[768,192]{1,0:T(8,128)(2,1)S(1)}, u32[]{:S(2)}, u32[]{:S(2)}) collective-permute-start(bf16[768,192]{1,0:T(8,128)(2,1)S(1)} %slice.73.p0.proj_t), channel_id=1, source_target_pairs={{0,2},{1,3},{2,0},{3,1},{4,6},{5,7},{6,4},{7,5},{8,10},{9,11},{10,... | collective-permute-start | bytes 884744 | tf_op jit(solution)/shard_map/ppermute | solution.py:529
  123.0 17.5 %collective-permute-start.6 = (bf16[192,1024]{1,0:T(8,128)(2,1)}, bf16[192,1024]{1,0:T(8,128)(2,1)S(1)}, u32[]{:S(2)}, u32[]{:S(2)}) collective-permute-start(bf16[192,1024]{1,0:T(8,128)(2,1)} %get-tuple-element.194.a0.attended_low), channel_id=1, source_target_pairs={{0,2},{1,3},{2,0},{3,1},{4,6},{5,7},{6,4},{7,5},{8,10},{9,11},{10,... | collective-permute-start | bytes 1179656 | tf_op jit(solution)/shard_map/ppermute | solution.py:529
  124.6 16.0 %collective-permute-start.1 = (bf16[192,1024]{1,0:T(8,128)(2,1)S(1)}, bf16[192,1024]{1,0:T(8,128)(2,1)S(1)}, u32[]{:S(2)}, u32[]{:S(2)}) collective-permute-start(bf16[192,1024]{1,0:T(8,128)(2,1)S(1)} %copy-done.13), channel_id=1, source_target_pairs={{0,1},{1,0},{2,3},{3,2},{4,5},{5,4},{6,7},{7,6},{8,9},{9,8},{10,11... | collective-permute-start | bytes 1179656 | tf_op jit(solution)/shard_map/ppermute | solution.py:529
  125.4 15.2 %collective-permute-start.2 = (bf16[192,1024]{1,0:T(8,128)(2,1)S(1)}, bf16[192,1024]{1,0:T(8,128)(2,1)}, u32[]{:S(2)}, u32[]{:S(2)}) collective-permute-start(bf16[192,1024]{1,0:T(8,128)(2,1)S(1)} %collective-permute-done.a1), channel_id=1, source_target_pairs={{0,1},{1,0},{2,3},{3,2},{4,5},{5,4},{6,7},{7,6},{8,9},{9,8},{10,11... | collective-permute-start | bytes 1179656 | tf_op jit(solution)/shard_map/ppermute | solution.py:529
  136.2 28.0 %collective-permute-start.7 = (bf16[192,1024]{1,0:T(8,128)(2,1)}, bf16[192,1024]{1,0:T(8,128)(2,1)S(1)}, u32[]{:S(2)}, u32[]{:S(2)}) collective-permute-start(bf16[192,1024]{1,0:T(8,128)(2,1)} %get-tuple-element.194.a0.attended_low), channel_id=1, source_target_pairs={{0,1},{1,0},{2,3},{3,2},{4,5},{5,4},{6,7},{7,6},{8,9},{9,8},{10,11... | collective-permute-start | bytes 1179656 | tf_op jit(solution)/shard_map/ppermute | solution.py:529
  140.5 23.6 %collective-permute-start.8 = (bf16[192,1024]{1,0:T(8,128)(2,1)S(1)}, bf16[192,1024]{1,0:T(8,128)(2,1)S(1)}, u32[]{:S(2)}, u32[]{:S(2)}) collective-permute-start(bf16[192,1024]{1,0:T(8,128)(2,1)S(1)} %collective-permute-done.6.a1), channel_id=1, source_target_pairs={{0,1},{1,0},{2,3},{3,2},{4,5},{5,4},{6,7},{7,6},{8,9},{9,8},{10,11... | collective-permute-start | bytes 1179656 | tf_op jit(solution)/shard_map/ppermute | solution.py:529
  161.9 26.8 %collective-permute-start.10 = (bf16[256,768]{1,0:T(8,128)(2,1)}, bf16[256,768]{1,0:T(8,128)(2,1)S(1)}, u32[]{:S(2)}, u32[]{:S(2)}) collective-permute-start(bf16[256,768]{1,0:T(8,128)(2,1)} %get-tuple-element.209), channel_id=1, source_target_pairs={{0,1},{1,0},{2,3},{3,2},{4,5},{5,4},{6,7},{7,6},{8,9},{9,8},{10,11... | collective-permute-start | bytes 1179656 | tf_op jit(solution)/shard_map/ppermute | solution.py:529
  162.4 26.2 %collective-permute-start.11 = (bf16[256,768]{1,0:T(8,128)(2,1)}, bf16[256,768]{1,0:T(8,128)(2,1)S(1)}, u32[]{:S(2)}, u32[]{:S(2)}) collective-permute-start(bf16[256,768]{1,0:T(8,128)(2,1)} %get-tuple-element.210), channel_id=1, source_target_pairs={{0,3},{1,2},{2,1},{3,0},{4,7},{5,6},{6,5},{7,4},{8,11},{9,10},{10,... | collective-permute-start | bytes 1179656 | tf_op jit(solution)/shard_map/ppermute | solution.py:529
  163.7 25.0 %collective-permute-start.9 = (bf16[256,768]{1,0:T(8,128)(2,1)}, bf16[256,768]{1,0:T(8,128)(2,1)S(1)}, u32[]{:S(2)}, u32[]{:S(2)}) collective-permute-start(bf16[256,768]{1,0:T(8,128)(2,1)} %get-tuple-element.208), channel_id=1, source_target_pairs={{0,2},{1,3},{2,0},{3,1},{4,6},{5,7},{6,4},{7,5},{8,10},{9,11},{10,... | collective-permute-start | bytes 1179656 | tf_op jit(solution)/shard_map/ppermute | solution.py:529
  188.5 17.6 %collective-permute-start.12 = (bf16[2,256,768]{2,1,0:T(8,128)(2,1)}, bf16[2,256,768]{2,1,0:T(8,128)(2,1)S(1)}, u32[]{:S(2)}, u32[]{:S(2)}) collective-permute-start(bf16[2,256,768]{2,1,0:T(8,128)(2,1)} %get-tuple-element.216), channel_id=1, source_target_pairs={{0,1},{1,0},{2,3},{3,2},{4,5},{5,4},{6,7},{7,6},{8,9},{9,8},{10,11... | collective-permute-start | bytes 2359304 | tf_op jit(solution)/shard_map/ppermute | solution.py:529
  196.0 15.2 %collective-permute-start.14 = (bf16[256,768]{1,0:T(8,128)(2,1)}, bf16[256,768]{1,0:T(8,128)(2,1)S(1)}, u32[]{:S(2)}, u32[]{:S(2)}) collective-permute-start(bf16[256,768]{1,0:T(8,128)(2,1)} %get-tuple-element.220.g0), channel_id=1, source_target_pairs={{0,1},{1,0},{2,3},{3,2},{4,5},{5,4},{6,7},{7,6},{8,9},{9,8},{10,11... | collective-permute-start | bytes 1179656 | tf_op jit(solution)/shard_map/ppermute | solution.py:529
  219.8 34.5 %all-to-all-start.2 = ((bf16[8,256,128]{2,1,0:T(8,128)(2,1)}), bf16[8,256,128]{2,1,0:T(8,128)(2,1)S(1)}, u32[]{:S(2)}, u32[]{:S(2)}) async-start(bf16[8,256,128]{2,1,0:T(8,128)(2,1)} %get-tuple-element.250), calls=%async_computation.2 | async-start | bytes 1048576 | tf_op jit(solution)/shard_map/all_to_all | solution.py:521
  223.7 16.5 %collective-permute-start.18 = (bf16[2,256,768]{2,1,0:T(8,128)(2,1)}, bf16[2,256,768]{2,1,0:T(8,128)(2,1)S(1)}, u32[]{:S(2)}, u32[]{:S(2)}) collective-permute-start(bf16[2,256,768]{2,1,0:T(8,128)(2,1)} %get-tuple-element.236), channel_id=1, source_target_pairs={{0,1},{1,0},{2,3},{3,2},{4,5},{5,4},{6,7},{7,6},{8,9},{9,8},{10,11... | collective-permute-start | bytes 2359304 | tf_op jit(solution)/shard_map/ppermute | solution.py:529
  223.7 16.6 %collective-permute-start.17 = (bf16[2,256,768]{2,1,0:T(8,128)(2,1)}, bf16[2,256,768]{2,1,0:T(8,128)(2,1)S(1)}, u32[]{:S(2)}, u32[]{:S(2)}) collective-permute-start(bf16[2,256,768]{2,1,0:T(8,128)(2,1)} %get-tuple-element.234), channel_id=1, source_target_pairs={{0,1},{1,0},{2,3},{3,2},{4,5},{5,4},{6,7},{7,6},{8,9},{9,8},{10,11... | collective-permute-start | bytes 2359304 | tf_op jit(solution)/shard_map/ppermute | solution.py:529
  229.4 16.3 %collective-permute-start.20 = (bf16[256,768]{1,0:T(8,128)(2,1)}, bf16[256,768]{1,0:T(8,128)(2,1)S(1)}, u32[]{:S(2)}, u32[]{:S(2)}) collective-permute-start(bf16[256,768]{1,0:T(8,128)(2,1)} %get-tuple-element.238.g0), channel_id=1, source_target_pairs={{0,1},{1,0},{2,3},{3,2},{4,5},{5,4},{6,7},{7,6},{8,9},{9,8},{10,11... | collective-permute-start | bytes 1179656 | tf_op jit(solution)/shard_map/ppermute | solution.py:529
  245.2 20.1 %collective-permute-start.22 = (bf16[2,256,768]{2,1,0:T(8,128)(2,1)}, bf16[2,256,768]{2,1,0:T(8,128)(2,1)S(1)}, u32[]{:S(2)}, u32[]{:S(2)}) collective-permute-start(bf16[2,256,768]{2,1,0:T(8,128)(2,1)} %shard_map.299), channel_id=1, source_target_pairs={{0,2},{1,3},{2,0},{3,1},{4,6},{5,7},{6,4},{7,5},{8,10},{9,11},{10,... | collective-permute-start | bytes 2359304 | tf_op jit(solution)/shard_map/ppermute | solution.py:529
  254.4 31.1 %all-to-all-start.3 = ((bf16[8,256,128]{2,1,0:T(8,128)(2,1)}), bf16[8,256,128]{2,1,0:T(8,128)(2,1)S(1)}, u32[]{:S(2)}, u32[]{:S(2)}) async-start(bf16[8,256,128]{2,1,0:T(8,128)(2,1)} %get-tuple-element.261), calls=%async_computation.3 | async-start | bytes 1048576 | tf_op jit(solution)/shard_map/all_to_all | solution.py:521
  304.3 80.1 %all-to-all-start.4 = ((bf16[8,144,768]{2,1,0:T(8,128)(2,1)}), bf16[8,144,768]{2,1,0:T(8,128)(2,1)S(1)}, u32[]{:S(2)}, u32[]{:S(2)}) async-start(bf16[8,144,768]{2,1,0:T(8,128)(2,1)} %get-tuple-element.297), calls=%async_computation.5 | async-start | bytes 3538944 | tf_op jit(solution)/shard_map/all_to_all | solution.py:521
  310.4 20.6 %collective-permute-start.27 = (bf16[2,256,768]{2,1,0:T(8,128)(2,1)S(1)}, bf16[2,256,768]{2,1,0:T(8,128)(2,1)}, u32[]{:S(2)}, u32[]{:S(2)}) collective-permute-start(bf16[2,256,768]{2,1,0:T(8,128)(2,1)S(1)} %copy-done.4), channel_id=1, source_target_pairs={{0,2},{1,3},{2,0},{3,1},{4,6},{5,7},{6,4},{7,5},{8,10},{9,11},{10,... | collective-permute-start | bytes 2359304 | tf_op jit(solution)/shard_map/ppermute | solution.py:529
  310.9 20.1 %collective-permute-start.23 = (bf16[2,256,768]{2,1,0:T(8,128)(2,1)}, bf16[2,256,768]{2,1,0:T(8,128)(2,1)S(1)}, u32[]{:S(2)}, u32[]{:S(2)}) collective-permute-start(bf16[2,256,768]{2,1,0:T(8,128)(2,1)} %get-tuple-element.274), channel_id=1, source_target_pairs={{0,1},{1,0},{2,3},{3,2},{4,5},{5,4},{6,7},{7,6},{8,9},{9,8},{10,11... | collective-permute-start | bytes 2359304 | tf_op jit(solution)/shard_map/ppermute | solution.py:529
  310.9 28.5 %collective-permute-start.24 = (bf16[256,768]{1,0:T(8,128)(2,1)}, bf16[256,768]{1,0:T(8,128)(2,1)}, u32[]{:S(2)}, u32[]{:S(2)}) collective-permute-start(bf16[256,768]{1,0:T(8,128)(2,1)} %get-tuple-element.278), channel_id=1, source_target_pairs={{0,2},{1,3},{2,0},{3,1},{4,6},{5,7},{6,4},{7,5},{8,10},{9,11},{10,... | collective-permute-start | bytes 1179656 | tf_op jit(solution)/shard_map/ppermute | solution.py:529
  312.5 26.9 %collective-permute-start.25 = (bf16[256,768]{1,0:T(8,128)(2,1)}, bf16[256,768]{1,0:T(8,128)(2,1)}, u32[]{:S(2)}, u32[]{:S(2)}) collective-permute-start(bf16[256,768]{1,0:T(8,128)(2,1)} %get-tuple-element.279), channel_id=1, source_target_pairs={{0,1},{1,0},{2,3},{3,2},{4,5},{5,4},{6,7},{7,6},{8,9},{9,8},{10,11... | collective-permute-start | bytes 1179656 | tf_op jit(solution)/shard_map/ppermute | solution.py:529
  312.7 31.8 %collective-permute-start.26 = (bf16[256,768]{1,0:T(8,128)(2,1)}, bf16[256,768]{1,0:T(8,128)(2,1)}, u32[]{:S(2)}, u32[]{:S(2)}) collective-permute-start(bf16[256,768]{1,0:T(8,128)(2,1)} %get-tuple-element.280), channel_id=1, source_target_pairs={{0,3},{1,2},{2,1},{3,0},{4,7},{5,6},{6,5},{7,4},{8,11},{9,10},{10,... | collective-permute-start | bytes 1179656 | tf_op jit(solution)/shard_map/ppermute | solution.py:529
  331.0 20.3 %collective-permute-start.28 = (bf16[2,256,768]{2,1,0:T(8,128)(2,1)S(1)}, bf16[2,256,768]{2,1,0:T(8,128)(2,1)}, u32[]{:S(2)}, u32[]{:S(2)}) collective-permute-start(bf16[2,256,768]{2,1,0:T(8,128)(2,1)S(1)} %copy-done.4), channel_id=1, source_target_pairs={{0,1},{1,0},{2,3},{3,2},{4,5},{5,4},{6,7},{7,6},{8,9},{9,8},{10,11... | collective-permute-start | bytes 2359304 | tf_op jit(solution)/shard_map/ppermute | solution.py:529
  331.0 20.3 %collective-permute-start.29 = (bf16[2,256,768]{2,1,0:T(8,128)(2,1)}, bf16[2,256,768]{2,1,0:T(8,128)(2,1)}, u32[]{:S(2)}, u32[]{:S(2)}) collective-permute-start(bf16[2,256,768]{2,1,0:T(8,128)(2,1)} %collective-permute-done.27.refs_1_), channel_id=1, source_target_pairs={{0,1},{1,0},{2,3},{3,2},{4,5},{5,4},{6,7},{7,6},{8,9},{9,8},{10,11... | collective-permute-start | bytes 2359304 | tf_op jit(solution)/shard_map/ppermute | solution.py:529
  349.5 18.9 %collective-permute-start.30 = (bf16[1,256,768]{2,1,0:T(8,128)(2,1)}, bf16[1,256,768]{2,1,0:T(8,128)(2,1)S(1)}, u32[]{:S(2)}, u32[]{:S(2)}) collective-permute-start(bf16[1,256,768]{2,1,0:T(8,128)(2,1)} %shard_map.304), channel_id=1, source_target_pairs={{0,2},{1,3},{2,0},{3,1},{4,6},{5,7},{6,4},{7,5},{8,10},{9,11},{10,... | collective-permute-start | bytes 1179656 | tf_op jit(solution)/shard_map/ppermute | solution.py:529
  350.3 24.0 %collective-permute-start.32 = (bf16[256,768]{1,0:T(8,128)(2,1)}, bf16[256,768]{1,0:T(8,128)(2,1)}, u32[]{:S(2)}, u32[]{:S(2)}) collective-permute-start(bf16[256,768]{1,0:T(8,128)(2,1)} %shard_map.305.refs_0_), channel_id=1, source_target_pairs={{0,1},{1,0},{2,3},{3,2},{4,5},{5,4},{6,7},{7,6},{8,9},{9,8},{10,11... | collective-permute-start | bytes 1179656 | tf_op jit(solution)/shard_map/ppermute | solution.py:529
  374.3 17.7 %collective-permute-start.35 = (bf16[256,768]{1,0:T(8,128)(2,1)}, bf16[256,768]{1,0:T(8,128)(2,1)S(1)}, u32[]{:S(2)}, u32[]{:S(2)}) collective-permute-start(bf16[256,768]{1,0:T(8,128)(2,1)} %shard_map.307.refs_0_), channel_id=1, source_target_pairs={{0,1},{1,0},{2,3},{3,2},{4,5},{5,4},{6,7},{7,6},{8,9},{9,8},{10,11... | collective-permute-start | bytes 1179656 | tf_op jit(solution)/shard_map/ppermute | solution.py:529
  (66 other events, 471.4 us)
Sparse Core Ops, SparseCore 0:
  25.4 65.7 all-gather.1
  211.3 79.5 reduce-scatter.1

commit v3 on v2

--- a/solution.py
+++ b/solution.py
@@ -14,6 +14,7 @@
 GELU_CUBIC = 0.044715
 PAD = 16
 SMALL = 48
+RATE = 1.1e9
 
 f32 = jnp.float32
 bf16 = jnp.bfloat16
@@ -66,7 +67,7 @@
     return jnp.concatenate([values, (rows == 0).astype(f32).astype(bf16)], axis=0)
 
 
-def call(kernel, grid, ids, inputs, outputs, scratch, flops, aliases=None):
+def call(kernel, grid, ids, inputs, outputs, scratch, micros, aliases=None):
     moved = sum(a.size * a.dtype.itemsize for a, _, _ in inputs)
     return pl.pallas_call(
         kernel,
@@ -81,7 +82,7 @@
             scratch_shapes=scratch,
         ),
         out_shape=[jax.ShapeDtypeStruct(shape, kind) for shape, kind, _, _ in outputs],
-        cost_estimate=pl.CostEstimate(flops=flops, bytes_accessed=moved, transcendentals=0),
+        cost_estimate=pl.CostEstimate(flops=int(micros * RATE), bytes_accessed=moved, transcendentals=0),
         input_output_aliases=aliases or {},
         compiler_params=pltpu.CompilerParams(dimension_semantics=("arbitrary",) * len(grid)),
     )(ids, *[a for a, _, _ in inputs])
@@ -131,11 +132,9 @@
 
     @pl.when(lax.rem(step, tiles) == tiles - 1)
     def _():
-        whole_state = jnp.concatenate(
+        state[...] = jnp.concatenate(
             [total[...], jnp.broadcast_to(seg_last[:, -1:], (PAD, 2 * size))], axis=0
         ).astype(bf16)
-        for copy in range(state.shape[0]):
-            state[copy] = whole_state
 
 
 def pair_mask(seg_col, seg_row):
@@ -146,8 +145,9 @@
 
 
 def attend_kernel(
-    heads, pieces, hops, ids, qkv_v, feats, seg, seg_col, received, attended, attended_low, denominators, states, state, previous
+    heads, pieces, hops, ids, qkv_v, feats, seg, seg_col, *refs
 ):
+    received, (attended, attended_low, denominators, states, state, previous) = refs[:hops], refs[hops:]
     step = pl.program_id(0)
     size = qkv_v.shape[0] // heads
     rows = size + PAD
@@ -157,12 +157,11 @@
     @pl.when(step == 0)
     def _():
         start = jnp.zeros((used, 2 * size), f32)
-        latest = received[jnp.maximum(ids[1] - 1, 0), used:, :].astype(f32)[:1]
+        latest = received[0][used:, :].astype(f32)[:1]
         for hop in range(hops):
-            source = jnp.maximum(ids[1] - 1 - hop, 0)
-            linked = (received[source, used:, :].astype(f32)[:1] == latest).astype(f32)
+            linked = (received[hop][used:, :].astype(f32)[:1] == latest).astype(f32)
             linked = linked * (place > hop).astype(f32)
-            start = start + linked * received[source, :used, :].astype(f32)
+            start = start + linked * received[hop][:used, :].astype(f32)
         state[...] = start
         first = latest[:, :1]
         previous[...] = jnp.broadcast_to(jnp.where(place > 0, first, -2.0), previous.shape)
@@ -529,9 +528,10 @@
     return lax.ppermute(array, "tensor", [(i, i ^ bit) for i in range(4)])
 
 
-def gather_tensor(array, direct=False):
-    across = swap(array, 2)
-    return (array, across, swap(array, 1), swap(array, 3) if direct else swap(across, 1))
+def gather_tensor(array, across=None):
+    if across is None:
+        return (array, swap(array, 2), swap(array, 1), swap(array, 3))
+    return (array, across, swap(array, 1), swap(across, 1))
 
 
 def scatter_tensor(slots):
@@ -564,7 +564,6 @@
 
     weight = gather_dp(jnp.concatenate([qkv_weight.reshape(shard, 3 * width), proj_weight.T], axis=1))
     proj_t = weight[:, 3 * width :]
-    proj_slots = gather_tensor(proj_t)
 
     row = lambda v: v.astype(f32).reshape(1, -1)
     gain_a, shift_a, gain_m, shift_m = row(attn_gain), row(attn_shift), row(mlp_gain), row(mlp_shift)
@@ -596,13 +595,10 @@
         return (seg_col, (None, None, tile, 1), lambda i, ids: (m, i if at is None else at(i, ids), 0, 0))
 
     def states_of(m):
-        return (incoming, (count, used + PAD, 2 * size), lambda i, ids: (0, m, 0))
+        return [(a, (used + PAD, 2 * size), lambda i, ids: (m, 0)) for a in incoming]
 
     def entering(m):
-        return (
-            incoming, (None, PAD, 2 * size),
-            lambda i, ids: (jnp.maximum(ids[1] - 1, 0), (m * (used + PAD) + used) // PAD, 0),
-        )
+        return (incoming[0], (PAD, 2 * size), lambda i, ids: ((m * (used + PAD) + used) // PAD, 0))
 
     def half(array, at):
         return (array, (None, tile, dim), lambda i, ids: (at, 0, 0))
@@ -621,30 +617,27 @@
         (result,) = run(
             functools.partial(fold_kernel, len(pairs)), (1,),
             [half(a, 1) for pair in pairs for a in pair],
-            [whole_out((len(pairs), tile, dim), bf16)], [], 0,
+            [whole_out((len(pairs), tile, dim), bf16)], [], 3,
         )
         return result
 
-    attn_ins = []
-    for m in range(micro):
-        (normed,) = run(
-            norm_kernel, (tiles,), [rows_of(inputs, m), whole(gain_a), whole(shift_a)],
-            [((1, tokens, dim), bf16, (None, tile, dim), lambda i, ids: (0, i, 0))], [], 0,
-        )
-        attn_ins.append(normed)
-        if m == 0:
-            fc_own, out_own = pin(fc_weight, out_weight)
-            rest = lax.all_gather(jnp.concatenate([fc_own, out_own.T], axis=1), "dp", axis=0, tiled=True)
+    rest_own = jnp.concatenate([fc_weight, out_weight.T], axis=1)
+    rest = lax.all_gather(rest_own, "dp", axis=0, tiled=True)
+    maps, maps_back, bias_qkv, seg, seg_col = pin(maps, maps_back, bias_qkv, seg, seg_col)
+    row_tile = lambda array: (array, (None, tile, dim), lambda i, ids: (lax.div(i, tiles), lax.rem(i, tiles), 0))
+    (attn_in,) = run(
+        norm_kernel, (micro * tiles,), [row_tile(inputs), whole(gain_a), whole(shift_a)],
+        [((micro, tokens, dim), bf16) + row_tile(inputs)[1:]], [], 8,
+    )
     fc_block = (rest, (dim, units), lambda i, ids: (0, 0))
     out_block = (rest, (dim, units), lambda i, ids: (0, 1))
     state_out = ((count, used + PAD, 2 * size), bf16)
+    proj_across = swap(proj_t, 2)
     every = micro * tiles
-    attn_in = jnp.concatenate(attn_ins, axis=0)
     qkv, feats, state = run(
         functools.partial(project_kernel, heads, tiles), (every,),
         [
-            (attn_in, (None, tile, dim), lambda i, ids: (lax.div(i, tiles), lax.rem(i, tiles), 0)),
-            whole(weight), whole(bias_qkv), whole(maps),
+            row_tile(attn_in), whole(weight), whole(bias_qkv), whole(maps),
             (seg, (None, None, 1, tile), lambda i, ids: (lax.div(i, tiles), lax.rem(i, tiles), 0, 0)),
             (seg, (None, None, 1, tile), lambda i, ids: (lax.div(i, tiles), tiles - 1, 0, 0)),
         ],
@@ -652,34 +645,43 @@
             ((3 * width, micro * tokens), bf16, (3 * width, tile), lambda i, ids: (0, i)),
             ((4 * width, micro * tokens), bf16, (4 * width, tile), lambda i, ids: (0, i)),
             (
-                (count, micro * (used + PAD), 2 * size), bf16, (count, used + PAD, 2 * size),
-                lambda i, ids: (0, lax.div(i, tiles), 0),
+                (micro * (used + PAD), 2 * size), bf16, (used + PAD, 2 * size),
+                lambda i, ids: (lax.div(i, tiles), 0),
             ),
         ],
         [pltpu.VMEM((used, 2 * size), f32), pltpu.VMEM((3 * width, dim), bf16)],
-        2 * micro * tokens * dim * 3 * width,
-    )
-    incoming = exchange(state)
-    attended, attended_low, denominators, states, slots = [], [], [], [], []
+        13,
+    )
+    incoming = [
+        lax.ppermute(state, "dp", [(i, i + k) for i in range(count) if i % pieces + k < pieces])
+        for k in range(1, hops + 1)
+    ]
+    (proj_across,) = pin(proj_across)
+    proj_slots = pin(*gather_tensor(proj_t, proj_across))
+    attended, attended_low, denominators, states = [], [], [], []
     for m in range(micro):
         result = run(
             functools.partial(attend_kernel, heads, pieces, hops), (tiles,),
             [
                 (qkv, (width, tile), lambda i, ids, m=m: (2, m * tiles + i)), columns(feats, None, m), seg_row(m), seg_column(m),
-                states_of(m),
-            ],
+            ]
+            + states_of(m),
             [
                 columns_out(width, f32), columns_out(width, bf16), columns_out(8, f32),
                 ((tiles, used, 2 * size), f32, (None, used, 2 * size), lambda i, ids: (i, 0, 0)),
             ],
             [pltpu.VMEM((used, 2 * size), f32), pltpu.VMEM((1, tile), f32)],
-            4 * tokens * tile * width,
+            6.5,
         )
         attended.append(result[0])
         attended_low.append(result[1])
         denominators.append(result[2])
         states.append(result[3])
-        slots.append(gather_tensor(result[1]))
+        if m == 0:
+            across = swap(result[1], 2)
+        else:
+            (across,) = pin(across)
+            slots = [gather_tensor(attended_low[0], across), gather_tensor(result[1])]
 
     acc = ()
     residuals, mlp_terms, out_pairs = [], [], []
@@ -699,7 +701,7 @@
             + pair
             + ([whole_out((3, dim), f32), whole_out((dim, 2 * units), bf16)] if final else [whole_out(*k) for k in kept]),
             [pltpu.VMEM(*k) for k in kept] if final else [],
-            2 * tokens * dim * (dim + 6 * units),
+            21,
         )
         residuals.append(result[0])
         parts = result[1:3] if final else result[1:5]
@@ -716,17 +718,19 @@
         grad_residual, grad_attn, sums = run(
             middle_kernel, (1,), [own_tile(residuals[m]), own_rows(cotangent, m), whole(gain_m)] + terms,
             [whole_out((tile, dim), f32), whole_out((tile, dim), bf16), whole_out((2, dim), f32)],
-            [], 0,
+            [], 4,
         )
         grad_residuals.append(grad_residual)
-        grad_slots.append(gather_tensor(grad_attn))
         row_sums.append(sums)
+        return grad_attn, swap(grad_attn, 2)
 
     proj_acc = ()
     grads, returned = [], []
 
-    def grads_in(m):
+    def grads_in(m, array, across):
         nonlocal proj_acc
+        (across,) = pin(across)
+        grad_slots.append(gather_tensor(array, across))
         result = run(
             functools.partial(grads_in_kernel, heads, pieces, m == 0), (tiles,),
             [whole(a) for a in grad_slots[m]]
@@ -738,7 +742,7 @@
             + [whole(a) for a in proj_acc],
             [columns_out(used, f32, near), whole_out(*state_out), whole_out((width, dim), f32)],
             [pltpu.VMEM((used, 2 * size), f32), pltpu.VMEM((width, dim), bf16)],
-            4 * tokens * dim * width,
+            7,
         )
         grads.append(result[0])
         proj_acc = (result[2],)
@@ -765,7 +769,7 @@
             ([whole_out((2, tile, dim), bf16)] * 2 if final else [whole_out((tile, dim), bf16)] * 4)
             + ([whole_out((count, SMALL + shard, 4 * width), bf16)] if final else [whole_out(*k) for k in kept]),
             ([pltpu.VMEM(*k) for k in kept] if final else []) + [pltpu.VMEM((used, 2 * size), f32)],
-            4 * tokens * dim * 3 * width + 16 * tokens * tile * width,
+            16,
         )
         acc = result[2:] if final else result[4:]
         return result[:2] if final else result[:4]
@@ -773,43 +777,50 @@
     def last(m, terms):
         (finished,) = run(
             last_kernel, (1,), [own_rows(inputs, m), whole(grad_residuals[m]), whole(gain_a)] + terms,
-            [whole_out((tile, dim), bf16)], [], 0,
-        )
-        return gather_tensor(finished)
+            [whole_out((tile, dim), bf16)], [], 4,
+        )
+        return finished
 
     def ordered(parts, m, base=()):
         (result,) = run(
             functools.partial(order_kernel, tiles), (tiles,),
             [whole(a) for a in parts] + [(a, None, None) for a in base],
             [((micro, tokens, dim), bf16, (None, tile, dim), lambda i, ids: (m, ids[0] ^ relative(i), 0))],
-            [], 0, aliases={tiles + 1: 0} if base else None,
+            [], 4, aliases={tiles + 1: 0} if base else None,
         )
         return result
 
     def paired(pair, crossed):
         return [half(pair[0], 0), half(pair[1], 0), half(crossed, 0)]
 
-    middle(0, [whole(a) for a in mlp_terms[0]])
-    crossed = swap(fold(mlp_terms[1]), 2)
     (rest_grads,) = pin(rest_grads)
     rest_sum = lax.psum_scatter(rest_grads, "dp", scatter_dimension=0, tiled=True)
-    grads_in(0)
-    middle(1, paired(mlp_terms[1], crossed))
+    moved = middle(0, [whole(a) for a in mlp_terms[0]])
+    crossed = swap(fold(mlp_terms[1]), 2)
+    grads_in(0, *moved)
+    moved = middle(1, paired(mlp_terms[1], crossed))
     out_crossed = swap(fold(*out_pairs), 2)
-    grads_in(1)
+    returned = list(pin(*returned))
+    grads_in(1, *moved)
     (finished,) = run(
         functools.partial(finish_kernel, micro), (1,),
         [whole(bias_o), whole(out_crossed)]
         + [spec for m in range(micro) for spec in (own_tile(residuals[m]), half(out_pairs[m][0], 0), half(out_pairs[m][1], 0))],
-        [whole_out((micro, tile, dim), bf16)], [], 0,
-    )
-    outputs = gather_tensor(finished)
-    first_terms = scatter_tensor(attention_back(0))
+        [whole_out((micro, tile, dim), bf16)], [], 4,
+    )
+    across = swap(finished, 2)
+    first_parts = attention_back(0)
+    (across,) = pin(across)
+    outputs = gather_tensor(finished, across)
+    first_terms = scatter_tensor(first_parts)
     kept, away = attention_back(1)
     last_pair = (kept, swap(away, 1))
     total = exchange(acc[0])
-    crossed = swap(fold(last_pair), 2)
+    (rest_sum,) = pin(rest_sum)
     early = last(0, [whole(a) for a in first_terms])
+    early, folded = pin(early, fold(last_pair))
+    crossed = swap(folded, 2)
+    early_across = swap(early, 2)
     (output,) = run(
         functools.partial(order_kernel, tiles), (every,),
         [(a, (None, tile, dim), lambda i, ids: (lax.div(i, tiles), 0, 0)) for a in outputs],
@@ -817,14 +828,16 @@
             (micro, tokens, dim), bf16, (None, tile, dim),
             lambda i, ids: (lax.div(i, tiles), ids[0] ^ relative(lax.rem(i, tiles)), 0),
         )],
-        [], 0,
-    )
-    (rest_sum,) = pin(rest_sum)
+        [], 6,
+    )
+    late = last(1, paired(last_pair, crossed))
+    late_across = swap(late, 2)
     rest_sum = rest_sum.astype(f32)
     fc_grad, out_grad = pin(rest_sum[:, :units], rest_sum[:, units:].T)
-    late = last(1, paired(last_pair, crossed))
-    input_grad = ordered(early, 0)
-    (input_grad,) = (ordered(late, 1, (input_grad,)),)
+    (early_across,) = pin(early_across)
+    input_grad = ordered(gather_tensor(early, early_across), 0)
+    total, late_across = pin(total, late_across)
+    input_grad = ordered(gather_tensor(late, late_across), 1, (input_grad,))
     total = jnp.sum(total.astype(f32), axis=0)
 
     shared = total[:6]

time: 406 us -> 356 us (0.88)
  waiting for transfers between devices: 129 us -> 73.3 us
  starting transfers between devices: 49.8 us -> 65.4 us
  local copies, waits for them, and re-layouts: 38.7 us -> 30.5 us
    ppermute x40, waiting for transfers between devices: 77.8 us -> 36.1 us  [swap(): return lax.ppermute(array, 'tensor', [(i, i ^ bit) for i in range(4)])]
    all_to_all x5 -> x4, waiting for transfers between devices: 51 us -> 30.7 us  [exchange(): return lax.all_to_all(array, 'dp', 0, 0)]
    ppermute x0 -> x4, starting transfers between devices: none -> 11.1 us  [on_device(): lax.ppermute(state, 'dp', [(i, i + k) for i in range(count) if i % pieces...]
    unnamed x107 -> x106, local copies, waits for them, and re-layouts: 21.3 us -> 14.8 us
    all_to_all x5 -> x4, starting transfers between devices: 27 us -> 32.2 us  [exchange(): return lax.all_to_all(array, 'dp', 0, 0)]
    ppermute x0 -> x4, waiting for transfers between devices: none -> 5.08 us  [on_device(): lax.ppermute(state, 'dp', [(i, i + k) for i in range(count) if i % pieces...]
    pallas_call x22 -> x21, Pallas kernels: 168 us -> 167 us  [call(): pl.pallas_call(kernel, grid_spec=pltpu.PrefetchScalarGridSpec(num_scalar_...]
  transfers between devices with their start and end apart: 47 -> 50, of which waited for: 14 -> 13; matrix products, arithmetic and copies ran while one was open for 6% -> 5% of each run, Pallas kernels for 41% -> 46%
where the time goes in v3:
time: 356 us; the launch traced here: 354 us
  Pallas kernels  167 us (47%)
  waiting for transfers between devices  73.3 us (21%)
  starting transfers between devices  65.4 us (18%)
  local copies, waits for them, and re-layouts  30.5 us (9%)
  between operations  14.7 us (4%)
  other arithmetic  3.69 us (1%)
    pallas_call x21, Pallas kernels, call(): pl.pallas_call(kernel, grid_spec=pltpu.PrefetchScalarGridSpec(num_scalar_...  167 us
    ppermute x40, waiting for transfers between devices, swap(): return lax.ppermute(array, 'tensor', [(i, i ^ bit) for i in range(4)])  36.1 us
    all_to_all x4, starting transfers between devices, exchange(): return lax.all_to_all(array, 'dp', 0, 0)  32.2 us
    all_to_all x4, waiting for transfers between devices, exchange(): return lax.all_to_all(array, 'dp', 0, 0)  30.7 us
    ppermute x40, starting transfers between devices, swap(): return lax.ppermute(array, 'tensor', [(i, i ^ bit) for i in range(4)])  22.1 us
    unnamed x106, local copies, waits for them, and re-layouts  14.8 us
    ppermute x4, starting transfers between devices, on_device(): lax.ppermute(state, 'dp', [(i, i + k) for i in range(count) if i % pieces...  11.1 us
  transfers between devices with their start and end apart: 50, of which 13 were waited for; matrix products, arithmetic and copies ran while one was open for 5% of the time, Pallas kernels for 46%

profile of v3, /device:TPU:0, one launch (start us, length us, event | category | flops | bytes accessed | tf_op | source)
XLA Modules:
  0.0 354.3 jit_solution(18152486572195336316)
XLA Ops:
  10.4 7.4 %all-to-all-start = ((bf16[8,96,768]{2,1,0:T(8,128)(2,1)}), bf16[8,96,768]{2,1,0:T(8,128)(2,1)S(1)}, u32[]{:S(2)}, u32[]{:S(2)}) async-start(bf16[8,96,768]{2,1,0:T(8,128)(2,1)} %broadcast_in_dim.2), calls=%async_computation | async-start | bytes 2359296 | tf_op jit(solution)/shard_map/all_to_all | solution.py:520
  21.9 7.8 %shard_map.288.attn_in = bf16[2,1024,768]{2,1,0:T(8,128)(2,1)} custom-call(s32[2]{0:T(128)} %pad_add_fusion.ids, bf16[2,1024,768]{2,1,0:T(8,128)(2,1)} %x.9, f32[1,768]{1,0:T(1,128)} %reshape.175.gain.refs_4_, f32[1,768]{1,0:T(1,128)} %reshape.177.shift.refs_5_), custom_call_target="tpu_custom_call" | custom-call | flops 8800000000 | bytes 3151872 | tf_op jit(solution)/shard_map/pallas_call | solution.py:72
  31.4 24.5 %all-to-all-done = bf16[8,96,768]{2,1,0:T(8,128)(2,1)S(1)} async-done(((bf16[8,96,768]{2,1,0:T(8,128)(2,1)}), bf16[8,96,768]{2,1,0:T(8,128)(2,1)S(1)}, u32[]{:S(2)}, u32[]{:S(2)}) %all-to-all-start) | async-done | bytes 1179680 | tf_op jit(solution)/shard_map/all_to_all | solution.py:520
  57.7 13.5 %shard_map.289 = (bf16[576,2048]{1,0:T(8,128)(2,1)}, bf16[768,2048]{1,0:T(8,128)(2,1)}, bf16[512,128]{1,0:T(8,128)(2,1)}) custom-call(s32[2]{0:T(128)} %pad_add_fusion.ids, bf16[2,1024,768]{2,1,0:T(8,128)(2,1)} %shard_map.288.attn_in, bf16[768,768]{1,0:T(8,128)(2,1)} %bitcast.16, f32[576,1]{1,0:T(8,128)} %copy.83.bias, bf16[2,192,192]{2,1,0:T(8,128)(2,1)} %copy.84.maps, ...), custom_call_target="tpu_custom_call" | custom-call | flops 14300000256 | bytes 4491520 | tf_op jit(solution)/shard_map/pallas_call | solution.py:72
  71.7 3.3 collective-permute-start.3
  76.4 4.3 %collective-permute-start.5 = (bf16[512,128]{1,0:T(8,128)(2,1)}, bf16[512,128]{1,0:T(8,128)(2,1)S(1)}, u32[]{:S(2)}, u32[]{:S(2)}) collective-permute-start(bf16[512,128]{1,0:T(8,128)(2,1)} %get-tuple-element.200), channel_id=1, source_target_pairs={{0,12},{4,16},{8,20},{12,24},{16,28},{1,13},{5,17},{9,21},{13,25},... | collective-permute-start | bytes 393224 | tf_op jit(solution)/shard_map/ppermute | solution.py:656
  90.0 6.5 %shard_map.290 = (f32[192,1024]{1,0:T(8,128)}, bf16[192,1024]{1,0:T(8,128)(2,1)}, f32[8,1024]{1,0:T(8,128)}, f32[4,240,128]{2,1,0:T(8,128)}) custom-call(s32[2]{0:T(128)} %pad_add_fusion.ids, bf16[576,2048]{1,0:T(8,128)(2,1)} %get-tuple-element.197.qkv_v.qkv, bf16[768,2048]{1,0:T(8,128)(2,1)} %get-tuple-element.198.feats.feats_q, ...), custom_call_target="tpu_custom_call" | custom-call | flops 7150000128 | bytes 6045696 | tf_op jit(solution)/shard_map/pallas_call | solution.py:72
  98.1 6.5 %shard_map.291 = (f32[192,1024]{1,0:T(8,128)}, bf16[192,1024]{1,0:T(8,128)(2,1)}, f32[8,1024]{1,0:T(8,128)}, f32[4,240,128]{2,1,0:T(8,128)}) custom-call(s32[2]{0:T(128)} %pad_add_fusion.ids, bf16[576,2048]{1,0:T(8,128)(2,1)} %get-tuple-element.197.qkv_v.qkv, bf16[768,2048]{1,0:T(8,128)(2,1)} %get-tuple-element.198.feats.feats_q, ...), custom_call_target="tpu_custom_call" | custom-call | flops 7150000128 | bytes 6045696 | tf_op jit(solution)/shard_map/pallas_call | solution.py:72
  104.6 3.1 collective-permute-done.7.a1
  113.1 20.4 %shard_map.292 = (f32[4,256,768]{2,1,0:T(8,128)}, bf16[256,768]{1,0:T(8,128)(2,1)}, bf16[256,768]{1,0:T(8,128)(2,1)}, bf16[256,768]{1,0:T(8,128)(2,1)}, bf16[256...) custom-call(s32[2]{0:T(128)} %pad_add_fusion.ids, ...), custom_call_target="tpu_custom_call" | custom-call | flops 23100000256 | bytes 13774848 | tf_op jit(solution)/shard_map/pallas_call | solution.py:72
  137.2 22.8 %shard_map.293 = (f32[4,256,768]{2,1,0:T(8,128)}, bf16[2,256,768]{2,1,0:T(8,128)(2,1)}, bf16[2,256,768]{2,1,0:T(8,128)(2,1)}, bf16[2,256,768]{2,1,0:T(8,128)(2,1...) custom-call(s32[2]{0:T(128)} %pad_add_fusion.ids, bf16[2,1024,768]{2,1,0:T(8,128)(2,1)} %x.9, ...), custom_call_target="tpu_custom_call" | custom-call | flops 23100000256 | bytes 18496512 | tf_op jit(solution)/shard_map/pallas_call | solution.py:72
  161.8 4.1 %shard_map.294 = (f32[256,768]{1,0:T(8,128)}, bf16[256,768]{1,0:T(8,128)(2,1)}, f32[2,768]{1,0:T(2,128)}) custom-call(s32[2]{0:T(128)} %pad_add_fusion.ids, f32[4,256,768]{2,1,0:T(8,128)} %get-tuple-element.243.residual.refs_0_, bf16[2,1024,768]{2,1,0:T(8,128)(2,1)} %cot.7, f32[1,768]{1,0:T(1,128)} %reshape.181.gain, ...), custom_call_target="tpu_custom_call" | custom-call | flops 4400000000 | bytes 7867392 | tf_op jit(solution)/shard_map/pallas_call | solution.py:72
  171.0 6.6 %collective-permute-done.17.g1 = bf16[256,768]{1,0:T(8,128)(2,1)S(1)} collective-permute-done((bf16[256,768]{1,0:T(8,128)(2,1)}, bf16[256,768]{1,0:T(8,128)(2,1)S(1)}, u32[]{:S(2)}, u32[]{:S(2)}) %collective-permute-start.17) | collective-permute-done | bytes 393248 | tf_op jit(solution)/shard_map/ppermute | solution.py:528
  180.4 7.2 %shard_map.296 = (f32[240,1024]{1,0:T(8,128)}, bf16[8,256,128]{2,1,0:T(8,128)(2,1)}, f32[192,768]{1,0:T(8,128)}) custom-call(s32[2]{0:T(128)} %pad_add_fusion.ids, bf16[256,768]{1,0:T(8,128)(2,1)} %get-tuple-element.255.g0, bf16[256,768]{1,0:T(8,128)(2,1)} %copy-done.42, bf16[256,768]{1,0:T(8,128)(2,1)} %copy-done.44, ...), custom_call_target="tpu_custom_call" | custom-call | flops 7699999744 | bytes 6365184 | tf_op jit(solution)/shard_map/pallas_call | solution.py:72
  187.5 12.8 %all-to-all-start.1 = ((bf16[8,256,128]{2,1,0:T(8,128)(2,1)}), bf16[8,256,128]{2,1,0:T(8,128)(2,1)S(1)}, u32[]{:S(2)}, u32[]{:S(2)}) async-start(bf16[8,256,128]{2,1,0:T(8,128)(2,1)} %get-tuple-element.275), calls=%async_computation.1 | async-start | bytes 1048576 | tf_op jit(solution)/shard_map/all_to_all | solution.py:520
  200.5 4.0 %shard_map.297 = (f32[256,768]{1,0:T(8,128)}, bf16[256,768]{1,0:T(8,128)(2,1)}, f32[2,768]{1,0:T(2,128)}) custom-call(s32[2]{0:T(128)} %pad_add_fusion.ids, f32[4,256,768]{2,1,0:T(8,128)} %get-tuple-element.264.residual.refs_3_, bf16[2,1024,768]{2,1,0:T(8,128)(2,1)} %cot.7, f32[1,768]{1,0:T(1,128)} %reshape.181.gain, ...), custom_call_target="tpu_custom_call" | custom-call | flops 4400000000 | bytes 8260608 | tf_op jit(solution)/shard_map/pallas_call | solution.py:72
  205.9 3.1 shard_map.298
  209.0 6.2 %all-to-all-done.1.received = bf16[8,256,128]{2,1,0:T(8,128)(2,1)S(1)} async-done(((bf16[8,256,128]{2,1,0:T(8,128)(2,1)}), bf16[8,256,128]{2,1,0:T(8,128)(2,1)S(1)}, u32[]{:S(2)}, u32[]{:S(2)}) %all-to-all-start.1) | async-done | bytes 524320 | tf_op jit(solution)/shard_map/all_to_all | solution.py:520
  218.1 7.1 %shard_map.299 = (f32[240,1024]{1,0:T(8,128)}, bf16[8,256,128]{2,1,0:T(8,128)(2,1)}, f32[192,768]{1,0:T(8,128)}) custom-call(s32[2]{0:T(128)} %pad_add_fusion.ids, bf16[256,768]{1,0:T(8,128)(2,1)} %get-tuple-element.277.g0, bf16[256,768]{1,0:T(8,128)(2,1)} %copy-done.41, bf16[256,768]{1,0:T(8,128)(2,1)} %collective-permute-done.24.g2, ...), custom_call_target="tpu_custom_call" | custom-call | flops 7699999744 | bytes 6955008 | tf_op jit(solution)/shard_map/pallas_call | solution.py:72
  225.2 10.5 %collective-permute-done.26.crossed = bf16[2,256,768]{2,1,0:T(8,128)(2,1)S(1)} collective-permute-done((bf16[2,256,768]{2,1,0:T(8,128)(2,1)}, bf16[2,256,768]{2,1,0:T(8,128)(2,1)S(1)}, u32[]{:S(2)}, u32[]{:S(2)}) %collective-permute-start.26) | collective-permute-done | bytes 786464 | tf_op jit(solution)/shard_map/ppermute | solution.py:528
  236.6 4.1 %shard_map.300.refs_0_ = bf16[2,256,768]{2,1,0:T(8,128)(2,1)} custom-call(s32[2]{0:T(128)} %pad_add_fusion.ids, f32[1,768]{1,0:T(1,128)} %reshape.187.bias, bf16[2,256,768]{2,1,0:T(8,128)(2,1)} %copy-done.24, f32[4,256,768]{2,1,0:T(8,128)} %get-tuple-element.243.residual.refs_0_, bf16[2,256,768]{2,1,0:T(8,128)(2,1)} %get-tuple-element.270.refs_0_.refs_1_, ...), custom_call_target="tpu_custom_call" | custom-call | flops 4400000000 | bytes 10226688 | tf_op jit(solution)/shard_map/pallas_call | solution.py:72
  241.2 5.8 %all-to-all-start.2 = ((bf16[8,256,128]{2,1,0:T(8,128)(2,1)}), bf16[8,256,128]{2,1,0:T(8,128)(2,1)S(1)}, u32[]{:S(2)}, u32[]{:S(2)}) async-start(bf16[8,256,128]{2,1,0:T(8,128)(2,1)} %get-tuple-element.305), calls=%async_computation.2 | async-start | bytes 1048576 | tf_op jit(solution)/shard_map/all_to_all | solution.py:520
  246.9 15.2 %shard_map.301 = (bf16[256,768]{1,0:T(8,128)(2,1)}, bf16[256,768]{1,0:T(8,128)(2,1)}, bf16[256,768]{1,0:T(8,128)(2,1)}, bf16[256,768]{1,0:T(8,128)(2,1)}, f32[57...) custom-call(s32[2]{0:T(128)} %pad_add_fusion.ids, bf16[576,2048]{1,0:T(8,128)(2,1)} %get-tuple-element.197.qkv_v.qkv, ...), custom_call_target="tpu_custom_call" | custom-call | flops 17600000000 | bytes 12279808 | tf_op jit(solution)/shard_map/pallas_call | solution.py:72
  265.3 18.0 %shard_map.302 = (bf16[2,256,768]{2,1,0:T(8,128)(2,1)}, bf16[2,256,768]{2,1,0:T(8,128)(2,1)}, bf16[8,144,768]{2,1,0:T(8,128)(2,1)}) custom-call(s32[2]{0:T(128)} %pad_add_fusion.ids, bf16[576,2048]{1,0:T(8,128)(2,1)} %get-tuple-element.197.qkv_v.qkv, bf16[768,2048]{1,0:T(8,128)(2,1)} %get-tuple-element.198.feats.feats_q, ...), custom_call_target="tpu_custom_call" | custom-call | flops 17600000000 | bytes 14963968 | tf_op jit(solution)/shard_map/pallas_call | solution.py:72
  283.4 6.1 %all-to-all-start.3 = ((bf16[8,144,768]{2,1,0:T(8,128)(2,1)}), bf16[8,144,768]{2,1,0:T(8,128)(2,1)S(1)}, u32[]{:S(2)}, u32[]{:S(2)}) async-start(bf16[8,144,768]{2,1,0:T(8,128)(2,1)} %get-tuple-element.343), calls=%async_computation.4 | async-start | bytes 3538944 | tf_op jit(solution)/shard_map/all_to_all | solution.py:520
  294.1 3.8 %shard_map.303.refs_0_ = bf16[256,768]{1,0:T(8,128)(2,1)} custom-call(s32[2]{0:T(128)} %pad_add_fusion.ids, bf16[2,1024,768]{2,1,0:T(8,128)(2,1)} %x.9, f32[256,768]{1,0:T(8,128)} %get-tuple-element.319.grad_residual, f32[1,768]{1,0:T(1,128)} %reshape.175.gain.refs_4_, bf16[256,768]{1,0:T(8,128)(2,1)} %get-tuple-element.320.refs_0_, ...), custom_call_target="tpu_custom_call" | custom-call | flops 4400000000 | bytes 5508096 | tf_op jit(solution)/shard_map/pallas_call | solution.py:72
  302.7 6.2 %shard_map.305 = bf16[2,1024,768]{2,1,0:T(8,128)(2,1)} custom-call(s32[2]{0:T(128)} %pad_add_fusion.ids, bf16[2,256,768]{2,1,0:T(8,128)(2,1)} %shard_map.300.refs_0_, bf16[2,256,768]{2,1,0:T(8,128)(2,1)} %copy-done.20, bf16[2,256,768]{2,1,0:T(8,128)(2,1)} %collective-permute-done.32.refs_2_, bf16[2,256,768]{2,1,0:T(8,128)(2,1)} %collective-permute-done.33.refs_3_), custom_call_target="tpu_custom_call" | custom-call | flops 6600000000 | bytes 3145728 | tf_op jit(solution)/shard_map/pallas_call | solution.py:72
  309.6 9.4 %collective-permute-done.34.refs_2_ = bf16[1,256,768]{2,1,0:T(8,128)(2,1)} collective-permute-done((bf16[1,256,768]{2,1,0:T(8,128)(2,1)}, bf16[1,256,768]{2,1,0:T(8,128)(2,1)}, u32[]{:S(2)}, u32[]{:S(2)}) %collective-permute-start.34) | collective-permute-done | bytes 393248 | tf_op jit(solution)/shard_map/ppermute | solution.py:528
  319.0 3.6 %shard_map.306.refs_0_ = bf16[256,768]{1,0:T(8,128)(2,1)} custom-call(s32[2]{0:T(128)} %pad_add_fusion.ids, bf16[2,1024,768]{2,1,0:T(8,128)(2,1)} %x.9, f32[256,768]{1,0:T(8,128)} %get-tuple-element.334.grad_residual, f32[1,768]{1,0:T(1,128)} %reshape.175.gain.refs_4_, bf16[2,256,768]{2,1,0:T(8,128)(2,1)} %get-tuple-element.325.refs_0_, ...), custom_call_target="tpu_custom_call" | custom-call | flops 4400000000 | bytes 5901312 | tf_op jit(solution)/shard_map/pallas_call | solution.py:72
  325.3 3.7 %shard_map.307.refs_4_ = bf16[2,1024,768]{2,1,0:T(8,128)(2,1)} custom-call(s32[2]{0:T(128)} %pad_add_fusion.ids, bf16[256,768]{1,0:T(8,128)(2,1)} %shard_map.303.refs_0_, bf16[256,768]{1,0:T(8,128)(2,1)} %collective-permute-done.35.refs_1_, bf16[256,768]{1,0:T(8,128)(2,1)} %collective-permute-done.36.refs_2_, bf16[256,768]{1,0:T(8,128)(2,1)} %copy-done.46), custom_call_target="tpu_custom_call" | custom-call | flops 4400000000 | bytes 1572864 | tf_op jit(solution)/shard_map/pallas_call | solution.py:72
  329.0 5.3 %collective-permute-done.38.refs_1_ = bf16[256,768]{1,0:T(8,128)(2,1)S(1)} collective-permute-done((bf16[256,768]{1,0:T(8,128)(2,1)}, bf16[256,768]{1,0:T(8,128)(2,1)S(1)}, u32[]{:S(2)}, u32[]{:S(2)}) %collective-permute-start.38) | collective-permute-done | bytes 393248 | tf_op jit(solution)/shard_map/ppermute | solution.py:528
  343.8 3.7 %shard_map.308 = bf16[2,1024,768]{2,1,0:T(8,128)(2,1)} custom-call(s32[2]{0:T(128)} %pad_add_fusion.ids, bf16[256,768]{1,0:T(8,128)(2,1)} %shard_map.306.refs_0_, bf16[256,768]{1,0:T(8,128)(2,1)} %copy-done.28, bf16[256,768]{1,0:T(8,128)(2,1)} %copy-done.29, bf16[256,768]{1,0:T(8,128)(2,1)} %copy-done.38, ...), custom_call_target="tpu_custom_call", output_to_operand_aliasing={{}: (5, {})} | custom-call | flops 4400000000 | bytes 4718592 | tf_op jit(solution)/shard_map/pallas_call | solution.py:72
  (240 shorter events, 72.9 us)
Async XLA Ops:
  10.4 45.5 %all-to-all-start = ((bf16[8,96,768]{2,1,0:T(8,128)(2,1)}), bf16[8,96,768]{2,1,0:T(8,128)(2,1)S(1)}, u32[]{:S(2)}, u32[]{:S(2)}) async-start(bf16[8,96,768]{2,1,0:T(8,128)(2,1)} %broadcast_in_dim.2), calls=%async_computation | async-start | bytes 2359296 | tf_op jit(solution)/shard_map/all_to_all | solution.py:520
  17.9 94.4 %all-gather.2.cloned.1.call-start = ((), (), s32[]{:S(2)}) async-start(), calls=%async_computation.5 | async-start | bytes 2654208 | tf_op jit(solution)/shard_map/all_gather | solution.py:625
  56.1 15.1 %collective-permute-start = (bf16[768,192]{1,0:T(8,128)(2,1)S(1)}, bf16[768,192]{1,0:T(8,128)(2,1)S(1)}, u32[]{:S(2)}, u32[]{:S(2)}) collective-permute-start(bf16[768,192]{1,0:T(8,128)(2,1)S(1)} %slice.73.p0.proj_t), channel_id=1, source_target_pairs={{0,2},{1,3},{2,0},{3,1},{4,6},{5,7},{6,4},{7,5},{8,10},{9,11},{10,... | collective-permute-start | bytes 884744 | tf_op jit(solution)/shard_map/ppermute | solution.py:528
  57.7 23.0 %collective-permute-start.1 = (bf16[768,192]{1,0:T(8,128)(2,1)S(1)}, bf16[768,192]{1,0:T(8,128)(2,1)S(1)}, u32[]{:S(2)}, u32[]{:S(2)}) collective-permute-start(bf16[768,192]{1,0:T(8,128)(2,1)S(1)} %slice.73.p0.proj_t), channel_id=1, source_target_pairs={{0,1},{1,0},{2,3},{3,2},{4,5},{5,4},{6,7},{7,6},{8,9},{9,8},{10,11... | collective-permute-start | bytes 884744 | tf_op jit(solution)/shard_map/ppermute | solution.py:528
  71.2 13.0 %collective-permute-start.2 = (bf16[768,192]{1,0:T(8,128)(2,1)S(1)}, bf16[768,192]{1,0:T(8,128)(2,1)S(1)}, u32[]{:S(2)}, u32[]{:S(2)}) collective-permute-start(bf16[768,192]{1,0:T(8,128)(2,1)S(1)} %collective-permute-done.p1), channel_id=1, source_target_pairs={{0,1},{1,0},{2,3},{3,2},{4,5},{5,4},{6,7},{7,6},{8,9},{9,8},{10,11... | collective-permute-start | bytes 884744 | tf_op jit(solution)/shard_map/ppermute | solution.py:528
  71.7 12.5 %collective-permute-start.3 = (bf16[512,128]{1,0:T(8,128)(2,1)}, bf16[512,128]{1,0:T(8,128)(2,1)S(1)}, u32[]{:S(2)}, u32[]{:S(2)}) collective-permute-start(bf16[512,128]{1,0:T(8,128)(2,1)} %get-tuple-element.200), channel_id=1, source_target_pairs={{0,4},{4,8},{8,12},{12,16},{16,20},{20,24},{24,28},{1,5},{5,9},{9,... | collective-permute-start | bytes 393224 | tf_op jit(solution)/shard_map/ppermute | solution.py:656
  98.1 14.1 %collective-permute-start.8 = (bf16[192,1024]{1,0:T(8,128)(2,1)}, bf16[192,1024]{1,0:T(8,128)(2,1)S(1)}, u32[]{:S(2)}, u32[]{:S(2)}) collective-permute-start(bf16[192,1024]{1,0:T(8,128)(2,1)} %get-tuple-element.211.a0.attended_low), channel_id=1, source_target_pairs={{0,1},{1,0},{2,3},{3,2},{4,5},{5,4},{6,7},{7,6},{8,9},{9,8},{10,11... | collective-permute-start | bytes 1179656 | tf_op jit(solution)/shard_map/ppermute | solution.py:528
  110.1 24.9 %collective-permute-start.10 = (bf16[192,1024]{1,0:T(8,128)(2,1)}, bf16[192,1024]{1,0:T(8,128)(2,1)S(1)}, u32[]{:S(2)}, u32[]{:S(2)}) collective-permute-start(bf16[192,1024]{1,0:T(8,128)(2,1)} %get-tuple-element.229.a0.attended_low), channel_id=1, source_target_pairs={{0,2},{1,3},{2,0},{3,1},{4,6},{5,7},{6,4},{7,5},{8,10},{9,11},{10,... | collective-permute-start | bytes 1179656 | tf_op jit(solution)/shard_map/ppermute | solution.py:528
  111.5 24.2 %collective-permute-start.11 = (bf16[192,1024]{1,0:T(8,128)(2,1)}, bf16[192,1024]{1,0:T(8,128)(2,1)S(1)}, u32[]{:S(2)}, u32[]{:S(2)}) collective-permute-start(bf16[192,1024]{1,0:T(8,128)(2,1)} %get-tuple-element.229.a0.attended_low), channel_id=1, source_target_pairs={{0,1},{1,0},{2,3},{3,2},{4,5},{5,4},{6,7},{7,6},{8,9},{9,8},{10,11... | collective-permute-start | bytes 1179656 | tf_op jit(solution)/shard_map/ppermute | solution.py:528
  111.7 24.0 %collective-permute-start.12 = (bf16[192,1024]{1,0:T(8,128)(2,1)}, bf16[192,1024]{1,0:T(8,128)(2,1)S(1)}, u32[]{:S(2)}, u32[]{:S(2)}) collective-permute-start(bf16[192,1024]{1,0:T(8,128)(2,1)} %get-tuple-element.229.a0.attended_low), channel_id=1, source_target_pairs={{0,3},{1,2},{2,1},{3,0},{4,7},{5,6},{6,5},{7,4},{8,11},{9,10},{10,... | collective-permute-start | bytes 1179656 | tf_op jit(solution)/shard_map/ppermute | solution.py:528
  133.5 26.6 %collective-permute-start.13 = (bf16[256,768]{1,0:T(8,128)(2,1)}, bf16[256,768]{1,0:T(8,128)(2,1)S(1)}, u32[]{:S(2)}, u32[]{:S(2)}) collective-permute-start(bf16[256,768]{1,0:T(8,128)(2,1)} %get-tuple-element.245), channel_id=1, source_target_pairs={{0,2},{1,3},{2,0},{3,1},{4,6},{5,7},{6,4},{7,5},{8,10},{9,11},{10,... | collective-permute-start | bytes 1179656 | tf_op jit(solution)/shard_map/ppermute | solution.py:528
  135.0 25.1 %collective-permute-start.14 = (bf16[256,768]{1,0:T(8,128)(2,1)}, bf16[256,768]{1,0:T(8,128)(2,1)S(1)}, u32[]{:S(2)}, u32[]{:S(2)}) collective-permute-start(bf16[256,768]{1,0:T(8,128)(2,1)} %get-tuple-element.246), channel_id=1, source_target_pairs={{0,1},{1,0},{2,3},{3,2},{4,5},{5,4},{6,7},{7,6},{8,9},{9,8},{10,11... | collective-permute-start | bytes 1179656 | tf_op jit(solution)/shard_map/ppermute | solution.py:528
  135.0 25.1 %collective-permute-start.15 = (bf16[256,768]{1,0:T(8,128)(2,1)}, bf16[256,768]{1,0:T(8,128)(2,1)S(1)}, u32[]{:S(2)}, u32[]{:S(2)}) collective-permute-start(bf16[256,768]{1,0:T(8,128)(2,1)} %get-tuple-element.247), channel_id=1, source_target_pairs={{0,3},{1,2},{2,1},{3,0},{4,7},{5,6},{6,5},{7,4},{8,11},{9,10},{10,... | collective-permute-start | bytes 1179656 | tf_op jit(solution)/shard_map/ppermute | solution.py:528
  177.6 27.4 %collective-permute-start.22 = (bf16[2,256,768]{2,1,0:T(8,128)(2,1)S(1)}, bf16[2,256,768]{2,1,0:T(8,128)(2,1)S(1)}, u32[]{:S(2)}, u32[]{:S(2)}) collective-permute-start(bf16[2,256,768]{2,1,0:T(8,128)(2,1)S(1)} %copy-done.21), channel_id=1, source_target_pairs={{0,1},{1,0},{2,3},{3,2},{4,5},{5,4},{6,7},{7,6},{8,9},{9,8},{10,11... | collective-permute-start | bytes 2359304 | tf_op jit(solution)/shard_map/ppermute | solution.py:528
  178.1 26.9 %collective-permute-start.21 = (bf16[2,256,768]{2,1,0:T(8,128)(2,1)S(1)}, bf16[2,256,768]{2,1,0:T(8,128)(2,1)}, u32[]{:S(2)}, u32[]{:S(2)}) collective-permute-start(bf16[2,256,768]{2,1,0:T(8,128)(2,1)S(1)} %copy-done.18), channel_id=1, source_target_pairs={{0,1},{1,0},{2,3},{3,2},{4,5},{5,4},{6,7},{7,6},{8,9},{9,8},{10,11... | collective-permute-start | bytes 2359304 | tf_op jit(solution)/shard_map/ppermute | solution.py:528
  178.2 22.3 %collective-permute-start.20 = (bf16[1,256,768]{2,1,0:T(8,128)(2,1)}, bf16[1,256,768]{2,1,0:T(8,128)(2,1)}, u32[]{:S(2)}, u32[]{:S(2)}) collective-permute-start(bf16[1,256,768]{2,1,0:T(8,128)(2,1)} %shard_map.295), channel_id=1, source_target_pairs={{0,2},{1,3},{2,0},{3,1},{4,6},{5,7},{6,4},{7,5},{8,10},{9,11},{10,... | collective-permute-start | bytes 1179656 | tf_op jit(solution)/shard_map/ppermute | solution.py:528
  187.5 27.6 %all-to-all-start.1 = ((bf16[8,256,128]{2,1,0:T(8,128)(2,1)}), bf16[8,256,128]{2,1,0:T(8,128)(2,1)S(1)}, u32[]{:S(2)}, u32[]{:S(2)}) async-start(bf16[8,256,128]{2,1,0:T(8,128)(2,1)} %get-tuple-element.275), calls=%async_computation.1 | async-start | bytes 1048576 | tf_op jit(solution)/shard_map/all_to_all | solution.py:520
  200.4 91.0 %reduce-scatter.2.cloned.1.call-start = ((), (), s32[]{:S(2)}) async-start(), calls=%async_computation.6 | async-start | bytes 2654208 | tf_op jit(solution)/shard_map/reduce_scatter | solution.py:797
  215.6 20.2 %collective-permute-start.26 = (bf16[2,256,768]{2,1,0:T(8,128)(2,1)}, bf16[2,256,768]{2,1,0:T(8,128)(2,1)S(1)}, u32[]{:S(2)}, u32[]{:S(2)}) collective-permute-start(bf16[2,256,768]{2,1,0:T(8,128)(2,1)} %shard_map.298), channel_id=1, source_target_pairs={{0,2},{1,3},{2,0},{3,1},{4,6},{5,7},{6,4},{7,5},{8,10},{9,11},{10,... | collective-permute-start | bytes 2359304 | tf_op jit(solution)/shard_map/ppermute | solution.py:528
  240.7 23.7 %collective-permute-start.27 = (bf16[2,256,768]{2,1,0:T(8,128)(2,1)}, bf16[2,256,768]{2,1,0:T(8,128)(2,1)S(1)}, u32[]{:S(2)}, u32[]{:S(2)}) collective-permute-start(bf16[2,256,768]{2,1,0:T(8,128)(2,1)} %shard_map.300.refs_0_), channel_id=1, source_target_pairs={{0,2},{1,3},{2,0},{3,1},{4,6},{5,7},{6,4},{7,5},{8,10},{9,11},{10,... | collective-permute-start | bytes 2359304 | tf_op jit(solution)/shard_map/ppermute | solution.py:528
  241.2 23.3 %all-to-all-start.2 = ((bf16[8,256,128]{2,1,0:T(8,128)(2,1)}), bf16[8,256,128]{2,1,0:T(8,128)(2,1)S(1)}, u32[]{:S(2)}, u32[]{:S(2)}) async-start(bf16[8,256,128]{2,1,0:T(8,128)(2,1)} %get-tuple-element.305), calls=%async_computation.2 | async-start | bytes 1048576 | tf_op jit(solution)/shard_map/all_to_all | solution.py:520
  262.2 27.4 %collective-permute-start.28 = (bf16[256,768]{1,0:T(8,128)(2,1)}, bf16[256,768]{1,0:T(8,128)(2,1)S(1)}, u32[]{:S(2)}, u32[]{:S(2)}) collective-permute-start(bf16[256,768]{1,0:T(8,128)(2,1)} %get-tuple-element.321), channel_id=1, source_target_pairs={{0,2},{1,3},{2,0},{3,1},{4,6},{5,7},{6,4},{7,5},{8,10},{9,11},{10,... | collective-permute-start | bytes 1179656 | tf_op jit(solution)/shard_map/ppermute | solution.py:528
  263.8 30.3 %collective-permute-start.29 = (bf16[256,768]{1,0:T(8,128)(2,1)}, bf16[256,768]{1,0:T(8,128)(2,1)}, u32[]{:S(2)}, u32[]{:S(2)}) collective-permute-start(bf16[256,768]{1,0:T(8,128)(2,1)} %get-tuple-element.322), channel_id=1, source_target_pairs={{0,1},{1,0},{2,3},{3,2},{4,5},{5,4},{6,7},{7,6},{8,9},{9,8},{10,11... | collective-permute-start | bytes 1179656 | tf_op jit(solution)/shard_map/ppermute | solution.py:528
  263.8 30.3 %collective-permute-start.30 = (bf16[256,768]{1,0:T(8,128)(2,1)}, bf16[256,768]{1,0:T(8,128)(2,1)}, u32[]{:S(2)}, u32[]{:S(2)}) collective-permute-start(bf16[256,768]{1,0:T(8,128)(2,1)} %get-tuple-element.323), channel_id=1, source_target_pairs={{0,3},{1,2},{2,1},{3,0},{4,7},{5,6},{6,5},{7,4},{8,11},{9,10},{10,... | collective-permute-start | bytes 1179656 | tf_op jit(solution)/shard_map/ppermute | solution.py:528
  283.3 14.6 %collective-permute-start.31 = (bf16[2,256,768]{2,1,0:T(8,128)(2,1)}, bf16[2,256,768]{2,1,0:T(8,128)(2,1)}, u32[]{:S(2)}, u32[]{:S(2)}) collective-permute-start(bf16[2,256,768]{2,1,0:T(8,128)(2,1)} %get-tuple-element.326), channel_id=1, source_target_pairs={{0,1},{1,0},{2,3},{3,2},{4,5},{5,4},{6,7},{7,6},{8,9},{9,8},{10,11... | collective-permute-start | bytes 2359304 | tf_op jit(solution)/shard_map/ppermute | solution.py:528
  283.4 51.0 %all-to-all-start.3 = ((bf16[8,144,768]{2,1,0:T(8,128)(2,1)}), bf16[8,144,768]{2,1,0:T(8,128)(2,1)S(1)}, u32[]{:S(2)}, u32[]{:S(2)}) async-start(bf16[8,144,768]{2,1,0:T(8,128)(2,1)} %get-tuple-element.343), calls=%async_computation.4 | async-start | bytes 3538944 | tf_op jit(solution)/shard_map/all_to_all | solution.py:520
  289.5 13.2 %collective-permute-start.32 = (bf16[2,256,768]{2,1,0:T(8,128)(2,1)S(1)}, bf16[2,256,768]{2,1,0:T(8,128)(2,1)}, u32[]{:S(2)}, u32[]{:S(2)}) collective-permute-start(bf16[2,256,768]{2,1,0:T(8,128)(2,1)S(1)} %copy-done.19), channel_id=1, source_target_pairs={{0,1},{1,0},{2,3},{3,2},{4,5},{5,4},{6,7},{7,6},{8,9},{9,8},{10,11... | collective-permute-start | bytes 2359304 | tf_op jit(solution)/shard_map/ppermute | solution.py:528
  289.6 13.1 %collective-permute-start.33 = (bf16[2,256,768]{2,1,0:T(8,128)(2,1)}, bf16[2,256,768]{2,1,0:T(8,128)(2,1)}, u32[]{:S(2)}, u32[]{:S(2)}) collective-permute-start(bf16[2,256,768]{2,1,0:T(8,128)(2,1)} %copy-done.20), channel_id=1, source_target_pairs={{0,1},{1,0},{2,3},{3,2},{4,5},{5,4},{6,7},{7,6},{8,9},{9,8},{10,11... | collective-permute-start | bytes 2359304 | tf_op jit(solution)/shard_map/ppermute | solution.py:528
  300.6 22.0 %collective-permute-start.35 = (bf16[256,768]{1,0:T(8,128)(2,1)S(1)}, bf16[256,768]{1,0:T(8,128)(2,1)}, u32[]{:S(2)}, u32[]{:S(2)}) collective-permute-start(bf16[256,768]{1,0:T(8,128)(2,1)S(1)} %copy-done.32), channel_id=1, source_target_pairs={{0,2},{1,3},{2,0},{3,1},{4,6},{5,7},{6,4},{7,5},{8,10},{9,11},{10,... | collective-permute-start | bytes 1179656 | tf_op jit(solution)/shard_map/ppermute | solution.py:528
  302.1 22.2 %collective-permute-start.36 = (bf16[256,768]{1,0:T(8,128)(2,1)S(1)}, bf16[256,768]{1,0:T(8,128)(2,1)}, u32[]{:S(2)}, u32[]{:S(2)}) collective-permute-start(bf16[256,768]{1,0:T(8,128)(2,1)S(1)} %copy-done.32), channel_id=1, source_target_pairs={{0,1},{1,0},{2,3},{3,2},{4,5},{5,4},{6,7},{7,6},{8,9},{9,8},{10,11... | collective-permute-start | bytes 1179656 | tf_op jit(solution)/shard_map/ppermute | solution.py:528
  302.1 16.9 %collective-permute-start.34 = (bf16[1,256,768]{2,1,0:T(8,128)(2,1)}, bf16[1,256,768]{2,1,0:T(8,128)(2,1)}, u32[]{:S(2)}, u32[]{:S(2)}) collective-permute-start(bf16[1,256,768]{2,1,0:T(8,128)(2,1)} %shard_map.304), channel_id=1, source_target_pairs={{0,2},{1,3},{2,0},{3,1},{4,6},{5,7},{6,4},{7,5},{8,10},{9,11},{10,... | collective-permute-start | bytes 1179656 | tf_op jit(solution)/shard_map/ppermute | solution.py:528
  324.2 18.1 %collective-permute-start.39 = (bf16[256,768]{1,0:T(8,128)(2,1)}, bf16[256,768]{1,0:T(8,128)(2,1)S(1)}, u32[]{:S(2)}, u32[]{:S(2)}) collective-permute-start(bf16[256,768]{1,0:T(8,128)(2,1)} %shard_map.306.refs_0_), channel_id=1, source_target_pairs={{0,1},{1,0},{2,3},{3,2},{4,5},{5,4},{6,7},{7,6},{8,9},{9,8},{10,11... | collective-permute-start | bytes 1179656 | tf_op jit(solution)/shard_map/ppermute | solution.py:528
  (69 other events, 466.4 us)
Sparse Core Ops, SparseCore 0:
  21.4 63.9 all-gather.1
  216.8 74.5 reduce-scatter.1

commit v4 on v3

--- a/solution.py
+++ b/solution.py
@@ -68,7 +68,7 @@
 
 
 def call(kernel, grid, ids, inputs, outputs, scratch, micros, aliases=None):
-    moved = sum(a.size * a.dtype.itemsize for a, _, _ in inputs)
+    moved = sum(a.size * a.dtype.itemsize for a, _, _ in inputs) if micros else 0
     return pl.pallas_call(
         kernel,
         grid_spec=pltpu.PrefetchScalarGridSpec(
@@ -333,7 +333,7 @@
     if first:
         grads, state, proj_acc, total, proj = refs
     else:
-        proj_in, grads, state, proj_acc, total, proj = refs
+        proj_in, grads, state, product, total, proj, proj_acc = refs
     step = pl.program_id(0)
     size = attended.shape[0] // heads
     rows = size + PAD
@@ -375,6 +375,8 @@
         ).astype(bf16)
         for copy in range(state.shape[0]):
             state[copy] = whole_state
+        if not first:
+            product[...] = proj_acc[...].T.astype(bf16)
 
 
 def softmax_back(grad, positive, negative):
@@ -390,7 +392,7 @@
     received, *refs
 ):
     if not first:
-        weight_in, map_in, bias_in, proj_in, gain, shift, mlp_rows, sums_a, sums_b = refs[:9]
+        weight_in, map_in, bias_in, product, gain, shift, mlp_rows, sums_a, sums_b = refs[:9]
         refs = refs[9:]
     slots, refs = (refs[:4], refs[4:]) if first else (refs[:2], refs[2:])
     if not first:
@@ -507,13 +509,12 @@
             ]
             small = jnp.concatenate(lines, axis=0)
             small = jnp.concatenate([small, jnp.zeros((SMALL - small.shape[0], dim), f32)], axis=0).astype(bf16)
-            proj_total = proj_in[...].T
-            shard = packed.shape[1] - SMALL
+            shard = total.shape[0] // packed.shape[0]
             for copy in range(packed.shape[0]):
                 packed[copy, :SMALL, :] = small
                 at = copy * shard
                 packed[copy, SMALL:, : 3 * width] = total[at : at + shard].astype(bf16)
-                packed[copy, SMALL:, 3 * width :] = proj_total[at : at + shard].astype(bf16)
+                packed[copy, SMALL:, 3 * width :] = product[at : at + shard, :]
 
 
 def exchange(array):
@@ -624,6 +625,7 @@
     rest_own = jnp.concatenate([fc_weight, out_weight.T], axis=1)
     rest = lax.all_gather(rest_own, "dp", axis=0, tiled=True)
     maps, maps_back, bias_qkv, seg, seg_col = pin(maps, maps_back, bias_qkv, seg, seg_col)
+    gain_a, shift_a, gain_m, shift_m, bias_p, bias_f, bias_o = pin(gain_a, shift_a, gain_m, shift_m, bias_p, bias_f, bias_o)
     row_tile = lambda array: (array, (None, tile, dim), lambda i, ids: (lax.div(i, tiles), lax.rem(i, tiles), 0))
     (attn_in,) = run(
         norm_kernel, (micro * tiles,), [row_tile(inputs), whole(gain_a), whole(shift_a)],
@@ -727,10 +729,9 @@
     proj_acc = ()
     grads, returned = [], []
 
-    def grads_in(m, array, across):
+    def grads_in(m, *gathered):
         nonlocal proj_acc
-        (across,) = pin(across)
-        grad_slots.append(gather_tensor(array, across))
+        grad_slots.append(gathered)
         result = run(
             functools.partial(grads_in_kernel, heads, pieces, m == 0), (tiles,),
             [whole(a) for a in grad_slots[m]]
@@ -740,8 +741,12 @@
                 seg_row(m, near), entering(m),
             ]
             + [whole(a) for a in proj_acc],
-            [columns_out(used, f32, near), whole_out(*state_out), whole_out((width, dim), f32)],
-            [pltpu.VMEM((used, 2 * size), f32), pltpu.VMEM((width, dim), bf16)],
+            [
+                columns_out(used, f32, near), whole_out(*state_out),
+                whole_out((width, dim), f32) if m == 0 else whole_out((dim, width), bf16),
+            ],
+            [pltpu.VMEM((used, 2 * size), f32), pltpu.VMEM((width, dim), bf16)]
+            + ([] if m == 0 else [pltpu.VMEM((width, dim), f32)]),
             7,
         )
         grads.append(result[0])
@@ -769,7 +774,7 @@
             ([whole_out((2, tile, dim), bf16)] * 2 if final else [whole_out((tile, dim), bf16)] * 4)
             + ([whole_out((count, SMALL + shard, 4 * width), bf16)] if final else [whole_out(*k) for k in kept]),
             ([pltpu.VMEM(*k) for k in kept] if final else []) + [pltpu.VMEM((used, 2 * size), f32)],
-            16,
+            0 if final else 16,
         )
         acc = result[2:] if final else result[4:]
         return result[:2] if final else result[:4]
@@ -797,30 +802,32 @@
     rest_sum = lax.psum_scatter(rest_grads, "dp", scatter_dimension=0, tiled=True)
     moved = middle(0, [whole(a) for a in mlp_terms[0]])
     crossed = swap(fold(mlp_terms[1]), 2)
-    grads_in(0, *moved)
+    array, across = moved
+    (across,) = pin(across)
+    grads_in(0, *gather_tensor(array, across))
     moved = middle(1, paired(mlp_terms[1], crossed))
     out_crossed = swap(fold(*out_pairs), 2)
-    returned = list(pin(*returned))
+    array, across = moved
+    returned[0], across = pin(returned[0], across)
+    moved = gather_tensor(array, across)
+    first_terms = scatter_tensor(attention_back(0))
     grads_in(1, *moved)
+    (rest_sum,) = pin(rest_sum)
     (finished,) = run(
         functools.partial(finish_kernel, micro), (1,),
         [whole(bias_o), whole(out_crossed)]
         + [spec for m in range(micro) for spec in (own_tile(residuals[m]), half(out_pairs[m][0], 0), half(out_pairs[m][1], 0))],
         [whole_out((micro, tile, dim), bf16)], [], 4,
     )
-    across = swap(finished, 2)
-    first_parts = attention_back(0)
-    (across,) = pin(across)
-    outputs = gather_tensor(finished, across)
-    first_terms = scatter_tensor(first_parts)
+    out_across = swap(finished, 2)
+    early = last(0, [whole(a) for a in first_terms])
+    early_across = swap(early, 2)
     kept, away = attention_back(1)
+    kept, away, packed, out_across, early_across = pin(kept, away, acc[0], out_across, early_across)
     last_pair = (kept, swap(away, 1))
-    total = exchange(acc[0])
-    (rest_sum,) = pin(rest_sum)
-    early = last(0, [whole(a) for a in first_terms])
-    early, folded = pin(early, fold(last_pair))
-    crossed = swap(folded, 2)
-    early_across = swap(early, 2)
+    total = exchange(packed)
+    crossed = swap(fold(last_pair), 2)
+    outputs = gather_tensor(finished, out_across)
     (output,) = run(
         functools.partial(order_kernel, tiles), (every,),
         [(a, (None, tile, dim), lambda i, ids: (lax.div(i, tiles), 0, 0)) for a in outputs],
@@ -830,31 +837,30 @@
         )],
         [], 6,
     )
+    rest_sum = rest_sum.astype(f32)
+    fc_grad, out_grad = pin(rest_sum[:, :units], rest_sum[:, units:].T)
     late = last(1, paired(last_pair, crossed))
     late_across = swap(late, 2)
-    rest_sum = rest_sum.astype(f32)
-    fc_grad, out_grad = pin(rest_sum[:, :units], rest_sum[:, units:].T)
-    (early_across,) = pin(early_across)
     input_grad = ordered(gather_tensor(early, early_across), 0)
-    total, late_across = pin(total, late_across)
+    (late_across,) = pin(late_across)
     input_grad = ordered(gather_tensor(late, late_across), 1, (input_grad,))
+    (total,) = pin(total)
     total = jnp.sum(total.astype(f32), axis=0)
-
     shared = total[:6]
     shared = (shared + swap(shared, 1)) + (swap(shared, 2) + swap(shared, 3))
     blocks = total[8 : 8 + size // 2].reshape(size // 2, 2, 2, heads, size)
     blocks = jnp.transpose(blocks, (2, 3, 1, 0, 4)).reshape(2, heads, size, size)
-    qkv_sum = total[SMALL:]
+    qkv_sum, proj_sum = total[SMALL:, : 3 * width], total[SMALL:, 3 * width :].T
     return (
         output,
         input_grad,
         shared[0],
         shared[1],
-        qkv_sum[:, : 3 * width].reshape(shard, 3, width),
+        qkv_sum.reshape(shard, 3, width),
         total[7, : 3 * width].reshape(3, width),
         blocks[0],
         blocks[1],
-        qkv_sum[:, 3 * width :].T,
+        proj_sum,
         shared[2],
         shared[4],
         shared[5],

time: 356 us -> 343 us (0.963)
  waiting for transfers between devices: 73.3 us -> 61.7 us
    ppermute x40, waiting for transfers between devices: 36.1 us -> 28.4 us  [swap(): return lax.ppermute(array, 'tensor', [(i, i ^ bit) for i in range(4)])]
    unnamed x106 -> x114, local copies, waits for them, and re-layouts: 14.8 us -> 17.7 us
  transfers between devices with their start and end apart: 50 -> 50, of which waited for: 13 -> 14; matrix products, arithmetic and copies ran while one was open for 5% -> 5% of each run, Pallas kernels for 46% -> 49%
where the time goes in v4:
time: 343 us; the launch traced here: 341 us
  Pallas kernels  167 us (49%)
  starting transfers between devices  62.8 us (18%)
  waiting for transfers between devices  61.7 us (18%)
  local copies, waits for them, and re-layouts  32.5 us (9%)
  between operations  14.8 us (4%)
    pallas_call x21, Pallas kernels, call(): pl.pallas_call(kernel, grid_spec=pltpu.PrefetchScalarGridSpec(num_scalar_...  167 us
    all_to_all x4, starting transfers between devices, exchange(): return lax.all_to_all(array, 'dp', 0, 0)  28.7 us
    ppermute x40, waiting for transfers between devices, swap(): return lax.ppermute(array, 'tensor', [(i, i ^ bit) for i in range(4)])  28.4 us
    all_to_all x4, waiting for transfers between devices, exchange(): return lax.all_to_all(array, 'dp', 0, 0)  28 us
    ppermute x40, starting transfers between devices, swap(): return lax.ppermute(array, 'tensor', [(i, i ^ bit) for i in range(4)])  23.1 us
    unnamed x114, local copies, waits for them, and re-layouts  17.7 us
    ppermute x4, starting transfers between devices, on_device(): lax.ppermute(state, 'dp', [(i, i + k) for i in range(count) if i % pieces...  11 us
  transfers between devices with their start and end apart: 50, of which 14 were waited for; matrix products, arithmetic and copies ran while one was open for 5% of the time, Pallas kernels for 49%

profile of v4, /device:TPU:0, one launch (start us, length us, event | category | flops | bytes accessed | tf_op | source)
XLA Modules:
  0.0 341.2 jit_solution(8687966043710099506)
XLA Ops:
  10.5 7.3 %all-to-all-start = ((bf16[8,96,768]{2,1,0:T(8,128)(2,1)}), bf16[8,96,768]{2,1,0:T(8,128)(2,1)S(1)}, u32[]{:S(2)}, u32[]{:S(2)}) async-start(bf16[8,96,768]{2,1,0:T(8,128)(2,1)} %broadcast_in_dim.2), calls=%async_computation | async-start | bytes 2359296 | tf_op jit(solution)/shard_map/all_to_all | solution.py:521
  26.4 7.8 %shard_map.288.attn_in = bf16[2,1024,768]{2,1,0:T(8,128)(2,1)} custom-call(s32[2]{0:T(128)} %pad_add_fusion.ids, bf16[2,1024,768]{2,1,0:T(8,128)(2,1)} %x.9, f32[1,768]{1,0:T(1,128)} %reshape.182.gain.refs_4_, f32[1,768]{1,0:T(1,128)} %reshape.184.shift.refs_5_), custom_call_target="tpu_custom_call" | custom-call | flops 8800000000 | bytes 3151872 | tf_op jit(solution)/shard_map/pallas_call | solution.py:72
  34.3 21.6 %all-to-all-done = bf16[8,96,768]{2,1,0:T(8,128)(2,1)S(1)} async-done(((bf16[8,96,768]{2,1,0:T(8,128)(2,1)}), bf16[8,96,768]{2,1,0:T(8,128)(2,1)S(1)}, u32[]{:S(2)}, u32[]{:S(2)}) %all-to-all-start) | async-done | bytes 1179680 | tf_op jit(solution)/shard_map/all_to_all | solution.py:521
  57.7 13.5 %shard_map.289 = (bf16[576,2048]{1,0:T(8,128)(2,1)}, bf16[768,2048]{1,0:T(8,128)(2,1)}, bf16[512,128]{1,0:T(8,128)(2,1)}) custom-call(s32[2]{0:T(128)} %pad_add_fusion.ids, bf16[2,1024,768]{2,1,0:T(8,128)(2,1)} %shard_map.288.attn_in, bf16[768,768]{1,0:T(8,128)(2,1)} %bitcast.16, f32[576,1]{1,0:T(8,128)} %copy.83.bias, bf16[2,192,192]{2,1,0:T(8,128)(2,1)} %copy.84.maps, ...), custom_call_target="tpu_custom_call" | custom-call | flops 14300000256 | bytes 4491520 | tf_op jit(solution)/shard_map/pallas_call | solution.py:72
  72.7 5.2 %collective-permute-start.5 = (bf16[512,128]{1,0:T(8,128)(2,1)}, bf16[512,128]{1,0:T(8,128)(2,1)S(1)}, u32[]{:S(2)}, u32[]{:S(2)}) collective-permute-start(bf16[512,128]{1,0:T(8,128)(2,1)} %get-tuple-element.208), channel_id=1, source_target_pairs={{0,12},{4,16},{8,20},{12,24},{16,28},{1,13},{5,17},{9,21},{13,25},... | collective-permute-start | bytes 393224 | tf_op jit(solution)/shard_map/ppermute | solution.py:658
  79.2 3.3 collective-permute-start.3
  84.9 3.6 %collective-permute-done.4.refs_1_ = bf16[512,128]{1,0:T(8,128)(2,1)S(1)} collective-permute-done((bf16[512,128]{1,0:T(8,128)(2,1)}, bf16[512,128]{1,0:T(8,128)(2,1)S(1)}, u32[]{:S(2)}, u32[]{:S(2)}) %collective-permute-start.4) | collective-permute-done | bytes 131104 | tf_op jit(solution)/shard_map/ppermute | solution.py:658
  89.8 6.5 %shard_map.290 = (f32[192,1024]{1,0:T(8,128)}, bf16[192,1024]{1,0:T(8,128)(2,1)}, f32[8,1024]{1,0:T(8,128)}, f32[4,240,128]{2,1,0:T(8,128)}) custom-call(s32[2]{0:T(128)} %pad_add_fusion.ids, bf16[576,2048]{1,0:T(8,128)(2,1)} %get-tuple-element.205.qkv_v.qkv, bf16[768,2048]{1,0:T(8,128)(2,1)} %get-tuple-element.206.feats.feats_q, ...), custom_call_target="tpu_custom_call" | custom-call | flops 7150000128 | bytes 6045696 | tf_op jit(solution)/shard_map/pallas_call | solution.py:72
  97.6 6.5 %shard_map.291 = (f32[192,1024]{1,0:T(8,128)}, bf16[192,1024]{1,0:T(8,128)(2,1)}, f32[8,1024]{1,0:T(8,128)}, f32[4,240,128]{2,1,0:T(8,128)}) custom-call(s32[2]{0:T(128)} %pad_add_fusion.ids, bf16[576,2048]{1,0:T(8,128)(2,1)} %get-tuple-element.205.qkv_v.qkv, bf16[768,2048]{1,0:T(8,128)(2,1)} %get-tuple-element.206.feats.feats_q, ...), custom_call_target="tpu_custom_call" | custom-call | flops 7150000128 | bytes 6045696 | tf_op jit(solution)/shard_map/pallas_call | solution.py:72
  104.1 4.1 %collective-permute-done.7.a1 = bf16[192,1024]{1,0:T(8,128)(2,1)S(1)} collective-permute-done((bf16[192,1024]{1,0:T(8,128)(2,1)}, bf16[192,1024]{1,0:T(8,128)(2,1)S(1)}, u32[]{:S(2)}, u32[]{:S(2)}) %collective-permute-start.7) | collective-permute-done | bytes 393248 | tf_op jit(solution)/shard_map/ppermute | solution.py:529
  111.2 20.4 %shard_map.292 = (f32[4,256,768]{2,1,0:T(8,128)}, bf16[256,768]{1,0:T(8,128)(2,1)}, bf16[256,768]{1,0:T(8,128)(2,1)}, bf16[256,768]{1,0:T(8,128)(2,1)}, bf16[256...) custom-call(s32[2]{0:T(128)} %pad_add_fusion.ids, ...), custom_call_target="tpu_custom_call" | custom-call | flops 23100000256 | bytes 13774848 | tf_op jit(solution)/shard_map/pallas_call | solution.py:72
  135.3 22.8 %shard_map.293 = (f32[4,256,768]{2,1,0:T(8,128)}, bf16[2,256,768]{2,1,0:T(8,128)(2,1)}, bf16[2,256,768]{2,1,0:T(8,128)(2,1)}, bf16[2,256,768]{2,1,0:T(8,128)(2,1...) custom-call(s32[2]{0:T(128)} %pad_add_fusion.ids, bf16[2,1024,768]{2,1,0:T(8,128)(2,1)} %x.9, ...), custom_call_target="tpu_custom_call" | custom-call | flops 23100000256 | bytes 18496512 | tf_op jit(solution)/shard_map/pallas_call | solution.py:72
  159.9 4.2 %shard_map.294 = (f32[256,768]{1,0:T(8,128)}, bf16[256,768]{1,0:T(8,128)(2,1)}, f32[2,768]{1,0:T(2,128)}) custom-call(s32[2]{0:T(128)} %pad_add_fusion.ids, f32[4,256,768]{2,1,0:T(8,128)} %get-tuple-element.255.residual.refs_0_, bf16[2,1024,768]{2,1,0:T(8,128)(2,1)} %cot.7, f32[1,768]{1,0:T(1,128)} %reshape.186.gain, ...), custom_call_target="tpu_custom_call" | custom-call | flops 4400000000 | bytes 7867392 | tf_op jit(solution)/shard_map/pallas_call | solution.py:72
  169.0 6.7 %collective-permute-done.17.g1 = bf16[256,768]{1,0:T(8,128)(2,1)S(1)} collective-permute-done((bf16[256,768]{1,0:T(8,128)(2,1)}, bf16[256,768]{1,0:T(8,128)(2,1)S(1)}, u32[]{:S(2)}, u32[]{:S(2)}) %collective-permute-start.17) | collective-permute-done | bytes 393248 | tf_op jit(solution)/shard_map/ppermute | solution.py:529
  178.1 7.4 %shard_map.296 = (f32[240,1024]{1,0:T(8,128)}, bf16[8,256,128]{2,1,0:T(8,128)(2,1)}, f32[192,768]{1,0:T(8,128)}) custom-call(s32[2]{0:T(128)} %pad_add_fusion.ids, bf16[256,768]{1,0:T(8,128)(2,1)} %get-tuple-element.267.g0, bf16[256,768]{1,0:T(8,128)(2,1)} %copy-done.45, bf16[256,768]{1,0:T(8,128)(2,1)} %copy-done.47, ...), custom_call_target="tpu_custom_call" | custom-call | flops 7699999744 | bytes 6365184 | tf_op jit(solution)/shard_map/pallas_call | solution.py:72
  185.4 12.4 %all-to-all-start.1 = ((bf16[8,256,128]{2,1,0:T(8,128)(2,1)}), bf16[8,256,128]{2,1,0:T(8,128)(2,1)S(1)}, u32[]{:S(2)}, u32[]{:S(2)}) async-start(bf16[8,256,128]{2,1,0:T(8,128)(2,1)} %get-tuple-element.287), calls=%async_computation.1 | async-start | bytes 1048576 | tf_op jit(solution)/shard_map/all_to_all | solution.py:521
  197.9 4.0 %shard_map.297 = (f32[256,768]{1,0:T(8,128)}, bf16[256,768]{1,0:T(8,128)(2,1)}, f32[2,768]{1,0:T(2,128)}) custom-call(s32[2]{0:T(128)} %pad_add_fusion.ids, f32[4,256,768]{2,1,0:T(8,128)} %get-tuple-element.276.residual.refs_3_, bf16[2,1024,768]{2,1,0:T(8,128)(2,1)} %cot.7, f32[1,768]{1,0:T(1,128)} %reshape.186.gain, ...), custom_call_target="tpu_custom_call" | custom-call | flops 4400000000 | bytes 8260608 | tf_op jit(solution)/shard_map/pallas_call | solution.py:72
  205.1 3.1 shard_map.298
  208.8 5.3 %collective-permute-done.23.g1 = bf16[256,768]{1,0:T(8,128)(2,1)S(1)} collective-permute-done((bf16[256,768]{1,0:T(8,128)(2,1)}, bf16[256,768]{1,0:T(8,128)(2,1)S(1)}, u32[]{:S(2)}, u32[]{:S(2)}) %collective-permute-start.23) | collective-permute-done | bytes 393248 | tf_op jit(solution)/shard_map/ppermute | solution.py:529
  216.9 15.3 %shard_map.299 = (bf16[256,768]{1,0:T(8,128)(2,1)}, bf16[256,768]{1,0:T(8,128)(2,1)}, bf16[256,768]{1,0:T(8,128)(2,1)}, bf16[256,768]{1,0:T(8,128)(2,1)}, f32[57...) custom-call(s32[2]{0:T(128)} %pad_add_fusion.ids, bf16[576,2048]{1,0:T(8,128)(2,1)} %get-tuple-element.205.qkv_v.qkv, ...), custom_call_target="tpu_custom_call" | custom-call | flops 17600000000 | bytes 12279808 | tf_op jit(solution)/shard_map/pallas_call | solution.py:72
  235.1 7.1 %shard_map.300 = (f32[240,1024]{1,0:T(8,128)}, bf16[8,256,128]{2,1,0:T(8,128)(2,1)}, bf16[768,192]{1,0:T(8,128)(2,1)}) custom-call(s32[2]{0:T(128)} %pad_add_fusion.ids, bf16[256,768]{1,0:T(8,128)(2,1)} %get-tuple-element.288.g0, bf16[256,768]{1,0:T(8,128)(2,1)} %copy-done.33, bf16[256,768]{1,0:T(8,128)(2,1)} %collective-permute-done.24.g2, ...), custom_call_target="tpu_custom_call" | custom-call | flops 7699999744 | bytes 6955008 | tf_op jit(solution)/shard_map/pallas_call | solution.py:72
  242.3 4.0 %all-to-all-start.2 = ((bf16[8,256,128]{2,1,0:T(8,128)(2,1)}), bf16[8,256,128]{2,1,0:T(8,128)(2,1)S(1)}, u32[]{:S(2)}, u32[]{:S(2)}) async-start(bf16[8,256,128]{2,1,0:T(8,128)(2,1)} %get-tuple-element.323), calls=%async_computation.3 | async-start | bytes 1048576 | tf_op jit(solution)/shard_map/all_to_all | solution.py:521
  247.6 4.0 %shard_map.301.refs_0_ = bf16[2,256,768]{2,1,0:T(8,128)(2,1)} custom-call(s32[2]{0:T(128)} %pad_add_fusion.ids, f32[1,768]{1,0:T(1,128)} %reshape.194.bias, bf16[2,256,768]{2,1,0:T(8,128)(2,1)} %copy-done.26, f32[4,256,768]{2,1,0:T(8,128)} %get-tuple-element.255.residual.refs_0_, bf16[2,256,768]{2,1,0:T(8,128)(2,1)} %get-tuple-element.282.refs_0_.refs_1_, ...), custom_call_target="tpu_custom_call" | custom-call | flops 4400000000 | bytes 10226688 | tf_op jit(solution)/shard_map/pallas_call | solution.py:72
  254.7 3.8 %shard_map.302.refs_0_ = bf16[256,768]{1,0:T(8,128)(2,1)} custom-call(s32[2]{0:T(128)} %pad_add_fusion.ids, bf16[2,1024,768]{2,1,0:T(8,128)(2,1)} %x.9, f32[256,768]{1,0:T(8,128)} %get-tuple-element.315.grad_residual, f32[1,768]{1,0:T(1,128)} %reshape.182.gain.refs_4_, bf16[256,768]{1,0:T(8,128)(2,1)} %get-tuple-element.316.refs_0_, ...), custom_call_target="tpu_custom_call" | custom-call | flops 4400000000 | bytes 5508096 | tf_op jit(solution)/shard_map/pallas_call | solution.py:72
  261.7 17.9 %shard_map.303 = (bf16[2,256,768]{2,1,0:T(8,128)(2,1)}, bf16[2,256,768]{2,1,0:T(8,128)(2,1)}, bf16[8,144,768]{2,1,0:T(8,128)(2,1)}) custom-call(s32[2]{0:T(128)} %pad_add_fusion.ids, bf16[576,2048]{1,0:T(8,128)(2,1)} %get-tuple-element.205.qkv_v.qkv, bf16[768,2048]{1,0:T(8,128)(2,1)} %get-tuple-element.206.feats.feats_q, ...), custom_call_target="tpu_custom_call" | custom-call | tf_op jit(solution)/shard_map/pallas_call | solution.py:72
  280.7 5.0 %all-to-all-start.3 = ((bf16[8,144,768]{2,1,0:T(8,128)(2,1)}), bf16[8,144,768]{2,1,0:T(8,128)(2,1)S(1)}, u32[]{:S(2)}, u32[]{:S(2)}) async-start(bf16[8,144,768]{2,1,0:T(8,128)(2,1)} %get-tuple-element.359), calls=%async_computation.4 | async-start | bytes 3538944 | tf_op jit(solution)/shard_map/all_to_all | solution.py:521
  292.4 6.2 %shard_map.305 = bf16[2,1024,768]{2,1,0:T(8,128)(2,1)} custom-call(s32[2]{0:T(128)} %pad_add_fusion.ids, bf16[2,256,768]{2,1,0:T(8,128)(2,1)} %shard_map.301.refs_0_, bf16[2,256,768]{2,1,0:T(8,128)(2,1)} %copy-done.24, bf16[2,256,768]{2,1,0:T(8,128)(2,1)} %collective-permute-done.33.refs_2_, bf16[2,256,768]{2,1,0:T(8,128)(2,1)} %collective-permute-done.34.refs_3_), custom_call_target="tpu_custom_call" | custom-call | flops 6600000000 | bytes 3145728 | tf_op jit(solution)/shard_map/pallas_call | solution.py:72
  298.6 3.7 %collective-permute-done.35.refs_2_ = bf16[1,256,768]{2,1,0:T(8,128)(2,1)} collective-permute-done((bf16[1,256,768]{2,1,0:T(8,128)(2,1)}, bf16[1,256,768]{2,1,0:T(8,128)(2,1)}, u32[]{:S(2)}, u32[]{:S(2)}) %collective-permute-start.35) | collective-permute-done | bytes 393248 | tf_op jit(solution)/shard_map/ppermute | solution.py:529
  302.4 3.6 %shard_map.306.refs_0_ = bf16[256,768]{1,0:T(8,128)(2,1)} custom-call(s32[2]{0:T(128)} %pad_add_fusion.ids, bf16[2,1024,768]{2,1,0:T(8,128)(2,1)} %x.9, f32[256,768]{1,0:T(8,128)} %get-tuple-element.349.grad_residual, f32[1,768]{1,0:T(1,128)} %reshape.182.gain.refs_4_, bf16[2,256,768]{2,1,0:T(8,128)(2,1)} %get-tuple-element.341.refs_0_, ...), custom_call_target="tpu_custom_call" | custom-call | flops 4400000000 | bytes 5901312 | tf_op jit(solution)/shard_map/pallas_call | solution.py:72
  307.5 3.7 %shard_map.307.refs_4_ = bf16[2,1024,768]{2,1,0:T(8,128)(2,1)} custom-call(s32[2]{0:T(128)} %pad_add_fusion.ids, bf16[256,768]{1,0:T(8,128)(2,1)} %shard_map.302.refs_0_, bf16[256,768]{1,0:T(8,128)(2,1)} %copy-done.31, bf16[256,768]{1,0:T(8,128)(2,1)} %collective-permute-done.36.refs_2_, bf16[256,768]{1,0:T(8,128)(2,1)} %collective-permute-done.37.refs_3_), custom_call_target="tpu_custom_call" | custom-call | flops 4400000000 | bytes 1572864 | tf_op jit(solution)/shard_map/pallas_call | solution.py:72
  311.2 6.5 %collective-permute-done.38.refs_1_ = bf16[256,768]{1,0:T(8,128)(2,1)S(1)} collective-permute-done((bf16[256,768]{1,0:T(8,128)(2,1)}, bf16[256,768]{1,0:T(8,128)(2,1)S(1)}, u32[]{:S(2)}, u32[]{:S(2)}) %collective-permute-start.38) | collective-permute-done | bytes 393248 | tf_op jit(solution)/shard_map/ppermute | solution.py:529
  320.2 3.7 %shard_map.308 = bf16[2,1024,768]{2,1,0:T(8,128)(2,1)} custom-call(s32[2]{0:T(128)} %pad_add_fusion.ids, bf16[256,768]{1,0:T(8,128)(2,1)} %shard_map.306.refs_0_, bf16[256,768]{1,0:T(8,128)(2,1)} %copy-done.50, bf16[256,768]{1,0:T(8,128)(2,1)} %copy-done.49, bf16[256,768]{1,0:T(8,128)(2,1)} %copy-done.51, ...), custom_call_target="tpu_custom_call", output_to_operand_aliasing={{}: (5, {})} | custom-call | flops 4400000000 | bytes 4718592 | tf_op jit(solution)/shard_map/pallas_call | solution.py:72
  (248 shorter events, 76.2 us)
Async XLA Ops:
  10.5 45.3 %all-to-all-start = ((bf16[8,96,768]{2,1,0:T(8,128)(2,1)}), bf16[8,96,768]{2,1,0:T(8,128)(2,1)S(1)}, u32[]{:S(2)}, u32[]{:S(2)}) async-start(bf16[8,96,768]{2,1,0:T(8,128)(2,1)} %broadcast_in_dim.2), calls=%async_computation | async-start | bytes 2359296 | tf_op jit(solution)/shard_map/all_to_all | solution.py:521
  17.8 92.5 %all-gather.2.cloned.1.call-start = ((), (), s32[]{:S(2)}) async-start(), calls=%async_computation.5 | async-start | bytes 2654208 | tf_op jit(solution)/shard_map/all_gather | solution.py:626
  18.6 228.1 %reduce-scatter.2.cloned.1.call-start = ((), (), s32[]{:S(2)}) async-start(), calls=%async_computation.6 | async-start | bytes 2654208 | tf_op jit(solution)/shard_map/reduce_scatter | solution.py:802
  56.1 23.1 %collective-permute-start.1 = (bf16[768,192]{1,0:T(8,128)(2,1)S(1)}, bf16[768,192]{1,0:T(8,128)(2,1)S(1)}, u32[]{:S(2)}, u32[]{:S(2)}) collective-permute-start(bf16[768,192]{1,0:T(8,128)(2,1)S(1)} %slice.70.p0.proj_t), channel_id=1, source_target_pairs={{0,1},{1,0},{2,3},{3,2},{4,5},{5,4},{6,7},{7,6},{8,9},{9,8},{10,11... | collective-permute-start | bytes 884744 | tf_op jit(solution)/shard_map/ppermute | solution.py:529
  56.1 15.1 %collective-permute-start = (bf16[768,192]{1,0:T(8,128)(2,1)S(1)}, bf16[768,192]{1,0:T(8,128)(2,1)S(1)}, u32[]{:S(2)}, u32[]{:S(2)}) collective-permute-start(bf16[768,192]{1,0:T(8,128)(2,1)S(1)} %slice.70.p0.proj_t), channel_id=1, source_target_pairs={{0,2},{1,3},{2,0},{3,1},{4,6},{5,7},{6,4},{7,5},{8,10},{9,11},{10,... | collective-permute-start | bytes 884744 | tf_op jit(solution)/shard_map/ppermute | solution.py:529
  71.2 12.6 %collective-permute-start.2 = (bf16[768,192]{1,0:T(8,128)(2,1)S(1)}, bf16[768,192]{1,0:T(8,128)(2,1)S(1)}, u32[]{:S(2)}, u32[]{:S(2)}) collective-permute-start(bf16[768,192]{1,0:T(8,128)(2,1)S(1)} %collective-permute-done.p1), channel_id=1, source_target_pairs={{0,1},{1,0},{2,3},{3,2},{4,5},{5,4},{6,7},{7,6},{8,9},{9,8},{10,11... | collective-permute-start | bytes 884744 | tf_op jit(solution)/shard_map/ppermute | solution.py:529
  71.4 12.4 %collective-permute-start.6 = (bf16[512,128]{1,0:T(8,128)(2,1)}, bf16[512,128]{1,0:T(8,128)(2,1)S(1)}, u32[]{:S(2)}, u32[]{:S(2)}) collective-permute-start(bf16[512,128]{1,0:T(8,128)(2,1)} %get-tuple-element.208), channel_id=1, source_target_pairs={{0,16},{4,20},{8,24},{12,28},{1,17},{5,21},{9,25},{13,29},{2,18},{... | collective-permute-start | bytes 393224 | tf_op jit(solution)/shard_map/ppermute | solution.py:658
  72.7 12.2 %collective-permute-start.5 = (bf16[512,128]{1,0:T(8,128)(2,1)}, bf16[512,128]{1,0:T(8,128)(2,1)S(1)}, u32[]{:S(2)}, u32[]{:S(2)}) collective-permute-start(bf16[512,128]{1,0:T(8,128)(2,1)} %get-tuple-element.208), channel_id=1, source_target_pairs={{0,12},{4,16},{8,20},{12,24},{16,28},{1,13},{5,17},{9,21},{13,25},... | collective-permute-start | bytes 393224 | tf_op jit(solution)/shard_map/ppermute | solution.py:658
  96.3 14.0 %collective-permute-start.8 = (bf16[192,1024]{1,0:T(8,128)(2,1)}, bf16[192,1024]{1,0:T(8,128)(2,1)S(1)}, u32[]{:S(2)}, u32[]{:S(2)}) collective-permute-start(bf16[192,1024]{1,0:T(8,128)(2,1)} %get-tuple-element.219.a0.attended_low), channel_id=1, source_target_pairs={{0,1},{1,0},{2,3},{3,2},{4,5},{5,4},{6,7},{7,6},{8,9},{9,8},{10,11... | collective-permute-start | bytes 1179656 | tf_op jit(solution)/shard_map/ppermute | solution.py:529
  108.2 24.6 %collective-permute-start.12 = (bf16[192,1024]{1,0:T(8,128)(2,1)}, bf16[192,1024]{1,0:T(8,128)(2,1)S(1)}, u32[]{:S(2)}, u32[]{:S(2)}) collective-permute-start(bf16[192,1024]{1,0:T(8,128)(2,1)} %get-tuple-element.241.a0.attended_low), channel_id=1, source_target_pairs={{0,3},{1,2},{2,1},{3,0},{4,7},{5,6},{6,5},{7,4},{8,11},{9,10},{10,... | collective-permute-start | bytes 1179656 | tf_op jit(solution)/shard_map/ppermute | solution.py:529
  109.3 24.5 %collective-permute-start.11 = (bf16[192,1024]{1,0:T(8,128)(2,1)}, bf16[192,1024]{1,0:T(8,128)(2,1)S(1)}, u32[]{:S(2)}, u32[]{:S(2)}) collective-permute-start(bf16[192,1024]{1,0:T(8,128)(2,1)} %get-tuple-element.241.a0.attended_low), channel_id=1, source_target_pairs={{0,1},{1,0},{2,3},{3,2},{4,5},{5,4},{6,7},{7,6},{8,9},{9,8},{10,11... | collective-permute-start | bytes 1179656 | tf_op jit(solution)/shard_map/ppermute | solution.py:529
  109.3 24.5 %collective-permute-start.10 = (bf16[192,1024]{1,0:T(8,128)(2,1)}, bf16[192,1024]{1,0:T(8,128)(2,1)S(1)}, u32[]{:S(2)}, u32[]{:S(2)}) collective-permute-start(bf16[192,1024]{1,0:T(8,128)(2,1)} %get-tuple-element.241.a0.attended_low), channel_id=1, source_target_pairs={{0,2},{1,3},{2,0},{3,1},{4,6},{5,7},{6,4},{7,5},{8,10},{9,11},{10,... | collective-permute-start | bytes 1179656 | tf_op jit(solution)/shard_map/ppermute | solution.py:529
  131.6 26.6 %collective-permute-start.13 = (bf16[256,768]{1,0:T(8,128)(2,1)}, bf16[256,768]{1,0:T(8,128)(2,1)S(1)}, u32[]{:S(2)}, u32[]{:S(2)}) collective-permute-start(bf16[256,768]{1,0:T(8,128)(2,1)} %get-tuple-element.257), channel_id=1, source_target_pairs={{0,2},{1,3},{2,0},{3,1},{4,6},{5,7},{6,4},{7,5},{8,10},{9,11},{10,... | collective-permute-start | bytes 1179656 | tf_op jit(solution)/shard_map/ppermute | solution.py:529
  132.7 25.5 %collective-permute-start.14 = (bf16[256,768]{1,0:T(8,128)(2,1)}, bf16[256,768]{1,0:T(8,128)(2,1)S(1)}, u32[]{:S(2)}, u32[]{:S(2)}) collective-permute-start(bf16[256,768]{1,0:T(8,128)(2,1)} %get-tuple-element.258), channel_id=1, source_target_pairs={{0,1},{1,0},{2,3},{3,2},{4,5},{5,4},{6,7},{7,6},{8,9},{9,8},{10,11... | collective-permute-start | bytes 1179656 | tf_op jit(solution)/shard_map/ppermute | solution.py:529
  132.7 25.5 %collective-permute-start.15 = (bf16[256,768]{1,0:T(8,128)(2,1)}, bf16[256,768]{1,0:T(8,128)(2,1)S(1)}, u32[]{:S(2)}, u32[]{:S(2)}) collective-permute-start(bf16[256,768]{1,0:T(8,128)(2,1)} %get-tuple-element.259), channel_id=1, source_target_pairs={{0,3},{1,2},{2,1},{3,0},{4,7},{5,6},{6,5},{7,4},{8,11},{9,10},{10,... | collective-permute-start | bytes 1179656 | tf_op jit(solution)/shard_map/ppermute | solution.py:529
  175.7 27.5 %collective-permute-start.22 = (bf16[2,256,768]{2,1,0:T(8,128)(2,1)}, bf16[2,256,768]{2,1,0:T(8,128)(2,1)S(1)}, u32[]{:S(2)}, u32[]{:S(2)}) collective-permute-start(bf16[2,256,768]{2,1,0:T(8,128)(2,1)} %get-tuple-element.285), channel_id=1, source_target_pairs={{0,1},{1,0},{2,3},{3,2},{4,5},{5,4},{6,7},{7,6},{8,9},{9,8},{10,11... | collective-permute-start | bytes 2359304 | tf_op jit(solution)/shard_map/ppermute | solution.py:529
  176.3 27.0 %collective-permute-start.21 = (bf16[2,256,768]{2,1,0:T(8,128)(2,1)S(1)}, bf16[2,256,768]{2,1,0:T(8,128)(2,1)S(1)}, u32[]{:S(2)}, u32[]{:S(2)}) collective-permute-start(bf16[2,256,768]{2,1,0:T(8,128)(2,1)S(1)} %copy-done.20), channel_id=1, source_target_pairs={{0,1},{1,0},{2,3},{3,2},{4,5},{5,4},{6,7},{7,6},{8,9},{9,8},{10,11... | collective-permute-start | bytes 2359304 | tf_op jit(solution)/shard_map/ppermute | solution.py:529
  176.3 21.6 %collective-permute-start.20 = (bf16[1,256,768]{2,1,0:T(8,128)(2,1)}, bf16[1,256,768]{2,1,0:T(8,128)(2,1)}, u32[]{:S(2)}, u32[]{:S(2)}) collective-permute-start(bf16[1,256,768]{2,1,0:T(8,128)(2,1)} %shard_map.295), channel_id=1, source_target_pairs={{0,2},{1,3},{2,0},{3,1},{4,6},{5,7},{6,4},{7,5},{8,10},{9,11},{10,... | collective-permute-start | bytes 1179656 | tf_op jit(solution)/shard_map/ppermute | solution.py:529
  185.4 30.7 %all-to-all-start.1 = ((bf16[8,256,128]{2,1,0:T(8,128)(2,1)}), bf16[8,256,128]{2,1,0:T(8,128)(2,1)S(1)}, u32[]{:S(2)}, u32[]{:S(2)}) async-start(bf16[8,256,128]{2,1,0:T(8,128)(2,1)} %get-tuple-element.287), calls=%async_computation.1 | async-start | bytes 1048576 | tf_op jit(solution)/shard_map/all_to_all | solution.py:521
  201.9 12.2 %collective-permute-start.23 = (bf16[256,768]{1,0:T(8,128)(2,1)}, bf16[256,768]{1,0:T(8,128)(2,1)S(1)}, u32[]{:S(2)}, u32[]{:S(2)}) collective-permute-start(bf16[256,768]{1,0:T(8,128)(2,1)} %get-tuple-element.288.g0), channel_id=1, source_target_pairs={{0,2},{1,3},{2,0},{3,1},{4,6},{5,7},{6,4},{7,5},{8,10},{9,11},{10,... | collective-permute-start | bytes 1179656 | tf_op jit(solution)/shard_map/ppermute | solution.py:529
  203.3 30.2 %collective-permute-start.24 = (bf16[256,768]{1,0:T(8,128)(2,1)}, bf16[256,768]{1,0:T(8,128)(2,1)}, u32[]{:S(2)}, u32[]{:S(2)}) collective-permute-start(bf16[256,768]{1,0:T(8,128)(2,1)} %get-tuple-element.288.g0), channel_id=1, source_target_pairs={{0,1},{1,0},{2,3},{3,2},{4,5},{5,4},{6,7},{7,6},{8,9},{9,8},{10,11... | collective-permute-start | bytes 1179656 | tf_op jit(solution)/shard_map/ppermute | solution.py:529
  208.2 38.6 %collective-permute-start.26 = (bf16[2,256,768]{2,1,0:T(8,128)(2,1)}, bf16[2,256,768]{2,1,0:T(8,128)(2,1)S(1)}, u32[]{:S(2)}, u32[]{:S(2)}) collective-permute-start(bf16[2,256,768]{2,1,0:T(8,128)(2,1)} %shard_map.298), channel_id=1, source_target_pairs={{0,2},{1,3},{2,0},{3,1},{4,6},{5,7},{6,4},{7,5},{8,10},{9,11},{10,... | collective-permute-start | bytes 2359304 | tf_op jit(solution)/shard_map/ppermute | solution.py:529
  216.1 18.3 %collective-permute-start.25 = (bf16[256,768]{1,0:T(8,128)(2,1)S(1)}, bf16[256,768]{1,0:T(8,128)(2,1)S(1)}, u32[]{:S(2)}, u32[]{:S(2)}) collective-permute-start(bf16[256,768]{1,0:T(8,128)(2,1)S(1)} %collective-permute-done.23.g1), channel_id=1, source_target_pairs={{0,1},{1,0},{2,3},{3,2},{4,5},{5,4},{6,7},{7,6},{8,9},{9,8},{10,11... | collective-permute-start | bytes 1179656 | tf_op jit(solution)/shard_map/ppermute | solution.py:529
  232.2 20.9 %collective-permute-start.27 = (bf16[256,768]{1,0:T(8,128)(2,1)}, bf16[256,768]{1,0:T(8,128)(2,1)S(1)}, u32[]{:S(2)}, u32[]{:S(2)}) collective-permute-start(bf16[256,768]{1,0:T(8,128)(2,1)} %get-tuple-element.317), channel_id=1, source_target_pairs={{0,2},{1,3},{2,0},{3,1},{4,6},{5,7},{6,4},{7,5},{8,10},{9,11},{10,... | collective-permute-start | bytes 1179656 | tf_op jit(solution)/shard_map/ppermute | solution.py:529
  233.5 19.6 %collective-permute-start.28 = (bf16[256,768]{1,0:T(8,128)(2,1)}, bf16[256,768]{1,0:T(8,128)(2,1)S(1)}, u32[]{:S(2)}, u32[]{:S(2)}) collective-permute-start(bf16[256,768]{1,0:T(8,128)(2,1)} %get-tuple-element.318), channel_id=1, source_target_pairs={{0,1},{1,0},{2,3},{3,2},{4,5},{5,4},{6,7},{7,6},{8,9},{9,8},{10,11... | collective-permute-start | bytes 1179656 | tf_op jit(solution)/shard_map/ppermute | solution.py:529
  233.5 19.6 %collective-permute-start.29 = (bf16[256,768]{1,0:T(8,128)(2,1)}, bf16[256,768]{1,0:T(8,128)(2,1)S(1)}, u32[]{:S(2)}, u32[]{:S(2)}) collective-permute-start(bf16[256,768]{1,0:T(8,128)(2,1)} %get-tuple-element.319), channel_id=1, source_target_pairs={{0,3},{1,2},{2,1},{3,0},{4,7},{5,6},{6,5},{7,4},{8,11},{9,10},{10,... | collective-permute-start | bytes 1179656 | tf_op jit(solution)/shard_map/ppermute | solution.py:529
  242.3 18.6 %all-to-all-start.2 = ((bf16[8,256,128]{2,1,0:T(8,128)(2,1)}), bf16[8,256,128]{2,1,0:T(8,128)(2,1)S(1)}, u32[]{:S(2)}, u32[]{:S(2)}) async-start(bf16[8,256,128]{2,1,0:T(8,128)(2,1)} %get-tuple-element.323), calls=%async_computation.3 | async-start | bytes 1048576 | tf_op jit(solution)/shard_map/all_to_all | solution.py:521
  251.6 28.0 %collective-permute-start.30 = (bf16[2,256,768]{2,1,0:T(8,128)(2,1)}, bf16[2,256,768]{2,1,0:T(8,128)(2,1)S(1)}, u32[]{:S(2)}, u32[]{:S(2)}) collective-permute-start(bf16[2,256,768]{2,1,0:T(8,128)(2,1)} %shard_map.301.refs_0_), channel_id=1, source_target_pairs={{0,2},{1,3},{2,0},{3,1},{4,6},{5,7},{6,4},{7,5},{8,10},{9,11},{10,... | collective-permute-start | bytes 2359304 | tf_op jit(solution)/shard_map/ppermute | solution.py:529
  258.5 21.1 %collective-permute-start.31 = (bf16[256,768]{1,0:T(8,128)(2,1)}, bf16[256,768]{1,0:T(8,128)(2,1)S(1)}, u32[]{:S(2)}, u32[]{:S(2)}) collective-permute-start(bf16[256,768]{1,0:T(8,128)(2,1)} %shard_map.302.refs_0_), channel_id=1, source_target_pairs={{0,2},{1,3},{2,0},{3,1},{4,6},{5,7},{6,4},{7,5},{8,10},{9,11},{10,... | collective-permute-start | bytes 1179656 | tf_op jit(solution)/shard_map/ppermute | solution.py:529
  280.7 45.9 %all-to-all-start.3 = ((bf16[8,144,768]{2,1,0:T(8,128)(2,1)}), bf16[8,144,768]{2,1,0:T(8,128)(2,1)S(1)}, u32[]{:S(2)}, u32[]{:S(2)}) async-start(bf16[8,144,768]{2,1,0:T(8,128)(2,1)} %get-tuple-element.359), calls=%async_computation.4 | async-start | bytes 3538944 | tf_op jit(solution)/shard_map/all_to_all | solution.py:521
  287.0 20.4 %collective-permute-start.36 = (bf16[256,768]{1,0:T(8,128)(2,1)S(1)}, bf16[256,768]{1,0:T(8,128)(2,1)}, u32[]{:S(2)}, u32[]{:S(2)}) collective-permute-start(bf16[256,768]{1,0:T(8,128)(2,1)S(1)} %copy-done.30), channel_id=1, source_target_pairs={{0,1},{1,0},{2,3},{3,2},{4,5},{5,4},{6,7},{7,6},{8,9},{9,8},{10,11... | collective-permute-start | bytes 1179656 | tf_op jit(solution)/shard_map/ppermute | solution.py:529
  287.9 19.6 %collective-permute-start.37 = (bf16[256,768]{1,0:T(8,128)(2,1)}, bf16[256,768]{1,0:T(8,128)(2,1)}, u32[]{:S(2)}, u32[]{:S(2)}) collective-permute-start(bf16[256,768]{1,0:T(8,128)(2,1)} %copy-done.31), channel_id=1, source_target_pairs={{0,1},{1,0},{2,3},{3,2},{4,5},{5,4},{6,7},{7,6},{8,9},{9,8},{10,11... | collective-permute-start | bytes 1179656 | tf_op jit(solution)/shard_map/ppermute | solution.py:529
  (73 other events, 460.0 us)
Sparse Core Ops, SparseCore 0:
  21.4 65.9 all-gather.1
  165.3 81.4 reduce-scatter.1

commit v5 on v4

--- a/solution.py
+++ b/solution.py
@@ -13,7 +13,7 @@
 GELU_SCALE = 0.7978845608028654
 GELU_CUBIC = 0.044715
 PAD = 16
-SMALL = 48
+SMALL = 40
 RATE = 1.1e9
 
 f32 = jnp.float32
@@ -75,8 +75,10 @@
             num_scalar_prefetch=1,
             grid=grid,
             in_specs=[
-                pl.BlockSpec(block, index) if block else pl.BlockSpec(memory_space=pl.ANY)
-                for _, block, index in inputs
+                pl.BlockSpec(memory_space=pl.ANY) if not block
+                else pl.BlockSpec(memory_space=pltpu.VMEM) if block == array.shape
+                else pl.BlockSpec(block, index)
+                for array, block, index in inputs
             ],
             out_specs=[pl.BlockSpec(block, index) for _, _, block, index in outputs],
             scratch_shapes=scratch,
@@ -507,8 +509,7 @@
                 jnp.concatenate([bias_row, jnp.zeros((1, dim - 3 * width), f32)], axis=1),
                 turned,
             ]
-            small = jnp.concatenate(lines, axis=0)
-            small = jnp.concatenate([small, jnp.zeros((SMALL - small.shape[0], dim), f32)], axis=0).astype(bf16)
+            small = jnp.concatenate(lines, axis=0).astype(bf16)
             shard = total.shape[0] // packed.shape[0]
             for copy in range(packed.shape[0]):
                 packed[copy, :SMALL, :] = small

time: 343 us -> 342 us (level)
    unnamed x114 -> x112, local copies, waits for them, and re-layouts: 17.7 us -> 16.9 us
where the time goes in v5:
time: 342 us; the launch traced here: 340 us
  Pallas kernels  167 us (49%)
  starting transfers between devices  62.9 us (18%)
  waiting for transfers between devices  61.1 us (18%)
  local copies, waits for them, and re-layouts  31.7 us (9%)
  between operations  14.7 us (4%)
    pallas_call x21, Pallas kernels, call(): pl.pallas_call(kernel, grid_spec=pltpu.PrefetchScalarGridSpec(num_scalar_...  167 us
    all_to_all x4, starting transfers between devices, exchange(): return lax.all_to_all(array, 'dp', 0, 0)  28.7 us
    ppermute x40, waiting for transfers between devices, swap(): return lax.ppermute(array, 'tensor', [(i, i ^ bit) for i in range(4)])  28.5 us
    all_to_all x4, waiting for transfers between devices, exchange(): return lax.all_to_all(array, 'dp', 0, 0)  26.5 us
    ppermute x40, starting transfers between devices, swap(): return lax.ppermute(array, 'tensor', [(i, i ^ bit) for i in range(4)])  23 us
    unnamed x112, local copies, waits for them, and re-layouts  16.9 us
    ppermute x4, starting transfers between devices, on_device(): lax.ppermute(state, 'dp', [(i, i + k) for i in range(count) if i % pieces...  11 us
  transfers between devices with their start and end apart: 50, of which 14 were waited for; matrix products, arithmetic and copies ran while one was open for 5% of the time, Pallas kernels for 49%

profile of v5, /device:TPU:0, one launch (start us, length us, event | category | flops | bytes accessed | tf_op | source)
XLA Modules:
  0.0 339.7 jit_solution(1048841955948903358)
XLA Ops:
  10.5 7.3 %all-to-all-start = ((bf16[8,96,768]{2,1,0:T(8,128)(2,1)}), bf16[8,96,768]{2,1,0:T(8,128)(2,1)S(1)}, u32[]{:S(2)}, u32[]{:S(2)}) async-start(bf16[8,96,768]{2,1,0:T(8,128)(2,1)} %broadcast_in_dim.2), calls=%async_computation | async-start | bytes 2359296 | tf_op jit(solution)/shard_map/all_to_all | solution.py:522
  26.4 7.8 %shard_map.288.attn_in = bf16[2,1024,768]{2,1,0:T(8,128)(2,1)} custom-call(s32[2]{0:T(128)} %pad_add_fusion.ids, bf16[2,1024,768]{2,1,0:T(8,128)(2,1)} %x.9, f32[1,768]{1,0:T(1,128)} %reshape.182.gain.refs_4_, f32[1,768]{1,0:T(1,128)} %reshape.184.shift.refs_5_), custom_call_target="tpu_custom_call" | custom-call | flops 8800000000 | bytes 3151872 | tf_op jit(solution)/shard_map/pallas_call | solution.py:72
  34.3 21.6 %all-to-all-done = bf16[8,96,768]{2,1,0:T(8,128)(2,1)S(1)} async-done(((bf16[8,96,768]{2,1,0:T(8,128)(2,1)}), bf16[8,96,768]{2,1,0:T(8,128)(2,1)S(1)}, u32[]{:S(2)}, u32[]{:S(2)}) %all-to-all-start) | async-done | bytes 1179680 | tf_op jit(solution)/shard_map/all_to_all | solution.py:522
  57.7 13.4 %shard_map.289 = (bf16[576,2048]{1,0:T(8,128)(2,1)}, bf16[768,2048]{1,0:T(8,128)(2,1)}, bf16[512,128]{1,0:T(8,128)(2,1)}) custom-call(s32[2]{0:T(128)} %pad_add_fusion.ids, bf16[2,1024,768]{2,1,0:T(8,128)(2,1)} %shard_map.288.attn_in, bf16[768,768]{1,0:T(8,128)(2,1)} %bitcast.16, f32[576,1]{1,0:T(8,128)} %copy.83.bias, bf16[2,192,192]{2,1,0:T(8,128)(2,1)} %copy.84.maps, ...), custom_call_target="tpu_custom_call" | custom-call | flops 14300000256 | bytes 4491520 | tf_op jit(solution)/shard_map/pallas_call | solution.py:72
  72.7 5.2 %collective-permute-start.5 = (bf16[512,128]{1,0:T(8,128)(2,1)}, bf16[512,128]{1,0:T(8,128)(2,1)S(1)}, u32[]{:S(2)}, u32[]{:S(2)}) collective-permute-start(bf16[512,128]{1,0:T(8,128)(2,1)} %get-tuple-element.208), channel_id=1, source_target_pairs={{0,12},{4,16},{8,20},{12,24},{16,28},{1,13},{5,17},{9,21},{13,25},... | collective-permute-start | bytes 393224 | tf_op jit(solution)/shard_map/ppermute | solution.py:659
  79.2 3.3 collective-permute-start.3
  84.9 3.6 %collective-permute-done.4.refs_1_ = bf16[512,128]{1,0:T(8,128)(2,1)S(1)} collective-permute-done((bf16[512,128]{1,0:T(8,128)(2,1)}, bf16[512,128]{1,0:T(8,128)(2,1)S(1)}, u32[]{:S(2)}, u32[]{:S(2)}) %collective-permute-start.4) | collective-permute-done | bytes 131104 | tf_op jit(solution)/shard_map/ppermute | solution.py:659
  89.8 6.5 %shard_map.290 = (f32[192,1024]{1,0:T(8,128)}, bf16[192,1024]{1,0:T(8,128)(2,1)}, f32[8,1024]{1,0:T(8,128)}, f32[4,240,128]{2,1,0:T(8,128)}) custom-call(s32[2]{0:T(128)} %pad_add_fusion.ids, bf16[576,2048]{1,0:T(8,128)(2,1)} %get-tuple-element.205.qkv_v.qkv, bf16[768,2048]{1,0:T(8,128)(2,1)} %get-tuple-element.206.feats.feats_q, ...), custom_call_target="tpu_custom_call" | custom-call | flops 7150000128 | bytes 6045696 | tf_op jit(solution)/shard_map/pallas_call | solution.py:72
  97.6 6.5 %shard_map.291 = (f32[192,1024]{1,0:T(8,128)}, bf16[192,1024]{1,0:T(8,128)(2,1)}, f32[8,1024]{1,0:T(8,128)}, f32[4,240,128]{2,1,0:T(8,128)}) custom-call(s32[2]{0:T(128)} %pad_add_fusion.ids, bf16[576,2048]{1,0:T(8,128)(2,1)} %get-tuple-element.205.qkv_v.qkv, bf16[768,2048]{1,0:T(8,128)(2,1)} %get-tuple-element.206.feats.feats_q, ...), custom_call_target="tpu_custom_call" | custom-call | flops 7150000128 | bytes 6045696 | tf_op jit(solution)/shard_map/pallas_call | solution.py:72
  104.0 4.1 %collective-permute-done.7.a1 = bf16[192,1024]{1,0:T(8,128)(2,1)S(1)} collective-permute-done((bf16[192,1024]{1,0:T(8,128)(2,1)}, bf16[192,1024]{1,0:T(8,128)(2,1)S(1)}, u32[]{:S(2)}, u32[]{:S(2)}) %collective-permute-start.7) | collective-permute-done | bytes 393248 | tf_op jit(solution)/shard_map/ppermute | solution.py:530
  111.2 20.4 %shard_map.292 = (f32[4,256,768]{2,1,0:T(8,128)}, bf16[256,768]{1,0:T(8,128)(2,1)}, bf16[256,768]{1,0:T(8,128)(2,1)}, bf16[256,768]{1,0:T(8,128)(2,1)}, bf16[256...) custom-call(s32[2]{0:T(128)} %pad_add_fusion.ids, ...), custom_call_target="tpu_custom_call" | custom-call | flops 23100000256 | bytes 13774848 | tf_op jit(solution)/shard_map/pallas_call | solution.py:72
  135.3 22.8 %shard_map.293 = (f32[4,256,768]{2,1,0:T(8,128)}, bf16[2,256,768]{2,1,0:T(8,128)(2,1)}, bf16[2,256,768]{2,1,0:T(8,128)(2,1)}, bf16[2,256,768]{2,1,0:T(8,128)(2,1...) custom-call(s32[2]{0:T(128)} %pad_add_fusion.ids, bf16[2,1024,768]{2,1,0:T(8,128)(2,1)} %x.9, ...), custom_call_target="tpu_custom_call" | custom-call | flops 23100000256 | bytes 18496512 | tf_op jit(solution)/shard_map/pallas_call | solution.py:72
  159.9 4.2 %shard_map.294 = (f32[256,768]{1,0:T(8,128)}, bf16[256,768]{1,0:T(8,128)(2,1)}, f32[2,768]{1,0:T(2,128)}) custom-call(s32[2]{0:T(128)} %pad_add_fusion.ids, f32[4,256,768]{2,1,0:T(8,128)} %get-tuple-element.255.residual.refs_0_, bf16[2,1024,768]{2,1,0:T(8,128)(2,1)} %cot.7, f32[1,768]{1,0:T(1,128)} %reshape.186.gain, ...), custom_call_target="tpu_custom_call" | custom-call | flops 4400000000 | bytes 7867392 | tf_op jit(solution)/shard_map/pallas_call | solution.py:72
  169.1 6.7 %collective-permute-done.17.g1 = bf16[256,768]{1,0:T(8,128)(2,1)S(1)} collective-permute-done((bf16[256,768]{1,0:T(8,128)(2,1)}, bf16[256,768]{1,0:T(8,128)(2,1)S(1)}, u32[]{:S(2)}, u32[]{:S(2)}) %collective-permute-start.17) | collective-permute-done | bytes 393248 | tf_op jit(solution)/shard_map/ppermute | solution.py:530
  178.1 7.4 %shard_map.296 = (f32[240,1024]{1,0:T(8,128)}, bf16[8,256,128]{2,1,0:T(8,128)(2,1)}, f32[192,768]{1,0:T(8,128)}) custom-call(s32[2]{0:T(128)} %pad_add_fusion.ids, bf16[256,768]{1,0:T(8,128)(2,1)} %get-tuple-element.267.g0, bf16[256,768]{1,0:T(8,128)(2,1)} %copy-done.44, bf16[256,768]{1,0:T(8,128)(2,1)} %copy-done.46, ...), custom_call_target="tpu_custom_call" | custom-call | flops 7699999744 | bytes 6365184 | tf_op jit(solution)/shard_map/pallas_call | solution.py:72
  185.5 12.4 %all-to-all-start.1 = ((bf16[8,256,128]{2,1,0:T(8,128)(2,1)}), bf16[8,256,128]{2,1,0:T(8,128)(2,1)S(1)}, u32[]{:S(2)}, u32[]{:S(2)}) async-start(bf16[8,256,128]{2,1,0:T(8,128)(2,1)} %get-tuple-element.287), calls=%async_computation.1 | async-start | bytes 1048576 | tf_op jit(solution)/shard_map/all_to_all | solution.py:522
  197.9 4.0 %shard_map.297 = (f32[256,768]{1,0:T(8,128)}, bf16[256,768]{1,0:T(8,128)(2,1)}, f32[2,768]{1,0:T(2,128)}) custom-call(s32[2]{0:T(128)} %pad_add_fusion.ids, f32[4,256,768]{2,1,0:T(8,128)} %get-tuple-element.276.residual.refs_3_, bf16[2,1024,768]{2,1,0:T(8,128)(2,1)} %cot.7, f32[1,768]{1,0:T(1,128)} %reshape.186.gain, ...), custom_call_target="tpu_custom_call" | custom-call | flops 4400000000 | bytes 8260608 | tf_op jit(solution)/shard_map/pallas_call | solution.py:72
  205.2 3.1 shard_map.298
  208.8 5.3 %collective-permute-done.23.g1 = bf16[256,768]{1,0:T(8,128)(2,1)S(1)} collective-permute-done((bf16[256,768]{1,0:T(8,128)(2,1)}, bf16[256,768]{1,0:T(8,128)(2,1)S(1)}, u32[]{:S(2)}, u32[]{:S(2)}) %collective-permute-start.23) | collective-permute-done | bytes 393248 | tf_op jit(solution)/shard_map/ppermute | solution.py:530
  217.0 15.3 %shard_map.299 = (bf16[256,768]{1,0:T(8,128)(2,1)}, bf16[256,768]{1,0:T(8,128)(2,1)}, bf16[256,768]{1,0:T(8,128)(2,1)}, bf16[256,768]{1,0:T(8,128)(2,1)}, f32[57...) custom-call(s32[2]{0:T(128)} %pad_add_fusion.ids, bf16[576,2048]{1,0:T(8,128)(2,1)} %get-tuple-element.205.qkv_v.qkv, ...), custom_call_target="tpu_custom_call" | custom-call | flops 17600000000 | bytes 12279808 | tf_op jit(solution)/shard_map/pallas_call | solution.py:72
  235.2 7.1 %shard_map.300 = (f32[240,1024]{1,0:T(8,128)}, bf16[8,256,128]{2,1,0:T(8,128)(2,1)}, bf16[768,192]{1,0:T(8,128)(2,1)}) custom-call(s32[2]{0:T(128)} %pad_add_fusion.ids, bf16[256,768]{1,0:T(8,128)(2,1)} %get-tuple-element.288.g0, bf16[256,768]{1,0:T(8,128)(2,1)} %copy-done.32, bf16[256,768]{1,0:T(8,128)(2,1)} %collective-permute-done.24.g2, ...), custom_call_target="tpu_custom_call" | custom-call | flops 7699999744 | bytes 6955008 | tf_op jit(solution)/shard_map/pallas_call | solution.py:72
  242.3 3.9 %all-to-all-start.2 = ((bf16[8,256,128]{2,1,0:T(8,128)(2,1)}), bf16[8,256,128]{2,1,0:T(8,128)(2,1)S(1)}, u32[]{:S(2)}, u32[]{:S(2)}) async-start(bf16[8,256,128]{2,1,0:T(8,128)(2,1)} %get-tuple-element.323), calls=%async_computation.3 | async-start | bytes 1048576 | tf_op jit(solution)/shard_map/all_to_all | solution.py:522
  248.5 4.0 %shard_map.301.refs_0_ = bf16[2,256,768]{2,1,0:T(8,128)(2,1)} custom-call(s32[2]{0:T(128)} %pad_add_fusion.ids, f32[1,768]{1,0:T(1,128)} %reshape.194.bias, bf16[2,256,768]{2,1,0:T(8,128)(2,1)} %copy-done.26, f32[4,256,768]{2,1,0:T(8,128)} %get-tuple-element.255.residual.refs_0_, bf16[2,256,768]{2,1,0:T(8,128)(2,1)} %get-tuple-element.282.refs_0_.refs_1_, ...), custom_call_target="tpu_custom_call" | custom-call | flops 4400000000 | bytes 10226688 | tf_op jit(solution)/shard_map/pallas_call | solution.py:72
  255.7 3.8 %shard_map.302.refs_0_ = bf16[256,768]{1,0:T(8,128)(2,1)} custom-call(s32[2]{0:T(128)} %pad_add_fusion.ids, bf16[2,1024,768]{2,1,0:T(8,128)(2,1)} %x.9, f32[256,768]{1,0:T(8,128)} %get-tuple-element.315.grad_residual, f32[1,768]{1,0:T(1,128)} %reshape.182.gain.refs_4_, bf16[256,768]{1,0:T(8,128)(2,1)} %get-tuple-element.316.refs_0_, ...), custom_call_target="tpu_custom_call" | custom-call | flops 4400000000 | bytes 5508096 | tf_op jit(solution)/shard_map/pallas_call | solution.py:72
  261.8 17.9 %shard_map.303 = (bf16[2,256,768]{2,1,0:T(8,128)(2,1)}, bf16[2,256,768]{2,1,0:T(8,128)(2,1)}, bf16[8,136,768]{2,1,0:T(8,128)(2,1)}) custom-call(s32[2]{0:T(128)} %pad_add_fusion.ids, bf16[576,2048]{1,0:T(8,128)(2,1)} %get-tuple-element.205.qkv_v.qkv, bf16[768,2048]{1,0:T(8,128)(2,1)} %get-tuple-element.206.feats.feats_q, ...), custom_call_target="tpu_custom_call" | custom-call | tf_op jit(solution)/shard_map/pallas_call | solution.py:72
  280.4 5.1 %all-to-all-start.3 = ((bf16[8,136,768]{2,1,0:T(8,128)(2,1)}), bf16[8,136,768]{2,1,0:T(8,128)(2,1)S(1)}, u32[]{:S(2)}, u32[]{:S(2)}) async-start(bf16[8,136,768]{2,1,0:T(8,128)(2,1)} %get-tuple-element.359), calls=%async_computation.4 | async-start | bytes 3342336 | tf_op jit(solution)/shard_map/all_to_all | solution.py:522
  291.7 6.2 %shard_map.305 = bf16[2,1024,768]{2,1,0:T(8,128)(2,1)} custom-call(s32[2]{0:T(128)} %pad_add_fusion.ids, bf16[2,256,768]{2,1,0:T(8,128)(2,1)} %shard_map.301.refs_0_, bf16[2,256,768]{2,1,0:T(8,128)(2,1)} %copy-done.24, bf16[2,256,768]{2,1,0:T(8,128)(2,1)} %collective-permute-done.33.refs_2_, bf16[2,256,768]{2,1,0:T(8,128)(2,1)} %collective-permute-done.34.refs_3_), custom_call_target="tpu_custom_call" | custom-call | flops 6600000000 | bytes 3145728 | tf_op jit(solution)/shard_map/pallas_call | solution.py:72
  297.9 3.8 %collective-permute-done.35.refs_2_ = bf16[1,256,768]{2,1,0:T(8,128)(2,1)} collective-permute-done((bf16[1,256,768]{2,1,0:T(8,128)(2,1)}, bf16[1,256,768]{2,1,0:T(8,128)(2,1)}, u32[]{:S(2)}, u32[]{:S(2)}) %collective-permute-start.35) | collective-permute-done | bytes 393248 | tf_op jit(solution)/shard_map/ppermute | solution.py:530
  301.6 3.6 %shard_map.306.refs_0_ = bf16[256,768]{1,0:T(8,128)(2,1)} custom-call(s32[2]{0:T(128)} %pad_add_fusion.ids, bf16[2,1024,768]{2,1,0:T(8,128)(2,1)} %x.9, f32[256,768]{1,0:T(8,128)} %get-tuple-element.349.grad_residual, f32[1,768]{1,0:T(1,128)} %reshape.182.gain.refs_4_, bf16[2,256,768]{2,1,0:T(8,128)(2,1)} %get-tuple-element.341.refs_0_, ...), custom_call_target="tpu_custom_call" | custom-call | flops 4400000000 | bytes 5901312 | tf_op jit(solution)/shard_map/pallas_call | solution.py:72
  306.7 3.7 %shard_map.307.refs_4_ = bf16[2,1024,768]{2,1,0:T(8,128)(2,1)} custom-call(s32[2]{0:T(128)} %pad_add_fusion.ids, bf16[256,768]{1,0:T(8,128)(2,1)} %shard_map.302.refs_0_, bf16[256,768]{1,0:T(8,128)(2,1)} %copy-done.30, bf16[256,768]{1,0:T(8,128)(2,1)} %collective-permute-done.36.refs_2_, bf16[256,768]{1,0:T(8,128)(2,1)} %collective-permute-done.37.refs_3_), custom_call_target="tpu_custom_call" | custom-call | flops 4400000000 | bytes 1572864 | tf_op jit(solution)/shard_map/pallas_call | solution.py:72
  310.4 6.6 %collective-permute-done.38.refs_1_ = bf16[256,768]{1,0:T(8,128)(2,1)S(1)} collective-permute-done((bf16[256,768]{1,0:T(8,128)(2,1)}, bf16[256,768]{1,0:T(8,128)(2,1)S(1)}, u32[]{:S(2)}, u32[]{:S(2)}) %collective-permute-start.38) | collective-permute-done | bytes 393248 | tf_op jit(solution)/shard_map/ppermute | solution.py:530
  319.5 3.7 %shard_map.308 = bf16[2,1024,768]{2,1,0:T(8,128)(2,1)} custom-call(s32[2]{0:T(128)} %pad_add_fusion.ids, bf16[256,768]{1,0:T(8,128)(2,1)} %shard_map.306.refs_0_, bf16[256,768]{1,0:T(8,128)(2,1)} %copy-done.49, bf16[256,768]{1,0:T(8,128)(2,1)} %copy-done.48, bf16[256,768]{1,0:T(8,128)(2,1)} %copy-done.50, ...), custom_call_target="tpu_custom_call", output_to_operand_aliasing={{}: (5, {})} | custom-call | flops 4400000000 | bytes 4718592 | tf_op jit(solution)/shard_map/pallas_call | solution.py:72
  (246 shorter events, 74.7 us)
Async XLA Ops:
  10.5 45.3 %all-to-all-start = ((bf16[8,96,768]{2,1,0:T(8,128)(2,1)}), bf16[8,96,768]{2,1,0:T(8,128)(2,1)S(1)}, u32[]{:S(2)}, u32[]{:S(2)}) async-start(bf16[8,96,768]{2,1,0:T(8,128)(2,1)} %broadcast_in_dim.2), calls=%async_computation | async-start | bytes 2359296 | tf_op jit(solution)/shard_map/all_to_all | solution.py:522
  17.8 92.5 %all-gather.2.cloned.1.call-start = ((), (), s32[]{:S(2)}) async-start(), calls=%async_computation.5 | async-start | bytes 2654208 | tf_op jit(solution)/shard_map/all_gather | solution.py:627
  18.6 229.0 %reduce-scatter.2.cloned.1.call-start = ((), (), s32[]{:S(2)}) async-start(), calls=%async_computation.6 | async-start | bytes 2654208 | tf_op jit(solution)/shard_map/reduce_scatter | solution.py:803
  56.1 23.1 %collective-permute-start.1 = (bf16[768,192]{1,0:T(8,128)(2,1)S(1)}, bf16[768,192]{1,0:T(8,128)(2,1)S(1)}, u32[]{:S(2)}, u32[]{:S(2)}) collective-permute-start(bf16[768,192]{1,0:T(8,128)(2,1)S(1)} %slice.70.p0.proj_t), channel_id=1, source_target_pairs={{0,1},{1,0},{2,3},{3,2},{4,5},{5,4},{6,7},{7,6},{8,9},{9,8},{10,11... | collective-permute-start | bytes 884744 | tf_op jit(solution)/shard_map/ppermute | solution.py:530
  56.1 15.0 %collective-permute-start = (bf16[768,192]{1,0:T(8,128)(2,1)S(1)}, bf16[768,192]{1,0:T(8,128)(2,1)S(1)}, u32[]{:S(2)}, u32[]{:S(2)}) collective-permute-start(bf16[768,192]{1,0:T(8,128)(2,1)S(1)} %slice.70.p0.proj_t), channel_id=1, source_target_pairs={{0,2},{1,3},{2,0},{3,1},{4,6},{5,7},{6,4},{7,5},{8,10},{9,11},{10,... | collective-permute-start | bytes 884744 | tf_op jit(solution)/shard_map/ppermute | solution.py:530
  71.2 12.7 %collective-permute-start.2 = (bf16[768,192]{1,0:T(8,128)(2,1)S(1)}, bf16[768,192]{1,0:T(8,128)(2,1)S(1)}, u32[]{:S(2)}, u32[]{:S(2)}) collective-permute-start(bf16[768,192]{1,0:T(8,128)(2,1)S(1)} %collective-permute-done.p1), channel_id=1, source_target_pairs={{0,1},{1,0},{2,3},{3,2},{4,5},{5,4},{6,7},{7,6},{8,9},{9,8},{10,11... | collective-permute-start | bytes 884744 | tf_op jit(solution)/shard_map/ppermute | solution.py:530
  71.4 12.5 %collective-permute-start.6 = (bf16[512,128]{1,0:T(8,128)(2,1)}, bf16[512,128]{1,0:T(8,128)(2,1)S(1)}, u32[]{:S(2)}, u32[]{:S(2)}) collective-permute-start(bf16[512,128]{1,0:T(8,128)(2,1)} %get-tuple-element.208), channel_id=1, source_target_pairs={{0,16},{4,20},{8,24},{12,28},{1,17},{5,21},{9,25},{13,29},{2,18},{... | collective-permute-start | bytes 393224 | tf_op jit(solution)/shard_map/ppermute | solution.py:659
  72.7 12.2 %collective-permute-start.5 = (bf16[512,128]{1,0:T(8,128)(2,1)}, bf16[512,128]{1,0:T(8,128)(2,1)S(1)}, u32[]{:S(2)}, u32[]{:S(2)}) collective-permute-start(bf16[512,128]{1,0:T(8,128)(2,1)} %get-tuple-element.208), channel_id=1, source_target_pairs={{0,12},{4,16},{8,20},{12,24},{16,28},{1,13},{5,17},{9,21},{13,25},... | collective-permute-start | bytes 393224 | tf_op jit(solution)/shard_map/ppermute | solution.py:659
  96.3 14.0 %collective-permute-start.8 = (bf16[192,1024]{1,0:T(8,128)(2,1)}, bf16[192,1024]{1,0:T(8,128)(2,1)S(1)}, u32[]{:S(2)}, u32[]{:S(2)}) collective-permute-start(bf16[192,1024]{1,0:T(8,128)(2,1)} %get-tuple-element.219.a0.attended_low), channel_id=1, source_target_pairs={{0,1},{1,0},{2,3},{3,2},{4,5},{5,4},{6,7},{7,6},{8,9},{9,8},{10,11... | collective-permute-start | bytes 1179656 | tf_op jit(solution)/shard_map/ppermute | solution.py:530
  108.2 24.6 %collective-permute-start.12 = (bf16[192,1024]{1,0:T(8,128)(2,1)}, bf16[192,1024]{1,0:T(8,128)(2,1)S(1)}, u32[]{:S(2)}, u32[]{:S(2)}) collective-permute-start(bf16[192,1024]{1,0:T(8,128)(2,1)} %get-tuple-element.241.a0.attended_low), channel_id=1, source_target_pairs={{0,3},{1,2},{2,1},{3,0},{4,7},{5,6},{6,5},{7,4},{8,11},{9,10},{10,... | collective-permute-start | bytes 1179656 | tf_op jit(solution)/shard_map/ppermute | solution.py:530
  109.3 24.5 %collective-permute-start.11 = (bf16[192,1024]{1,0:T(8,128)(2,1)}, bf16[192,1024]{1,0:T(8,128)(2,1)S(1)}, u32[]{:S(2)}, u32[]{:S(2)}) collective-permute-start(bf16[192,1024]{1,0:T(8,128)(2,1)} %get-tuple-element.241.a0.attended_low), channel_id=1, source_target_pairs={{0,1},{1,0},{2,3},{3,2},{4,5},{5,4},{6,7},{7,6},{8,9},{9,8},{10,11... | collective-permute-start | bytes 1179656 | tf_op jit(solution)/shard_map/ppermute | solution.py:530
  109.4 24.5 %collective-permute-start.10 = (bf16[192,1024]{1,0:T(8,128)(2,1)}, bf16[192,1024]{1,0:T(8,128)(2,1)S(1)}, u32[]{:S(2)}, u32[]{:S(2)}) collective-permute-start(bf16[192,1024]{1,0:T(8,128)(2,1)} %get-tuple-element.241.a0.attended_low), channel_id=1, source_target_pairs={{0,2},{1,3},{2,0},{3,1},{4,6},{5,7},{6,4},{7,5},{8,10},{9,11},{10,... | collective-permute-start | bytes 1179656 | tf_op jit(solution)/shard_map/ppermute | solution.py:530
  131.6 26.6 %collective-permute-start.13 = (bf16[256,768]{1,0:T(8,128)(2,1)}, bf16[256,768]{1,0:T(8,128)(2,1)S(1)}, u32[]{:S(2)}, u32[]{:S(2)}) collective-permute-start(bf16[256,768]{1,0:T(8,128)(2,1)} %get-tuple-element.257), channel_id=1, source_target_pairs={{0,2},{1,3},{2,0},{3,1},{4,6},{5,7},{6,4},{7,5},{8,10},{9,11},{10,... | collective-permute-start | bytes 1179656 | tf_op jit(solution)/shard_map/ppermute | solution.py:530
  132.7 25.5 %collective-permute-start.14 = (bf16[256,768]{1,0:T(8,128)(2,1)}, bf16[256,768]{1,0:T(8,128)(2,1)S(1)}, u32[]{:S(2)}, u32[]{:S(2)}) collective-permute-start(bf16[256,768]{1,0:T(8,128)(2,1)} %get-tuple-element.258), channel_id=1, source_target_pairs={{0,1},{1,0},{2,3},{3,2},{4,5},{5,4},{6,7},{7,6},{8,9},{9,8},{10,11... | collective-permute-start | bytes 1179656 | tf_op jit(solution)/shard_map/ppermute | solution.py:530
  132.8 25.5 %collective-permute-start.15 = (bf16[256,768]{1,0:T(8,128)(2,1)}, bf16[256,768]{1,0:T(8,128)(2,1)S(1)}, u32[]{:S(2)}, u32[]{:S(2)}) collective-permute-start(bf16[256,768]{1,0:T(8,128)(2,1)} %get-tuple-element.259), channel_id=1, source_target_pairs={{0,3},{1,2},{2,1},{3,0},{4,7},{5,6},{6,5},{7,4},{8,11},{9,10},{10,... | collective-permute-start | bytes 1179656 | tf_op jit(solution)/shard_map/ppermute | solution.py:530
  175.8 27.6 %collective-permute-start.22 = (bf16[2,256,768]{2,1,0:T(8,128)(2,1)}, bf16[2,256,768]{2,1,0:T(8,128)(2,1)S(1)}, u32[]{:S(2)}, u32[]{:S(2)}) collective-permute-start(bf16[2,256,768]{2,1,0:T(8,128)(2,1)} %get-tuple-element.285), channel_id=1, source_target_pairs={{0,1},{1,0},{2,3},{3,2},{4,5},{5,4},{6,7},{7,6},{8,9},{9,8},{10,11... | collective-permute-start | bytes 2359304 | tf_op jit(solution)/shard_map/ppermute | solution.py:530
  176.3 27.1 %collective-permute-start.21 = (bf16[2,256,768]{2,1,0:T(8,128)(2,1)S(1)}, bf16[2,256,768]{2,1,0:T(8,128)(2,1)S(1)}, u32[]{:S(2)}, u32[]{:S(2)}) collective-permute-start(bf16[2,256,768]{2,1,0:T(8,128)(2,1)S(1)} %copy-done.20), channel_id=1, source_target_pairs={{0,1},{1,0},{2,3},{3,2},{4,5},{5,4},{6,7},{7,6},{8,9},{9,8},{10,11... | collective-permute-start | bytes 2359304 | tf_op jit(solution)/shard_map/ppermute | solution.py:530
  176.3 21.6 %collective-permute-start.20 = (bf16[1,256,768]{2,1,0:T(8,128)(2,1)}, bf16[1,256,768]{2,1,0:T(8,128)(2,1)}, u32[]{:S(2)}, u32[]{:S(2)}) collective-permute-start(bf16[1,256,768]{2,1,0:T(8,128)(2,1)} %shard_map.295), channel_id=1, source_target_pairs={{0,2},{1,3},{2,0},{3,1},{4,6},{5,7},{6,4},{7,5},{8,10},{9,11},{10,... | collective-permute-start | bytes 1179656 | tf_op jit(solution)/shard_map/ppermute | solution.py:530
  185.5 30.7 %all-to-all-start.1 = ((bf16[8,256,128]{2,1,0:T(8,128)(2,1)}), bf16[8,256,128]{2,1,0:T(8,128)(2,1)S(1)}, u32[]{:S(2)}, u32[]{:S(2)}) async-start(bf16[8,256,128]{2,1,0:T(8,128)(2,1)} %get-tuple-element.287), calls=%async_computation.1 | async-start | bytes 1048576 | tf_op jit(solution)/shard_map/all_to_all | solution.py:522
  201.9 12.2 %collective-permute-start.23 = (bf16[256,768]{1,0:T(8,128)(2,1)}, bf16[256,768]{1,0:T(8,128)(2,1)S(1)}, u32[]{:S(2)}, u32[]{:S(2)}) collective-permute-start(bf16[256,768]{1,0:T(8,128)(2,1)} %get-tuple-element.288.g0), channel_id=1, source_target_pairs={{0,2},{1,3},{2,0},{3,1},{4,6},{5,7},{6,4},{7,5},{8,10},{9,11},{10,... | collective-permute-start | bytes 1179656 | tf_op jit(solution)/shard_map/ppermute | solution.py:530
  203.4 30.1 %collective-permute-start.24 = (bf16[256,768]{1,0:T(8,128)(2,1)}, bf16[256,768]{1,0:T(8,128)(2,1)}, u32[]{:S(2)}, u32[]{:S(2)}) collective-permute-start(bf16[256,768]{1,0:T(8,128)(2,1)} %get-tuple-element.288.g0), channel_id=1, source_target_pairs={{0,1},{1,0},{2,3},{3,2},{4,5},{5,4},{6,7},{7,6},{8,9},{9,8},{10,11... | collective-permute-start | bytes 1179656 | tf_op jit(solution)/shard_map/ppermute | solution.py:530
  208.3 39.4 %collective-permute-start.26 = (bf16[2,256,768]{2,1,0:T(8,128)(2,1)}, bf16[2,256,768]{2,1,0:T(8,128)(2,1)S(1)}, u32[]{:S(2)}, u32[]{:S(2)}) collective-permute-start(bf16[2,256,768]{2,1,0:T(8,128)(2,1)} %shard_map.298), channel_id=1, source_target_pairs={{0,2},{1,3},{2,0},{3,1},{4,6},{5,7},{6,4},{7,5},{8,10},{9,11},{10,... | collective-permute-start | bytes 2359304 | tf_op jit(solution)/shard_map/ppermute | solution.py:530
  216.2 18.3 %collective-permute-start.25 = (bf16[256,768]{1,0:T(8,128)(2,1)S(1)}, bf16[256,768]{1,0:T(8,128)(2,1)S(1)}, u32[]{:S(2)}, u32[]{:S(2)}) collective-permute-start(bf16[256,768]{1,0:T(8,128)(2,1)S(1)} %collective-permute-done.23.g1), channel_id=1, source_target_pairs={{0,1},{1,0},{2,3},{3,2},{4,5},{5,4},{6,7},{7,6},{8,9},{9,8},{10,11... | collective-permute-start | bytes 1179656 | tf_op jit(solution)/shard_map/ppermute | solution.py:530
  232.3 21.8 %collective-permute-start.27 = (bf16[256,768]{1,0:T(8,128)(2,1)}, bf16[256,768]{1,0:T(8,128)(2,1)S(1)}, u32[]{:S(2)}, u32[]{:S(2)}) collective-permute-start(bf16[256,768]{1,0:T(8,128)(2,1)} %get-tuple-element.317), channel_id=1, source_target_pairs={{0,2},{1,3},{2,0},{3,1},{4,6},{5,7},{6,4},{7,5},{8,10},{9,11},{10,... | collective-permute-start | bytes 1179656 | tf_op jit(solution)/shard_map/ppermute | solution.py:530
  233.5 20.6 %collective-permute-start.28 = (bf16[256,768]{1,0:T(8,128)(2,1)}, bf16[256,768]{1,0:T(8,128)(2,1)S(1)}, u32[]{:S(2)}, u32[]{:S(2)}) collective-permute-start(bf16[256,768]{1,0:T(8,128)(2,1)} %get-tuple-element.318), channel_id=1, source_target_pairs={{0,1},{1,0},{2,3},{3,2},{4,5},{5,4},{6,7},{7,6},{8,9},{9,8},{10,11... | collective-permute-start | bytes 1179656 | tf_op jit(solution)/shard_map/ppermute | solution.py:530
  233.5 20.6 %collective-permute-start.29 = (bf16[256,768]{1,0:T(8,128)(2,1)}, bf16[256,768]{1,0:T(8,128)(2,1)S(1)}, u32[]{:S(2)}, u32[]{:S(2)}) collective-permute-start(bf16[256,768]{1,0:T(8,128)(2,1)} %get-tuple-element.319), channel_id=1, source_target_pairs={{0,3},{1,2},{2,1},{3,0},{4,7},{5,6},{6,5},{7,4},{8,11},{9,10},{10,... | collective-permute-start | bytes 1179656 | tf_op jit(solution)/shard_map/ppermute | solution.py:530
  242.3 18.7 %all-to-all-start.2 = ((bf16[8,256,128]{2,1,0:T(8,128)(2,1)}), bf16[8,256,128]{2,1,0:T(8,128)(2,1)S(1)}, u32[]{:S(2)}, u32[]{:S(2)}) async-start(bf16[8,256,128]{2,1,0:T(8,128)(2,1)} %get-tuple-element.323), calls=%async_computation.3 | async-start | bytes 1048576 | tf_op jit(solution)/shard_map/all_to_all | solution.py:522
  252.6 27.2 %collective-permute-start.30 = (bf16[2,256,768]{2,1,0:T(8,128)(2,1)}, bf16[2,256,768]{2,1,0:T(8,128)(2,1)S(1)}, u32[]{:S(2)}, u32[]{:S(2)}) collective-permute-start(bf16[2,256,768]{2,1,0:T(8,128)(2,1)} %shard_map.301.refs_0_), channel_id=1, source_target_pairs={{0,2},{1,3},{2,0},{3,1},{4,6},{5,7},{6,4},{7,5},{8,10},{9,11},{10,... | collective-permute-start | bytes 2359304 | tf_op jit(solution)/shard_map/ppermute | solution.py:530
  259.5 20.2 %collective-permute-start.31 = (bf16[256,768]{1,0:T(8,128)(2,1)}, bf16[256,768]{1,0:T(8,128)(2,1)S(1)}, u32[]{:S(2)}, u32[]{:S(2)}) collective-permute-start(bf16[256,768]{1,0:T(8,128)(2,1)} %shard_map.302.refs_0_), channel_id=1, source_target_pairs={{0,2},{1,3},{2,0},{3,1},{4,6},{5,7},{6,4},{7,5},{8,10},{9,11},{10,... | collective-permute-start | bytes 1179656 | tf_op jit(solution)/shard_map/ppermute | solution.py:530
  280.4 44.7 %all-to-all-start.3 = ((bf16[8,136,768]{2,1,0:T(8,128)(2,1)}), bf16[8,136,768]{2,1,0:T(8,128)(2,1)S(1)}, u32[]{:S(2)}, u32[]{:S(2)}) async-start(bf16[8,136,768]{2,1,0:T(8,128)(2,1)} %get-tuple-element.359), calls=%async_computation.4 | async-start | bytes 3342336 | tf_op jit(solution)/shard_map/all_to_all | solution.py:522
  286.3 20.4 %collective-permute-start.36 = (bf16[256,768]{1,0:T(8,128)(2,1)}, bf16[256,768]{1,0:T(8,128)(2,1)}, u32[]{:S(2)}, u32[]{:S(2)}) collective-permute-start(bf16[256,768]{1,0:T(8,128)(2,1)} %shard_map.302.refs_0_), channel_id=1, source_target_pairs={{0,1},{1,0},{2,3},{3,2},{4,5},{5,4},{6,7},{7,6},{8,9},{9,8},{10,11... | collective-permute-start | bytes 1179656 | tf_op jit(solution)/shard_map/ppermute | solution.py:530
  287.2 19.5 %collective-permute-start.37 = (bf16[256,768]{1,0:T(8,128)(2,1)}, bf16[256,768]{1,0:T(8,128)(2,1)}, u32[]{:S(2)}, u32[]{:S(2)}) collective-permute-start(bf16[256,768]{1,0:T(8,128)(2,1)} %copy-done.30), channel_id=1, source_target_pairs={{0,1},{1,0},{2,3},{3,2},{4,5},{5,4},{6,7},{7,6},{8,9},{9,8},{10,11... | collective-permute-start | bytes 1179656 | tf_op jit(solution)/shard_map/ppermute | solution.py:530
  (72 other events, 480.9 us)
Sparse Core Ops, SparseCore 0:
  21.4 65.9 all-gather.1
  165.3 82.3 reduce-scatter.1
